TPU v7x, 128 devices: a whole 4x4x4 slice. The times are simulated.
128 devices in a mesh: dp: 16 (over y_lo, x, core), seq: 8 (over z, y_hi).
Axes of the slice: x: 4, y: 4 (y_hi: 2, y_lo: 2; y = y_hi * 2 + y_lo), z: 4, core: 2. Of those that a mesh axis runs over, the one named last changes fastest.
Arguments:
- queries: bfloat16 [16, 4096, 2048], P('dp', 'seq'), may hold values from -650 to 650
- keys_values: bfloat16 [16, 4096, 1024], P('dp', 'seq'), may hold values from -28 to 28
- doc_blocks: int32 [16, 32], P('dp'), may hold values from 0 to 7, never falling along the last dimension, each value on 1 to 16 neighbouring positions
- route_plan: int32 [8, 4], P('seq'), may hold values from 0 to 15, as said below
- out_weight: bfloat16 [2048, 4096], P('dp'), may hold values from -0.125 to 0.125
Outputs:
- layer_out: bfloat16 [16, 4096, 4096], P('dp', 'seq')
Inputs may be any that keep to these rules, and one draw needn't show every extreme that they name: Within a row of route_plan the entries are distinct.
All inputs are finite; a program needn't handle non-finite values.
Results may differ from a plain program's by a relative error of at most 0.0053.
Values may be sent and summed in bfloat16 or wider, within the bound.
No kernel may reach another device: no remote copies, remote signals or barrier semaphores. Data moves between devices by JAX's collectives and lax.ppermute only.
A program may use at most 256 MiB of HBM per device.

v0:
```python
import math

import jax
import jax.numpy as jnp
from jax import lax
from jax.experimental import pallas as pl
from jax.experimental.pallas import tpu as pltpu
from jax.sharding import PartitionSpec as P

HEAD_DIM = 128
BLOCK = 128
GROUPS = 4
GQ = 512
GK = 256
GW = GQ + GK
TILE = 4
PAD = TILE - 1
NB = 32
NEG = -1e30


def prep_kernel(z_ref, marks_ref, q_ref, qs_ref, k_ref, ks_ref, *out_refs):
    for j, out in enumerate(out_refs):
        rows = slice(j * BLOCK, (j + 1) * BLOCK)

        @pl.when(marks_ref[0, j] % 2 == 0)
        def _():
            out[0, :, :GQ] = q_ref[rows, :]
            out[0, :, GQ:] = k_ref[rows, :]

        @pl.when(marks_ref[0, j] % 2 != 0)
        def _():
            out[0, :, :GQ] = qs_ref[rows, :]
            out[0, :, GQ:] = ks_ref[rows, :]


def prep(z, marks, q, qs, kv, kvs):
    rows = q.shape[0]
    blocks = rows // BLOCK
    q_spec = pl.BlockSpec((rows, GQ), lambda k, z, m: (0, (z[0] + k) % GROUPS))
    k_spec = pl.BlockSpec((rows, GK), lambda k, z, m: (0, (z[0] + k) % GROUPS))
    o_spec = pl.BlockSpec((1, BLOCK, GW), lambda k, z, m: (k, 0, 0))
    return pl.pallas_call(
        prep_kernel,
        out_shape=[jax.ShapeDtypeStruct((GROUPS, BLOCK, GW), q.dtype)] * blocks,
        grid_spec=pltpu.PrefetchScalarGridSpec(
            num_scalar_prefetch=2,
            grid=(GROUPS,),
            in_specs=[q_spec, q_spec, k_spec, k_spec],
            out_specs=[o_spec] * blocks,
        ),
        name="prep",
    )(z, marks, q, qs, kv, kvs)


def flip(value):
    return [(i, i ^ value) for i in range(16)]


def moves():
    yield lambda x: x
    for code in range(1, 8):
        yield lambda x, code=code: lax.ppermute(x, "dp", flip(code << 1))


def z_shift(x, k):
    return lax.ppermute(x, "seq", [(s, (((s // 2) + k) % 4) * 2 + s % 2) for s in range(8)])


def attend_kernel(where_ref, docs_ref, *refs):
    own = [[refs[j]] + [refs[4 + 3 * j + k] for k in range(3)] for j in range(4)]
    other = refs[16:20]
    outs = refs[20:24]
    q_all, k_all, vt_all = refs[24:]
    z, h = where_ref[0], where_ref[1]

    k_all[pl.ds(0, PAD * BLOCK), :] = jnp.zeros((PAD * BLOCK, HEAD_DIM), k_all.dtype)
    vt_all[pl.ds(0, PAD)] = jnp.zeros((PAD, HEAD_DIM, BLOCK), vt_all.dtype)

    def put_kv(place, kv):
        k_all[pl.ds(pl.multiple_of((place + PAD) * BLOCK, BLOCK), BLOCK), :] = kv[:, :HEAD_DIM]
        vt_all[place + PAD] = kv[:, HEAD_DIM:].T

    for j in range(4):
        for k in range(4):
            zs = (z + 4 - k) % 4
            piece = own[j][k][0] if k == 0 else own[j][k][...]
            for g in range(4):
                q_all[zs * 4 + j, g * BLOCK : (g + 1) * BLOCK, :] = piece[
                    :, g * HEAD_DIM : (g + 1) * HEAD_DIM
                ]
            put_kv((zs * 2 + h) * 4 + j, piece[:, GQ:])
            put_kv((zs * 2 + 1 - h) * 4 + j, other[j][k])

    factor = math.log2(math.e) / math.sqrt(HEAD_DIM)
    keys = TILE * BLOCK
    lanes = 2 * BLOCK
    key_row = lax.broadcasted_iota(jnp.int32, (BLOCK, lanes), 0)
    query_row = lax.broadcasted_iota(jnp.int32, (BLOCK, lanes), 1) % BLOCK
    causal = key_row <= query_row

    for k in range(4):
        zd = (z + k) % 4

        def per_block(j, _, k=k, zd=zd):
            place = (zd * 2 + h) * 4 + j
            doc = docs_ref[0, place]
            start = lax.fori_loop(
                0, NB, lambda n, c: c + jnp.where(docs_ref[0, n] < doc, 1, 0), jnp.int32(0)
            )
            qs = [q_all[zd * 4 + j, i * lanes : (i + 1) * lanes, :] for i in range(2)]

            def tile(n, states, first):
                base = place - n * TILE
                kt = k_all[pl.ds(pl.multiple_of(base * BLOCK, BLOCK), keys), :]
                vt = jnp.concatenate([vt_all[base + u] for u in range(TILE)], axis=1)
                new = []
                for q, state in zip(qs, states):
                    s = lax.dot_general(
                        kt, q, (((1,), (1,)), ((), ())), preferred_element_type=jnp.float32
                    )
                    parts = []
                    for u in range(TILE):
                        part = s[u * BLOCK : (u + 1) * BLOCK]
                        if first and u == TILE - 1:
                            part = jnp.where(causal, part, NEG)
                        else:
                            part = jnp.where(base + u >= start + PAD, part, NEG)
                        parts.append(part)
                    s = jnp.concatenate(parts, axis=0)
                    peak = jnp.max(s, axis=0, keepdims=True)
                    if not first:
                        peak = jnp.maximum(peak, state[0])
                    w = jnp.exp2((s - peak) * factor)
                    w_sum = jnp.sum(w, axis=0, keepdims=True)
                    mixed = jnp.dot(vt, w.astype(jnp.bfloat16), preferred_element_type=jnp.float32)
                    if first:
                        new.append((peak, w_sum, mixed))
                    else:
                        keep = jnp.exp2((state[0] - peak) * factor)
                        new.append((peak, state[1] * keep + w_sum, state[2] * keep + mixed))
                return tuple(new)

            states = tile(0, (None, None), True)
            count = (place - start) // TILE + 1
            states = lax.fori_loop(1, count, lambda n, st: tile(n, st, False), states)
            rows = pl.ds(pl.multiple_of(j * BLOCK, BLOCK), BLOCK)
            for i, (_, total, acc) in enumerate(states):
                done = acc / total
                for g in range(2):
                    cols = (2 * i + g) * HEAD_DIM
                    outs[k][rows, cols : cols + HEAD_DIM] = done[
                        :, g * BLOCK : (g + 1) * BLOCK
                    ].T.astype(jnp.bfloat16)
            return 0

        lax.fori_loop(0, 4, per_block, 0)


def attend(where, docs, blocks, pieces, other):
    vmem = pl.BlockSpec(memory_space=pltpu.VMEM)
    smem = pl.BlockSpec(memory_space=pltpu.SMEM)
    first = pl.BlockSpec((1, BLOCK, GW), lambda i: (0, 0, 0))
    return pl.pallas_call(
        attend_kernel,
        grid=(1,),
        out_shape=[jax.ShapeDtypeStruct((4 * BLOCK, GQ), jnp.bfloat16)] * 4,
        in_specs=[smem] * 2 + [first] * 4 + [vmem] * 16,
        out_specs=[vmem] * 4,
        scratch_shapes=[
            pltpu.VMEM((16, 4 * BLOCK, HEAD_DIM), jnp.bfloat16),
            pltpu.VMEM(((NB + PAD) * BLOCK, HEAD_DIM), jnp.bfloat16),
            pltpu.VMEM((NB + PAD, HEAD_DIM, BLOCK), jnp.bfloat16),
        ],
        name="attend",
    )(where, docs, *blocks, *pieces, *other)


def tie_kernel(w_ref, token_ref, out_ref, sem):
    copy = pltpu.make_async_copy(w_ref, out_ref, sem)
    copy.start()
    copy.wait()


def tie(weight, token):
    any_spec = pl.BlockSpec(memory_space=pl.ANY)
    return pl.pallas_call(
        tie_kernel,
        out_shape=jax.ShapeDtypeStruct(weight.shape, weight.dtype),
        in_specs=[any_spec] * 2,
        out_specs=any_spec,
        scratch_shapes=[pltpu.SemaphoreType.DMA],
        name="tie",
    )(weight, token)


def body(queries, keys_values, doc_blocks, route_plan, out_weight):
    seq = lax.axis_index("seq")
    z, h = seq >> 1, seq & 1
    q, kv = queries[0], keys_values[0]
    qs = lax.ppermute(q, "dp", flip(1))
    kvs = lax.ppermute(kv, "dp", flip(1))
    where = jnp.stack([z, h]).astype(jnp.int32)
    blocks = list(prep(where, route_plan, q, qs, kv, kvs))

    pieces, other = [], []
    for j in range(4):
        block = lax.switch(route_plan[0, j] >> 1, list(moves()), blocks[j])
        blocks[j] = block
        came = []
        for k in range(1, 4):
            came.append(z_shift(block[k], k))
        pieces += came
        mine = jnp.stack([block[0, :, GQ:]] + [piece[:, GQ:] for piece in came])
        other.append(lax.ppermute(mine, "seq", [(s, s ^ 1) for s in range(8)]))
    weight = lax.all_gather(tie(out_weight, blocks[3]), "dp", axis=0, tiled=True)

    outs = attend(where, doc_blocks, blocks, pieces, other)
    parts = [outs[0]] + [z_shift(outs[k], k) for k in range(1, 4)]
    stacked = jnp.stack(parts)
    attended = jnp.concatenate(
        [lax.dynamic_index_in_dim(stacked, (z + 4 - c) & 3, 0, keepdims=False) for c in range(4)],
        axis=1,
    )
    out = jnp.dot(attended, weight, preferred_element_type=jnp.float32)
    return out.astype(jnp.bfloat16)[None]


def solution(mesh):
    in_specs = (
        P("dp", "seq", None),
        P("dp", "seq", None),
        P("dp", None),
        P("seq", None),
        P("dp", None),
    )
    out_specs = P("dp", "seq", None)

    return jax.shard_map(body, mesh=mesh, in_specs=in_specs, out_specs=out_specs, check_vma=False)
```

profile of v0, /device:TPU:1, one launch (start us, length us, event | category | flops | bytes accessed | tf_op | source)
XLA Modules:
  0.0 317.9 jit_solution(13680752891837167672)
XLA Ops:
  10.6 2.8 collective-permute-done.29.ks_ref
  14.4 4.3 %prep.1 = (bf16[4,128,768]{2,1,0:T(8,128)(2,1)S(1)}, bf16[4,128,768]{2,1,0:T(8,128)(2,1)S(1)}, bf16[4,128,768]{2,1,0:T(8,128)(2,1)S(1)}, bf16[4,128,768]{2,1,0:T(8,128)(2,1)S(1)}) custom-call(s32[2]{0:T(128)} %pad_add_fusion.z_ref.where_ref, s32[1,4]{1,0:T(1,128)} %marks_ref.1, bf16[512,2048]{1,0:T(8,128)(2,1)} %bitcast.72, ...), custom_call_target="tpu_custom_call" | custom-call | tf_op jit(solution)/shard_map/prep/pallas_call | solution.py:43
  18.7 20.1 %conditional.7 = (bf16[4,128,768]{2,1,0:T(8,128)(2,1)S(1)}) conditional(s32[]{:T(128)} %bitcast.7, bf16[4,128,768]{2,1,0:T(8,128)(2,1)S(1)} %get-tuple-element.84, bf16[4,128,768]{2,1,0:T(8,128)(2,1)S(1)} %get-tuple-element.84, bf16[4,128,768]{2,1,0:T(8,128)(2,1)S(1)} %get-tuple-element.84, ...), branch_computations={%region_24.0_spmd, %region_25.0_spmd, %region_26.0_spmd, %region_2... | conditional | bytes 4718640 | solution.py:208
  18.7 2.7 collective-permute-start.23
  21.4 17.3 %collective-permute-done.23 = bf16[4,128,768]{2,1,0:T(8,128)(2,1)S(1)} collective-permute-done((bf16[4,128,768]{2,1,0:T(8,128)(2,1)S(1)}, bf16[4,128,768]{2,1,0:T(8,128)(2,1)S(1)}, u32[]{:S(2)}, u32[]{:S(2)}) %collective-permute-start.23) | collective-permute-done | bytes 786464 | tf_op jit(solution)/shard_map/cond/branch_3_fun/ppermute | solution.py:63
  38.8 32.9 %tie.1 = bf16[128,4096]{1,0:T(8,128)(2,1)} custom-call(bf16[128,4096]{1,0:T(8,128)(2,1)} %w_ref.1, bf16[4,128,768]{2,1,0:T(8,128)(2,1)S(1)} %get-tuple-element.112.refs_3_.token_ref), custom_call_target="tpu_custom_call" | custom-call | tf_op jit(solution)/shard_map/tie/pallas_call | solution.py:187
  74.2 23.4 %conditional.4 = (bf16[4,128,768]{2,1,0:T(8,128)(2,1)S(1)}) conditional(s32[]{:T(128)} %bitcast.2, bf16[4,128,768]{2,1,0:T(8,128)(2,1)S(1)} %get-tuple-element.81, bf16[4,128,768]{2,1,0:T(8,128)(2,1)S(1)} %get-tuple-element.81, bf16[4,128,768]{2,1,0:T(8,128)(2,1)S(1)} %get-tuple-element.81, ...), branch_computations={%region_0.0_spmd, %region_1.0_spmd, %region_2.0_spmd, %region_3.0_... | conditional | bytes 4718640 | solution.py:208
  74.3 23.2 %collective-permute-done = bf16[4,128,768]{2,1,0:T(8,128)(2,1)S(1)} collective-permute-done((bf16[4,128,768]{2,1,0:T(8,128)(2,1)S(1)}, bf16[4,128,768]{2,1,0:T(8,128)(2,1)S(1)}, u32[]{:S(2)}, u32[]{:S(2)}) %collective-permute-start) | collective-permute-done | bytes 786464 | tf_op jit(solution)/shard_map/cond/branch_1_fun/ppermute | solution.py:63
  99.1 6.9 %collective-permute-start.31 = (bf16[128,768]{1,0:T(8,128)(2,1)}, bf16[128,768]{1,0:T(8,128)(2,1)S(1)}, u32[]{:S(2)}, u32[]{:S(2)}) collective-permute-start(bf16[128,768]{1,0:T(8,128)(2,1)} %get-tuple-element.103), channel_id=1, source_target_pairs={{0,4},{1,5},{2,6},{3,7},{4,0},{5,1},{6,2},{7,3},{8,12},{9,13},{10,... | collective-permute-start | bytes 589832 | tf_op jit(solution)/shard_map/ppermute | solution.py:67
  107.7 1.8 collective-permute-start.41
  109.5 16.4 %conditional.5 = (bf16[4,128,768]{2,1,0:T(8,128)(2,1)S(1)}) conditional(s32[]{:T(128)} %bitcast.5, bf16[4,128,768]{2,1,0:T(8,128)(2,1)S(1)} %get-tuple-element.82, bf16[4,128,768]{2,1,0:T(8,128)(2,1)S(1)} %get-tuple-element.82, bf16[4,128,768]{2,1,0:T(8,128)(2,1)S(1)} %get-tuple-element.82, ...), branch_computations={%region_8.0_spmd, %region_9.0_spmd, %region_10.0_spmd, %region_11.... | conditional | bytes 4718640 | solution.py:208
  109.5 4.6 %collective-permute-start.13 = (bf16[4,128,768]{2,1,0:T(8,128)(2,1)S(1)}, bf16[4,128,768]{2,1,0:T(8,128)(2,1)S(1)}, u32[]{:S(2)}, u32[]{:S(2)}) collective-permute-start(bf16[4,128,768]{2,1,0:T(8,128)(2,1)S(1)} %param.15), channel_id=1, source_target_pairs={{0,112},{8,120},{16,96},{24,104},{32,80},{40,88},{48,64},{56,72},{... | collective-permute-start | bytes 2359304 | tf_op jit(solution)/shard_map/cond/branch_7_fun/ppermute | solution.py:63
  114.1 11.8 %collective-permute-done.13 = bf16[4,128,768]{2,1,0:T(8,128)(2,1)S(1)} collective-permute-done((bf16[4,128,768]{2,1,0:T(8,128)(2,1)S(1)}, bf16[4,128,768]{2,1,0:T(8,128)(2,1)S(1)}, u32[]{:S(2)}, u32[]{:S(2)}) %collective-permute-start.13) | collective-permute-done | bytes 786464 | tf_op jit(solution)/shard_map/cond/branch_7_fun/ppermute | solution.py:63
  125.9 45.8 %conditional.6 = (bf16[4,128,768]{2,1,0:T(8,128)(2,1)S(1)}) conditional(s32[]{:T(128)} %bitcast.6, bf16[4,128,768]{2,1,0:T(8,128)(2,1)S(1)} %get-tuple-element.83, bf16[4,128,768]{2,1,0:T(8,128)(2,1)S(1)} %get-tuple-element.83, bf16[4,128,768]{2,1,0:T(8,128)(2,1)S(1)} %get-tuple-element.83, ...), branch_computations={%region_16.0_spmd, %region_17.0_spmd, %region_18.0_spmd, %region_1... | conditional | bytes 4718640 | solution.py:208
  125.9 14.2 %collective-permute-start.14 = (bf16[4,128,768]{2,1,0:T(8,128)(2,1)S(1)}, bf16[4,128,768]{2,1,0:T(8,128)(2,1)S(1)}, u32[]{:S(2)}, u32[]{:S(2)}) collective-permute-start(bf16[4,128,768]{2,1,0:T(8,128)(2,1)S(1)} %param.17), channel_id=1, source_target_pairs={{0,16},{8,24},{16,0},{24,8},{32,48},{40,56},{48,32},{56,40},{64,80... | collective-permute-start | bytes 2359304 | tf_op jit(solution)/shard_map/cond/branch_1_fun/ppermute | solution.py:63
  140.1 31.3 %collective-permute-done.14 = bf16[4,128,768]{2,1,0:T(8,128)(2,1)S(1)} collective-permute-done((bf16[4,128,768]{2,1,0:T(8,128)(2,1)S(1)}, bf16[4,128,768]{2,1,0:T(8,128)(2,1)S(1)}, u32[]{:S(2)}, u32[]{:S(2)}) %collective-permute-start.14) | collective-permute-done | bytes 786464 | tf_op jit(solution)/shard_map/cond/branch_1_fun/ppermute | solution.py:63
  172.6 11.0 %collective-permute-start.39 = (bf16[128,768]{1,0:T(8,128)(2,1)S(1)}, bf16[128,768]{1,0:T(8,128)(2,1)S(1)}, u32[]{:S(2)}, u32[]{:S(2)}) collective-permute-start(bf16[128,768]{1,0:T(8,128)(2,1)S(1)} %copy-done.14), channel_id=1, source_target_pairs={{0,2},{1,3},{2,4},{3,5},{4,6},{5,7},{6,0},{7,1},{8,10},{9,11},{10,... | collective-permute-start | bytes 589832 | tf_op jit(solution)/shard_map/ppermute | solution.py:67
  183.6 1.9 collective-permute-start.35
  189.3 1.9 collective-permute-start.38
  192.8 3.5 %collective-permute-start.42 = (bf16[4,128,256]{2,1,0:T(8,128)(2,1)S(1)}, bf16[4,128,256]{2,1,0:T(8,128)(2,1)}, u32[]{:S(2)}, u32[]{:S(2)}) collective-permute-start(bf16[4,128,256]{2,1,0:T(8,128)(2,1)S(1)} %pad_maximum_fusion.1), channel_id=1, source_target_pairs={{0,1},{1,0},{2,3},{3,2},{4,5},{5,4},{6,7},{7,6},{8,9},{9,8},{10,11... | collective-permute-start | bytes 786440 | tf_op jit(solution)/shard_map/ppermute | solution.py:215
  197.3 4.1 %collective-permute-start.43 = (bf16[4,128,256]{2,1,0:T(8,128)(2,1)S(1)}, bf16[4,128,256]{2,1,0:T(8,128)(2,1)}, u32[]{:S(2)}, u32[]{:S(2)}) collective-permute-start(bf16[4,128,256]{2,1,0:T(8,128)(2,1)S(1)} %pad_maximum_fusion.2), channel_id=1, source_target_pairs={{0,1},{1,0},{2,3},{3,2},{4,5},{5,4},{6,7},{7,6},{8,9},{9,8},{10,11... | collective-permute-start | bytes 786440 | tf_op jit(solution)/shard_map/ppermute | solution.py:215
  202.1 1.5 collective-permute-done.36.refs_10_
  204.4 2.4 collective-permute-start.44
  206.8 7.0 %collective-permute-done.44.refs_18_ = bf16[4,128,256]{2,1,0:T(8,128)(2,1)} collective-permute-done((bf16[4,128,256]{2,1,0:T(8,128)(2,1)S(1)}, bf16[4,128,256]{2,1,0:T(8,128)(2,1)}, u32[]{:S(2)}, u32[]{:S(2)}) %collective-permute-start.44) | collective-permute-done | bytes 262176 | tf_op jit(solution)/shard_map/ppermute | solution.py:215
  213.8 38.9 %attend.1 = (bf16[512,512]{1,0:T(8,128)(2,1)}, bf16[512,512]{1,0:T(8,128)(2,1)}, bf16[512,512]{1,0:T(8,128)(2,1)}, bf16[512,512]{1,0:T(8,128)(2,1)}) custom-call(s32[2]{0:T(128)} %pad_add_fusion.z_ref.where_ref, s32[1,32]{1,0:T(1,128)} %docs_ref.1, bf16[4,128,768]{2,1,0:T(8,128)(2,1)S(1)} %get-tuple-element.109.refs_0_, ...), custom_call_target="tpu_custom_call" | custom-call | tf_op jit(solution)/shard_map/attend/pallas_call | solution.py:164
  252.6 16.0 %collective-permute-start.46 = (bf16[512,512]{1,0:T(8,128)(2,1)}, bf16[512,512]{1,0:T(8,128)(2,1)S(1)}, u32[]{:S(2)}, u32[]{:S(2)}) collective-permute-start(bf16[512,512]{1,0:T(8,128)(2,1)} %get-tuple-element.86), channel_id=1, source_target_pairs={{0,2},{1,3},{2,4},{3,5},{4,6},{5,7},{6,0},{7,1},{8,10},{9,11},{10,... | collective-permute-start | bytes 1572872 | tf_op jit(solution)/shard_map/ppermute | solution.py:67
  268.6 3.0 collective-permute-start.47
  271.6 2.0 collective-permute-start.48
  273.5 7.1 %collective-permute-done.46 = bf16[512,512]{1,0:T(8,128)(2,1)S(1)} collective-permute-done((bf16[512,512]{1,0:T(8,128)(2,1)}, bf16[512,512]{1,0:T(8,128)(2,1)S(1)}, u32[]{:S(2)}, u32[]{:S(2)}) %collective-permute-start.46) | collective-permute-done | bytes 524320 | tf_op jit(solution)/shard_map/ppermute | solution.py:67
  280.6 13.1 %collective-permute-done.47 = bf16[512,512]{1,0:T(8,128)(2,1)S(1)} collective-permute-done((bf16[512,512]{1,0:T(8,128)(2,1)}, bf16[512,512]{1,0:T(8,128)(2,1)S(1)}, u32[]{:S(2)}, u32[]{:S(2)}) %collective-permute-start.47) | collective-permute-done | bytes 524320 | tf_op jit(solution)/shard_map/ppermute | solution.py:67
  294.5 1.5 pad_maximum_fusion
  297.2 13.9 %fusion = bf16[1,512,4096]{2,1,0:T(8,128)(2,1)} fusion(bf16[2048,4096]{1,0:T(8,128)(2,1)} %all-gather.2.cloned.1.call-done, bf16[512,512]{1,0:T(8,128)(2,1)S(1)} %get-tuple-element.90, bf16[512,512]{1,0:T(8,128)(2,1)} %get-tuple-element.91, bf16[512,512]{1,0:T(8,128)(2,1)} %get-tuple-element.92, bf16[512,512]{1,0:T(8,128)(2,1)S(1)} %get-tuple-element.89), kind=kOutput, calls=%fused_computation.1 | convolution fusion | flops 8600420352 | bytes 23068672 | tf_op jit(solution)/shard_map/dot_general | solution.py:225
  (91 shorter events, 19.1 us)
Async XLA Ops:
  6.5 290.6 %all-gather.2.cloned.1.call-start = ((), (), s32[]{:S(2)}) async-start(), calls=%async_computation | async-start | bytes 17825792 | tf_op jit(solution)/shard_map/all_gather | solution.py:216
  6.5 7.9 %collective-permute-start.28 = (bf16[512,2048]{1,0:T(8,128)(2,1)}, bf16[512,2048]{1,0:T(8,128)(2,1)}, u32[]{:S(2)}, u32[]{:S(2)}) collective-permute-start(bf16[512,2048]{1,0:T(8,128)(2,1)} %bitcast.71), channel_id=1, source_target_pairs={{0,8},{8,0},{16,24},{24,16},{32,40},{40,32},{48,56},{56,48},{64,72... | collective-permute-start | bytes 6291464 | tf_op jit(solution)/shard_map/ppermute | solution.py:201
  7.9 5.5 %collective-permute-start.29 = (bf16[512,1024]{1,0:T(8,128)(2,1)}, bf16[512,1024]{1,0:T(8,128)(2,1)S(1)}, u32[]{:S(2)}, u32[]{:S(2)}) collective-permute-start(bf16[512,1024]{1,0:T(8,128)(2,1)} %bitcast.73), channel_id=1, source_target_pairs={{0,8},{8,0},{16,24},{24,16},{32,40},{40,32},{48,56},{56,48},{64,72... | collective-permute-start | bytes 3145736 | tf_op jit(solution)/shard_map/ppermute | solution.py:202
  18.7 20.0 %collective-permute-start.23 = (bf16[4,128,768]{2,1,0:T(8,128)(2,1)S(1)}, bf16[4,128,768]{2,1,0:T(8,128)(2,1)S(1)}, u32[]{:S(2)}, u32[]{:S(2)}) collective-permute-start(bf16[4,128,768]{2,1,0:T(8,128)(2,1)S(1)} %param.27), channel_id=1, source_target_pairs={{0,48},{8,56},{16,32},{24,40},{32,16},{40,24},{48,0},{56,8},{64,11... | collective-permute-start | bytes 2359304 | tf_op jit(solution)/shard_map/cond/branch_3_fun/ppermute | solution.py:63
  74.2 23.3 %collective-permute-start = (bf16[4,128,768]{2,1,0:T(8,128)(2,1)S(1)}, bf16[4,128,768]{2,1,0:T(8,128)(2,1)S(1)}, u32[]{:S(2)}, u32[]{:S(2)}) collective-permute-start(bf16[4,128,768]{2,1,0:T(8,128)(2,1)S(1)} %param.1), channel_id=1, source_target_pairs={{0,16},{8,24},{16,0},{24,8},{32,48},{40,56},{48,32},{56,40},{64,80... | collective-permute-start | bytes 2359304 | tf_op jit(solution)/shard_map/cond/branch_1_fun/ppermute | solution.py:63
  99.1 72.9 %collective-permute-start.32 = (bf16[128,768]{1,0:T(8,128)(2,1)}, bf16[128,768]{1,0:T(8,128)(2,1)S(1)}, u32[]{:S(2)}, u32[]{:S(2)}) collective-permute-start(bf16[128,768]{1,0:T(8,128)(2,1)} %get-tuple-element.102), channel_id=1, source_target_pairs={{0,6},{1,7},{2,0},{3,1},{4,2},{5,3},{6,4},{7,5},{8,14},{9,15},{10,... | collective-permute-start | bytes 589832 | tf_op jit(solution)/shard_map/ppermute | solution.py:67
  99.1 84.6 %collective-permute-start.31 = (bf16[128,768]{1,0:T(8,128)(2,1)}, bf16[128,768]{1,0:T(8,128)(2,1)S(1)}, u32[]{:S(2)}, u32[]{:S(2)}) collective-permute-start(bf16[128,768]{1,0:T(8,128)(2,1)} %get-tuple-element.103), channel_id=1, source_target_pairs={{0,4},{1,5},{2,6},{3,7},{4,0},{5,1},{6,2},{7,3},{8,12},{9,13},{10,... | collective-permute-start | bytes 589832 | tf_op jit(solution)/shard_map/ppermute | solution.py:67
  105.9 79.6 %collective-permute-start.30 = (bf16[128,768]{1,0:T(8,128)(2,1)}, bf16[128,768]{1,0:T(8,128)(2,1)}, u32[]{:S(2)}, u32[]{:S(2)}) collective-permute-start(bf16[128,768]{1,0:T(8,128)(2,1)} %get-tuple-element.104), channel_id=1, source_target_pairs={{0,2},{1,3},{2,4},{3,5},{4,6},{5,7},{6,0},{7,1},{8,10},{9,11},{10,... | collective-permute-start | bytes 589832 | tf_op jit(solution)/shard_map/ppermute | solution.py:67
  107.7 80.0 %collective-permute-start.41 = (bf16[128,768]{1,0:T(8,128)(2,1)}, bf16[128,768]{1,0:T(8,128)(2,1)}, u32[]{:S(2)}, u32[]{:S(2)}) collective-permute-start(bf16[128,768]{1,0:T(8,128)(2,1)} %get-tuple-element.93), channel_id=1, source_target_pairs={{0,6},{1,7},{2,0},{3,1},{4,2},{5,3},{6,4},{7,5},{8,14},{9,15},{10,... | collective-permute-start | bytes 589832 | tf_op jit(solution)/shard_map/ppermute | solution.py:67
  109.5 16.4 %collective-permute-start.13 = (bf16[4,128,768]{2,1,0:T(8,128)(2,1)S(1)}, bf16[4,128,768]{2,1,0:T(8,128)(2,1)S(1)}, u32[]{:S(2)}, u32[]{:S(2)}) collective-permute-start(bf16[4,128,768]{2,1,0:T(8,128)(2,1)S(1)} %param.15), channel_id=1, source_target_pairs={{0,112},{8,120},{16,96},{24,104},{32,80},{40,88},{48,64},{56,72},{... | collective-permute-start | bytes 2359304 | tf_op jit(solution)/shard_map/cond/branch_7_fun/ppermute | solution.py:63
  125.9 45.5 %collective-permute-start.14 = (bf16[4,128,768]{2,1,0:T(8,128)(2,1)S(1)}, bf16[4,128,768]{2,1,0:T(8,128)(2,1)S(1)}, u32[]{:S(2)}, u32[]{:S(2)}) collective-permute-start(bf16[4,128,768]{2,1,0:T(8,128)(2,1)S(1)} %param.17), channel_id=1, source_target_pairs={{0,16},{8,24},{16,0},{24,8},{32,48},{40,56},{48,32},{56,40},{64,80... | collective-permute-start | bytes 2359304 | tf_op jit(solution)/shard_map/cond/branch_1_fun/ppermute | solution.py:63
  171.7 20.3 %copy-start.13 = (bf16[1,128,256]{2,1,0:T(8,128)(2,1)S(1)}, bf16[1,128,256]{2,1,0:T(8,128)(2,1)}, u32[]{:S(2)}) copy-start(bf16[1,128,256]{2,1,0:T(8,128)(2,1)} %slice.140) | copy-start | bytes 196612
  171.7 20.3 %copy-start.12 = (bf16[1,128,256]{2,1,0:T(8,128)(2,1)S(1)}, bf16[1,128,256]{2,1,0:T(8,128)(2,1)}, u32[]{:S(2)}) copy-start(bf16[1,128,256]{2,1,0:T(8,128)(2,1)} %slice.152) | copy-start | bytes 196612
  171.7 17.6 %collective-permute-start.40 = (bf16[128,768]{1,0:T(8,128)(2,1)}, bf16[128,768]{1,0:T(8,128)(2,1)S(1)}, u32[]{:S(2)}, u32[]{:S(2)}) collective-permute-start(bf16[128,768]{1,0:T(8,128)(2,1)} %get-tuple-element.94), channel_id=1, source_target_pairs={{0,4},{1,5},{2,6},{3,7},{4,0},{5,1},{6,2},{7,3},{8,12},{9,13},{10,... | collective-permute-start | bytes 589832 | tf_op jit(solution)/shard_map/ppermute | solution.py:67
  172.0 41.8 %copy-start.2 = (bf16[128,768]{1,0:T(8,128)(2,1)}, bf16[128,768]{1,0:T(8,128)(2,1)S(1)}, u32[]{:S(2)}) copy-start(bf16[128,768]{1,0:T(8,128)(2,1)S(1)} %collective-permute-done.32.refs_6_) | copy-start | bytes 589828
  172.6 18.6 %collective-permute-start.39 = (bf16[128,768]{1,0:T(8,128)(2,1)S(1)}, bf16[128,768]{1,0:T(8,128)(2,1)S(1)}, u32[]{:S(2)}, u32[]{:S(2)}) collective-permute-start(bf16[128,768]{1,0:T(8,128)(2,1)S(1)} %copy-done.14), channel_id=1, source_target_pairs={{0,2},{1,3},{2,4},{3,5},{4,6},{5,7},{6,0},{7,1},{8,10},{9,11},{10,... | collective-permute-start | bytes 589832 | tf_op jit(solution)/shard_map/ppermute | solution.py:67
  183.6 30.1 %copy-start.3 = (bf16[128,768]{1,0:T(8,128)(2,1)}, bf16[128,768]{1,0:T(8,128)(2,1)S(1)}, u32[]{:S(2)}) copy-start(bf16[128,768]{1,0:T(8,128)(2,1)S(1)} %collective-permute-done.31.refs_5_) | copy-start | bytes 589828
  183.6 8.4 %collective-permute-start.35 = (bf16[128,768]{1,0:T(8,128)(2,1)S(1)}, bf16[128,768]{1,0:T(8,128)(2,1)S(1)}, u32[]{:S(2)}, u32[]{:S(2)}) collective-permute-start(bf16[128,768]{1,0:T(8,128)(2,1)S(1)} %get-tuple-element.99), channel_id=1, source_target_pairs={{0,6},{1,7},{2,0},{3,1},{4,2},{5,3},{6,4},{7,5},{8,14},{9,15},{10,... | collective-permute-start | bytes 589832 | tf_op jit(solution)/shard_map/ppermute | solution.py:67
  185.5 7.3 %collective-permute-start.34 = (bf16[128,768]{1,0:T(8,128)(2,1)S(1)}, bf16[128,768]{1,0:T(8,128)(2,1)S(1)}, u32[]{:S(2)}, u32[]{:S(2)}) collective-permute-start(bf16[128,768]{1,0:T(8,128)(2,1)S(1)} %get-tuple-element.100), channel_id=1, source_target_pairs={{0,4},{1,5},{2,6},{3,7},{4,0},{5,1},{6,2},{7,3},{8,12},{9,13},{10,... | collective-permute-start | bytes 589832 | tf_op jit(solution)/shard_map/ppermute | solution.py:67
  187.7 8.6 %collective-permute-start.33 = (bf16[128,768]{1,0:T(8,128)(2,1)S(1)}, bf16[128,768]{1,0:T(8,128)(2,1)S(1)}, u32[]{:S(2)}, u32[]{:S(2)}) collective-permute-start(bf16[128,768]{1,0:T(8,128)(2,1)S(1)} %get-tuple-element.101), channel_id=1, source_target_pairs={{0,2},{1,3},{2,4},{3,5},{4,6},{5,7},{6,0},{7,1},{8,10},{9,11},{10,... | collective-permute-start | bytes 589832 | tf_op jit(solution)/shard_map/ppermute | solution.py:67
  189.3 8.0 %collective-permute-start.38 = (bf16[128,768]{1,0:T(8,128)(2,1)S(1)}, bf16[128,768]{1,0:T(8,128)(2,1)S(1)}, u32[]{:S(2)}, u32[]{:S(2)}) collective-permute-start(bf16[128,768]{1,0:T(8,128)(2,1)S(1)} %get-tuple-element.96), channel_id=1, source_target_pairs={{0,6},{1,7},{2,0},{3,1},{4,2},{5,3},{6,4},{7,5},{8,14},{9,15},{10,... | collective-permute-start | bytes 589832 | tf_op jit(solution)/shard_map/ppermute | solution.py:67
  191.3 10.2 %collective-permute-start.37 = (bf16[128,768]{1,0:T(8,128)(2,1)S(1)}, bf16[128,768]{1,0:T(8,128)(2,1)S(1)}, u32[]{:S(2)}, u32[]{:S(2)}) collective-permute-start(bf16[128,768]{1,0:T(8,128)(2,1)S(1)} %get-tuple-element.97), channel_id=1, source_target_pairs={{0,4},{1,5},{2,6},{3,7},{4,0},{5,1},{6,2},{7,3},{8,12},{9,13},{10,... | collective-permute-start | bytes 589832 | tf_op jit(solution)/shard_map/ppermute | solution.py:67
  192.1 11.6 %collective-permute-start.36 = (bf16[128,768]{1,0:T(8,128)(2,1)S(1)}, bf16[128,768]{1,0:T(8,128)(2,1)S(1)}, u32[]{:S(2)}, u32[]{:S(2)}) collective-permute-start(bf16[128,768]{1,0:T(8,128)(2,1)S(1)} %get-tuple-element.98), channel_id=1, source_target_pairs={{0,2},{1,3},{2,4},{3,5},{4,6},{5,7},{6,0},{7,1},{8,10},{9,11},{10,... | collective-permute-start | bytes 589832 | tf_op jit(solution)/shard_map/ppermute | solution.py:67
  192.8 3.5 %copy-start.7 = (bf16[128,768]{1,0:T(8,128)(2,1)}, bf16[128,768]{1,0:T(8,128)(2,1)S(1)}, u32[]{:S(2)}) copy-start(bf16[128,768]{1,0:T(8,128)(2,1)S(1)} %collective-permute-done.34.refs_8_) | copy-start | bytes 589828
  192.8 13.9 %collective-permute-start.42 = (bf16[4,128,256]{2,1,0:T(8,128)(2,1)S(1)}, bf16[4,128,256]{2,1,0:T(8,128)(2,1)}, u32[]{:S(2)}, u32[]{:S(2)}) collective-permute-start(bf16[4,128,256]{2,1,0:T(8,128)(2,1)S(1)} %pad_maximum_fusion.1), channel_id=1, source_target_pairs={{0,1},{1,0},{2,3},{3,2},{4,5},{5,4},{6,7},{7,6},{8,9},{9,8},{10,11... | collective-permute-start | bytes 786440 | tf_op jit(solution)/shard_map/ppermute | solution.py:215
  196.3 10.5 %collective-permute-start.45 = (bf16[4,128,256]{2,1,0:T(8,128)(2,1)S(1)}, bf16[4,128,256]{2,1,0:T(8,128)(2,1)}, u32[]{:S(2)}, u32[]{:S(2)}) collective-permute-start(bf16[4,128,256]{2,1,0:T(8,128)(2,1)S(1)} %pad_maximum_fusion.4), channel_id=1, source_target_pairs={{0,1},{1,0},{2,3},{3,2},{4,5},{5,4},{6,7},{7,6},{8,9},{9,8},{10,11... | collective-permute-start | bytes 786440 | tf_op jit(solution)/shard_map/ppermute | solution.py:215
  197.3 4.1 %copy-start.9 = (bf16[128,768]{1,0:T(8,128)(2,1)}, bf16[128,768]{1,0:T(8,128)(2,1)S(1)}, u32[]{:S(2)}) copy-start(bf16[128,768]{1,0:T(8,128)(2,1)S(1)} %collective-permute-done.38.refs_12_) | copy-start | bytes 589828
  197.3 9.4 %collective-permute-start.43 = (bf16[4,128,256]{2,1,0:T(8,128)(2,1)S(1)}, bf16[4,128,256]{2,1,0:T(8,128)(2,1)}, u32[]{:S(2)}, u32[]{:S(2)}) collective-permute-start(bf16[4,128,256]{2,1,0:T(8,128)(2,1)S(1)} %pad_maximum_fusion.2), channel_id=1, source_target_pairs={{0,1},{1,0},{2,3},{3,2},{4,5},{5,4},{6,7},{7,6},{8,9},{9,8},{10,11... | collective-permute-start | bytes 786440 | tf_op jit(solution)/shard_map/ppermute | solution.py:215
  204.4 9.4 %collective-permute-start.44 = (bf16[4,128,256]{2,1,0:T(8,128)(2,1)S(1)}, bf16[4,128,256]{2,1,0:T(8,128)(2,1)}, u32[]{:S(2)}, u32[]{:S(2)}) collective-permute-start(bf16[4,128,256]{2,1,0:T(8,128)(2,1)S(1)} %pad_maximum_fusion.3), channel_id=1, source_target_pairs={{0,1},{1,0},{2,3},{3,2},{4,5},{5,4},{6,7},{7,6},{8,9},{9,8},{10,11... | collective-permute-start | bytes 786440 | tf_op jit(solution)/shard_map/ppermute | solution.py:215
  252.6 28.0 %collective-permute-start.46 = (bf16[512,512]{1,0:T(8,128)(2,1)}, bf16[512,512]{1,0:T(8,128)(2,1)S(1)}, u32[]{:S(2)}, u32[]{:S(2)}) collective-permute-start(bf16[512,512]{1,0:T(8,128)(2,1)} %get-tuple-element.86), channel_id=1, source_target_pairs={{0,2},{1,3},{2,4},{3,5},{4,6},{5,7},{6,0},{7,1},{8,10},{9,11},{10,... | collective-permute-start | bytes 1572872 | tf_op jit(solution)/shard_map/ppermute | solution.py:67
  268.6 25.2 %collective-permute-start.47 = (bf16[512,512]{1,0:T(8,128)(2,1)}, bf16[512,512]{1,0:T(8,128)(2,1)S(1)}, u32[]{:S(2)}, u32[]{:S(2)}) collective-permute-start(bf16[512,512]{1,0:T(8,128)(2,1)} %get-tuple-element.87), channel_id=1, source_target_pairs={{0,4},{1,5},{2,6},{3,7},{4,0},{5,1},{6,2},{7,3},{8,12},{9,13},{10,... | collective-permute-start | bytes 1572872 | tf_op jit(solution)/shard_map/ppermute | solution.py:67
  271.6 22.2 %collective-permute-start.48 = (bf16[512,512]{1,0:T(8,128)(2,1)}, bf16[512,512]{1,0:T(8,128)(2,1)S(1)}, u32[]{:S(2)}, u32[]{:S(2)}) collective-permute-start(bf16[512,512]{1,0:T(8,128)(2,1)} %get-tuple-element.88), channel_id=1, source_target_pairs={{0,6},{1,7},{2,0},{3,1},{4,2},{5,3},{6,4},{7,5},{8,14},{9,15},{10,... | collective-permute-start | bytes 1572872 | tf_op jit(solution)/shard_map/ppermute | solution.py:67
  (9 other events, 8.3 us)
Sparse Core Ops, SparseCore 0:
  71.9 121.8 all-gather.1
where the time goes:
time: 318 us
  waiting for transfers between devices  115 us (36%)
  starting transfers between devices  82.6 us (26%)
  Pallas kernels  76 us (24%)
  between operations  16.2 us (5%)
  matrix products  13.9 us (4%)
  local copies, waits for them, and re-layouts  11.4 us (4%)
    ppermute x4, waiting for transfers between devices, moves(): yield (lambda x, code=code: lax.ppermute(x, 'dp', flip(code << 1)))  83.7 us
    ppermute x15, starting transfers between devices, z_shift(): lax.ppermute(x, 'seq', [(s, (s // 2 + k) % 4 * 2 + s % 2) for s in range(...  48.8 us
    pallas_call x1, Pallas kernels, attend(): pl.pallas_call(attend_kernel, grid=(1,), out_shape=[jax.ShapeDtypeStruct(...  38.9 us
    pallas_call x1, Pallas kernels, tie(): pl.pallas_call(tie_kernel, out_shape=jax.ShapeDtypeStruct(weight.shape, w...  32.9 us
    ppermute x15, waiting for transfers between devices, z_shift(): lax.ppermute(x, 'seq', [(s, (s // 2 + k) % 4 * 2 + s % 2) for s in range(...  21.8 us
    ppermute x4, starting transfers between devices, moves(): yield (lambda x, code=code: lax.ppermute(x, 'dp', flip(code << 1)))  21.5 us
    dot_general x1, matrix products, body(): out = jnp.dot(attended, weight, preferred_element_type=jnp.float32)  13.9 us
    ppermute x4, starting transfers between devices, body(): other.append(lax.ppermute(mine, 'seq', [(s, s ^ 1) for s in range(8)]))  10.9 us
  transfers between devices with their start and end apart: 26, of which 9 were waited for; matrix products, arithmetic and copies ran while one was open for 3% of the time, Pallas kernels for 12%

commit v1 on v0

--- a/solution.py
+++ b/solution.py
@@ -13,8 +13,9 @@
 GQ = 512
 GK = 256
 GW = GQ + GK
-TILE = 4
+TILE = 2
 PAD = TILE - 1
+CHAINS = 1
 NB = 32
 NEG = -1e30
 
@@ -67,7 +68,7 @@
     return lax.ppermute(x, "seq", [(s, (((s // 2) + k) % 4) * 2 + s % 2) for s in range(8)])
 
 
-def attend_kernel(where_ref, docs_ref, *refs):
+def attend_kernel(where_ref, starts_ref, *refs):
     own = [[refs[j]] + [refs[4 + 3 * j + k] for k in range(3)] for j in range(4)]
     other = refs[16:20]
     outs = refs[20:24]
@@ -94,7 +95,7 @@
 
     factor = math.log2(math.e) / math.sqrt(HEAD_DIM)
     keys = TILE * BLOCK
-    lanes = 2 * BLOCK
+    lanes = 4 // CHAINS * BLOCK
     key_row = lax.broadcasted_iota(jnp.int32, (BLOCK, lanes), 0)
     query_row = lax.broadcasted_iota(jnp.int32, (BLOCK, lanes), 1) % BLOCK
     causal = key_row <= query_row
@@ -104,11 +105,8 @@
 
         def per_block(j, _, k=k, zd=zd):
             place = (zd * 2 + h) * 4 + j
-            doc = docs_ref[0, place]
-            start = lax.fori_loop(
-                0, NB, lambda n, c: c + jnp.where(docs_ref[0, n] < doc, 1, 0), jnp.int32(0)
-            )
-            qs = [q_all[zd * 4 + j, i * lanes : (i + 1) * lanes, :] for i in range(2)]
+            start = starts_ref[0, place]
+            qs = [q_all[zd * 4 + j, i * lanes : (i + 1) * lanes, :] for i in range(CHAINS)]
 
             def tile(n, states, first):
                 base = place - n * TILE
@@ -141,14 +139,14 @@
                         new.append((peak, state[1] * keep + w_sum, state[2] * keep + mixed))
                 return tuple(new)
 
-            states = tile(0, (None, None), True)
+            states = tile(0, (None,) * CHAINS, True)
             count = (place - start) // TILE + 1
             states = lax.fori_loop(1, count, lambda n, st: tile(n, st, False), states)
             rows = pl.ds(pl.multiple_of(j * BLOCK, BLOCK), BLOCK)
             for i, (_, total, acc) in enumerate(states):
                 done = acc / total
-                for g in range(2):
-                    cols = (2 * i + g) * HEAD_DIM
+                for g in range(4 // CHAINS):
+                    cols = (4 // CHAINS * i + g) * HEAD_DIM
                     outs[k][rows, cols : cols + HEAD_DIM] = done[
                         :, g * BLOCK : (g + 1) * BLOCK
                     ].T.astype(jnp.bfloat16)
@@ -157,7 +155,7 @@
         lax.fori_loop(0, 4, per_block, 0)
 
 
-def attend(where, docs, blocks, pieces, other):
+def attend(where, starts, blocks, pieces, other):
     vmem = pl.BlockSpec(memory_space=pltpu.VMEM)
     smem = pl.BlockSpec(memory_space=pltpu.SMEM)
     first = pl.BlockSpec((1, BLOCK, GW), lambda i: (0, 0, 0))
@@ -173,23 +171,42 @@
             pltpu.VMEM((NB + PAD, HEAD_DIM, BLOCK), jnp.bfloat16),
         ],
         name="attend",
-    )(where, docs, *blocks, *pieces, *other)
-
-
-def tie_kernel(w_ref, token_ref, out_ref, sem):
-    copy = pltpu.make_async_copy(w_ref, out_ref, sem)
-    copy.start()
-    copy.wait()
+    )(where, starts, *blocks, *pieces, *other)
+
+
+def collect_kernel(*refs):
+    out = refs[-1]
+    out[0] = refs[0][0]
+    for k in range(1, GROUPS):
+        out[k] = refs[k][...]
+
+
+def collect(block, came):
+    first = pl.BlockSpec((1, BLOCK, GK), lambda i: (0, 0, GQ // GK))
+    rest = pl.BlockSpec((BLOCK, GK), lambda i: (0, GQ // GK))
+    return pl.pallas_call(
+        collect_kernel,
+        grid=(1,),
+        out_shape=jax.ShapeDtypeStruct((GROUPS, BLOCK, GK), block.dtype),
+        in_specs=[first] + [rest] * 3,
+        out_specs=pl.BlockSpec((GROUPS, BLOCK, GK), lambda i: (0, 0, 0)),
+        name="collect",
+    )(block, *came)
+
+
+def tie_kernel(w_ref, token_ref, out_ref):
+    out_ref[...] = w_ref[...]
 
 
 def tie(weight, token):
-    any_spec = pl.BlockSpec(memory_space=pl.ANY)
+    rows, cols = weight.shape
+    spec = pl.BlockSpec((rows, cols // 2), lambda i: (0, i))
     return pl.pallas_call(
         tie_kernel,
+        grid=(2,),
         out_shape=jax.ShapeDtypeStruct(weight.shape, weight.dtype),
-        in_specs=[any_spec] * 2,
-        out_specs=any_spec,
-        scratch_shapes=[pltpu.SemaphoreType.DMA],
+        in_specs=[spec, pl.BlockSpec(memory_space=pl.ANY)],
+        out_specs=spec,
         name="tie",
     )(weight, token)
 
@@ -201,6 +218,8 @@
     qs = lax.ppermute(q, "dp", flip(1))
     kvs = lax.ppermute(kv, "dp", flip(1))
     where = jnp.stack([z, h]).astype(jnp.int32)
+    docs = doc_blocks[0]
+    starts = jnp.sum((docs[None, :] < docs[:, None]).astype(jnp.int32), axis=1)[None]
     blocks = list(prep(where, route_plan, q, qs, kv, kvs))
 
     pieces, other = [], []
@@ -211,11 +230,11 @@
         for k in range(1, 4):
             came.append(z_shift(block[k], k))
         pieces += came
-        mine = jnp.stack([block[0, :, GQ:]] + [piece[:, GQ:] for piece in came])
+        mine = collect(block, came)
         other.append(lax.ppermute(mine, "seq", [(s, s ^ 1) for s in range(8)]))
-    weight = lax.all_gather(tie(out_weight, blocks[3]), "dp", axis=0, tiled=True)
-
-    outs = attend(where, doc_blocks, blocks, pieces, other)
+    weight = lax.all_gather(tie(out_weight, blocks[2]), "dp", axis=0, tiled=True)
+
+    outs = attend(where, starts, blocks, pieces, other)
     parts = [outs[0]] + [z_shift(outs[k], k) for k in range(1, 4)]
     stacked = jnp.stack(parts)
     attended = jnp.concatenate(

time: 318 us -> 280 us (0.88)
  Pallas kernels: 76 us -> 45 us
  waiting for transfers between devices: 115 us -> 99.9 us
  starting transfers between devices: 82.6 us -> 94 us
  local copies, waits for them, and re-layouts: 11.4 us -> 7.9 us
    ppermute x15, starting transfers between devices: 48.8 us -> 75 us  [z_shift(): lax.ppermute(x, 'seq', [(s, (s // 2 + k) % 4 * 2 + s % 2) for s in range(...]
    pallas_call x1 -> x5, Pallas kernels: 32.9 us -> 8.58 us  [the longest x4 6.53 us: collect(): pl.pallas_call(collect_kernel, grid=(1,), out_shape=jax.ShapeDtypeStruct(...]
    ppermute x4, waiting for transfers between devices: 83.7 us -> 65.1 us  [moves(): yield (lambda x, code=code: lax.ppermute(x, 'dp', flip(code << 1)))]
    ppermute x4, starting transfers between devices: 21.5 us -> 8.63 us  [moves(): yield (lambda x, code=code: lax.ppermute(x, 'dp', flip(code << 1)))]
    pallas_call x1, Pallas kernels: 38.9 us -> 32.2 us  [attend(): pl.pallas_call(attend_kernel, grid=(1,), out_shape=[jax.ShapeDtypeStruct(...]
  transfers between devices with their start and end apart: 26 -> 26, of which waited for: 9 -> 9; matrix products, arithmetic and copies ran while one was open for 3% -> 3% of each run, Pallas kernels for 12% -> 14%
where the time goes in v1:
time: 280 us
  waiting for transfers between devices  99.9 us (36%)
  starting transfers between devices  94 us (34%)
  Pallas kernels  45 us (16%)
  between operations  16 us (6%)
  matrix products  13.9 us (5%)
  local copies, waits for them, and re-layouts  7.9 us (3%)
  other arithmetic  2.83 us (1%)
    ppermute x15, starting transfers between devices, z_shift(): lax.ppermute(x, 'seq', [(s, (s // 2 + k) % 4 * 2 + s % 2) for s in range(...  75 us
    ppermute x4, waiting for transfers between devices, moves(): yield (lambda x, code=code: lax.ppermute(x, 'dp', flip(code << 1)))  65.1 us
    pallas_call x1, Pallas kernels, attend(): pl.pallas_call(attend_kernel, grid=(1,), out_shape=[jax.ShapeDtypeStruct(...  32.2 us
    ppermute x15, waiting for transfers between devices, z_shift(): lax.ppermute(x, 'seq', [(s, (s // 2 + k) % 4 * 2 + s % 2) for s in range(...  24.1 us
    dot_general x1, matrix products, body(): out = jnp.dot(attended, weight, preferred_element_type=jnp.float32)  13.9 us
    ppermute x4, starting transfers between devices, body(): other.append(lax.ppermute(mine, 'seq', [(s, s ^ 1) for s in range(8)]))  9.04 us
    ppermute x4, starting transfers between devices, moves(): yield (lambda x, code=code: lax.ppermute(x, 'dp', flip(code << 1)))  8.63 us
    ppermute x4, waiting for transfers between devices, body(): other.append(lax.ppermute(mine, 'seq', [(s, s ^ 1) for s in range(8)]))  7.93 us
  transfers between devices with their start and end apart: 26, of which 9 were waited for; matrix products, arithmetic and copies ran while one was open for 3% of the time, Pallas kernels for 14%

profile of v1, /device:TPU:1, one launch (start us, length us, event | category | flops | bytes accessed | tf_op | source)
XLA Modules:
  0.0 280.0 jit_solution(6102355031626413258)
XLA Ops:
  7.9 1.5 fusion.9
  10.6 2.8 collective-permute-done.29.ks_ref
  14.4 4.3 %prep.1 = (bf16[4,128,768]{2,1,0:T(8,128)(2,1)S(1)}, bf16[4,128,768]{2,1,0:T(8,128)(2,1)S(1)}, bf16[4,128,768]{2,1,0:T(8,128)(2,1)S(1)}, bf16[4,128,768]{2,1,0:T(8,128)(2,1)S(1)}) custom-call(s32[2]{0:T(128)} %pad_add_fusion.z_ref.where_ref, s32[1,4]{1,0:T(1,128)} %marks_ref.1, bf16[512,2048]{1,0:T(8,128)(2,1)} %bitcast.50, ...), custom_call_target="tpu_custom_call" | custom-call | tf_op jit(solution)/shard_map/prep/pallas_call | solution.py:44
  18.7 18.9 %conditional.6 = (bf16[4,128,768]{2,1,0:T(8,128)(2,1)S(1)}) conditional(s32[]{:T(128)} %bitcast.8, bf16[4,128,768]{2,1,0:T(8,128)(2,1)S(1)} %get-tuple-element.83, bf16[4,128,768]{2,1,0:T(8,128)(2,1)S(1)} %get-tuple-element.83, bf16[4,128,768]{2,1,0:T(8,128)(2,1)S(1)} %get-tuple-element.83, ...), branch_computations={%region_17.0_spmd, %region_18.0_spmd, %region_19.0_spmd, %region_2... | conditional | bytes 4718640 | solution.py:227
  20.1 17.4 %collective-permute-done.14 = bf16[4,128,768]{2,1,0:T(8,128)(2,1)S(1)} collective-permute-done((bf16[4,128,768]{2,1,0:T(8,128)(2,1)S(1)}, bf16[4,128,768]{2,1,0:T(8,128)(2,1)S(1)}, u32[]{:S(2)}, u32[]{:S(2)}) %collective-permute-start.14) | collective-permute-done | bytes 786464 | tf_op jit(solution)/shard_map/cond/branch_1_fun/ppermute | solution.py:64
  37.6 2.1 tie.1
  41.6 21.3 %conditional.4 = (bf16[4,128,768]{2,1,0:T(8,128)(2,1)S(1)}) conditional(s32[]{:T(128)} %bitcast.4, bf16[4,128,768]{2,1,0:T(8,128)(2,1)S(1)} %get-tuple-element.81, bf16[4,128,768]{2,1,0:T(8,128)(2,1)S(1)} %get-tuple-element.81, bf16[4,128,768]{2,1,0:T(8,128)(2,1)S(1)} %get-tuple-element.81, ...), branch_computations={%region_1.0_spmd, %region_2.0_spmd, %region_3.0_spmd, %region_4.0_... | conditional | bytes 4718640 | solution.py:227
  43.0 19.8 %collective-permute-done = bf16[4,128,768]{2,1,0:T(8,128)(2,1)S(1)} collective-permute-done((bf16[4,128,768]{2,1,0:T(8,128)(2,1)S(1)}, bf16[4,128,768]{2,1,0:T(8,128)(2,1)S(1)}, u32[]{:S(2)}, u32[]{:S(2)}) %collective-permute-start) | collective-permute-done | bytes 786464 | tf_op jit(solution)/shard_map/cond/branch_1_fun/ppermute | solution.py:64
  63.7 6.7 %collective-permute-start.31 = (bf16[128,768]{1,0:T(8,128)(2,1)}, bf16[128,768]{1,0:T(8,128)(2,1)S(1)}, u32[]{:S(2)}, u32[]{:S(2)}) collective-permute-start(bf16[128,768]{1,0:T(8,128)(2,1)} %get-tuple-element.103), channel_id=1, source_target_pairs={{0,4},{1,5},{2,6},{3,7},{4,0},{5,1},{6,2},{7,3},{8,12},{9,13},{10,... | collective-permute-start | bytes 589832 | tf_op jit(solution)/shard_map/ppermute | solution.py:68
  72.1 1.8 collective-permute-start.38
  73.9 16.4 %conditional.5 = (bf16[4,128,768]{2,1,0:T(8,128)(2,1)S(1)}) conditional(s32[]{:T(128)} %bitcast.7, bf16[4,128,768]{2,1,0:T(8,128)(2,1)S(1)} %get-tuple-element.82, bf16[4,128,768]{2,1,0:T(8,128)(2,1)S(1)} %get-tuple-element.82, bf16[4,128,768]{2,1,0:T(8,128)(2,1)S(1)} %get-tuple-element.82, ...), branch_computations={%region_9.0_spmd, %region_10.0_spmd, %region_11.0_spmd, %region_12... | conditional | bytes 4718640 | solution.py:227
  73.9 4.6 %collective-permute-start.13 = (bf16[4,128,768]{2,1,0:T(8,128)(2,1)S(1)}, bf16[4,128,768]{2,1,0:T(8,128)(2,1)S(1)}, u32[]{:S(2)}, u32[]{:S(2)}) collective-permute-start(bf16[4,128,768]{2,1,0:T(8,128)(2,1)S(1)} %param.15), channel_id=1, source_target_pairs={{0,112},{8,120},{16,96},{24,104},{32,80},{40,88},{48,64},{56,72},{... | collective-permute-start | bytes 2359304 | tf_op jit(solution)/shard_map/cond/branch_7_fun/ppermute | solution.py:64
  78.5 11.8 %collective-permute-done.13 = bf16[4,128,768]{2,1,0:T(8,128)(2,1)S(1)} collective-permute-done((bf16[4,128,768]{2,1,0:T(8,128)(2,1)S(1)}, bf16[4,128,768]{2,1,0:T(8,128)(2,1)S(1)}, u32[]{:S(2)}, u32[]{:S(2)}) %collective-permute-start.13) | collective-permute-done | bytes 786464 | tf_op jit(solution)/shard_map/cond/branch_7_fun/ppermute | solution.py:64
  90.4 17.6 %conditional.7 = (bf16[4,128,768]{2,1,0:T(8,128)(2,1)S(1)}) conditional(s32[]{:T(128)} %bitcast.9, bf16[4,128,768]{2,1,0:T(8,128)(2,1)S(1)} %get-tuple-element.84, bf16[4,128,768]{2,1,0:T(8,128)(2,1)S(1)} %get-tuple-element.84, bf16[4,128,768]{2,1,0:T(8,128)(2,1)S(1)} %get-tuple-element.84, ...), branch_computations={%region_25.0_spmd, %region_26.0_spmd, %region_27.0_spmd, %region_2... | conditional | bytes 4718640 | solution.py:227
  91.7 16.1 %collective-permute-done.23 = bf16[4,128,768]{2,1,0:T(8,128)(2,1)S(1)} collective-permute-done((bf16[4,128,768]{2,1,0:T(8,128)(2,1)S(1)}, bf16[4,128,768]{2,1,0:T(8,128)(2,1)S(1)}, u32[]{:S(2)}, u32[]{:S(2)}) %collective-permute-start.23) | collective-permute-done | bytes 786464 | tf_op jit(solution)/shard_map/cond/branch_3_fun/ppermute | solution.py:64
  108.0 40.0 %collective-permute-start.37 = (bf16[128,768]{1,0:T(8,128)(2,1)}, bf16[128,768]{1,0:T(8,128)(2,1)}, u32[]{:S(2)}, u32[]{:S(2)}) collective-permute-start(bf16[128,768]{1,0:T(8,128)(2,1)} %get-tuple-element.97), channel_id=1, source_target_pairs={{0,4},{1,5},{2,6},{3,7},{4,0},{5,1},{6,2},{7,3},{8,12},{9,13},{10,... | collective-permute-start | bytes 589832 | tf_op jit(solution)/shard_map/ppermute | solution.py:68
  148.8 2.7 collective-permute-start.35
  152.9 2.1 collective-permute-start.41
  155.1 1.7 collective-permute-start.40
  156.8 1.6 collect.4
  158.4 1.6 collect.6
  160.8 4.6 %collective-permute-start.42 = (bf16[4,128,256]{2,1,0:T(8,128)(2,1)}, bf16[4,128,256]{2,1,0:T(8,128)(2,1)S(1)}, u32[]{:S(2)}, u32[]{:S(2)}) collective-permute-start(bf16[4,128,256]{2,1,0:T(8,128)(2,1)} %collect.4), channel_id=1, source_target_pairs={{0,1},{1,0},{2,3},{3,2},{4,5},{5,4},{6,7},{7,6},{8,9},{9,8},{10,11... | collective-permute-start | bytes 786440 | tf_op jit(solution)/shard_map/ppermute | solution.py:234
  165.5 2.3 collective-permute-start.44
  167.7 1.6 collect.5
  170.0 3.3 %collective-permute-done.39.refs_1_.refs_13_ = bf16[128,768]{1,0:T(8,128)(2,1)} collective-permute-done((bf16[128,768]{1,0:T(8,128)(2,1)}, bf16[128,768]{1,0:T(8,128)(2,1)}, u32[]{:S(2)}, u32[]{:S(2)}) %collective-permute-start.39) | collective-permute-done | bytes 196640 | tf_op jit(solution)/shard_map/ppermute | solution.py:68
  173.4 1.6 collect.7
  177.2 7.9 %collective-permute-done.45.refs_19_ = bf16[4,128,256]{2,1,0:T(8,128)(2,1)} collective-permute-done((bf16[4,128,256]{2,1,0:T(8,128)(2,1)}, bf16[4,128,256]{2,1,0:T(8,128)(2,1)}, u32[]{:S(2)}, u32[]{:S(2)}) %collective-permute-start.45) | collective-permute-done | bytes 262176 | tf_op jit(solution)/shard_map/ppermute | solution.py:234
  185.1 32.2 %attend.1 = (bf16[512,512]{1,0:T(8,128)(2,1)}, bf16[512,512]{1,0:T(8,128)(2,1)}, bf16[512,512]{1,0:T(8,128)(2,1)}, bf16[512,512]{1,0:T(8,128)(2,1)}) custom-call(s32[2]{0:T(128)} %pad_add_fusion.z_ref.where_ref, s32[1,32]{1,0:T(1,128)} %bitcast.57, bf16[4,128,768]{2,1,0:T(8,128)(2,1)S(1)} %get-tuple-element.109.refs_0_, ...), custom_call_target="tpu_custom_call" | custom-call | tf_op jit(solution)/shard_map/attend/pallas_call | solution.py:162
  217.3 16.5 %collective-permute-start.47 = (bf16[512,512]{1,0:T(8,128)(2,1)}, bf16[512,512]{1,0:T(8,128)(2,1)S(1)}, u32[]{:S(2)}, u32[]{:S(2)}) collective-permute-start(bf16[512,512]{1,0:T(8,128)(2,1)} %get-tuple-element.87), channel_id=1, source_target_pairs={{0,4},{1,5},{2,6},{3,7},{4,0},{5,1},{6,2},{7,3},{8,12},{9,13},{10,... | collective-permute-start | bytes 1572872 | tf_op jit(solution)/shard_map/ppermute | solution.py:68
  233.8 2.0 collective-permute-start.48
  235.8 20.0 %collective-permute-done.47 = bf16[512,512]{1,0:T(8,128)(2,1)S(1)} collective-permute-done((bf16[512,512]{1,0:T(8,128)(2,1)}, bf16[512,512]{1,0:T(8,128)(2,1)S(1)}, u32[]{:S(2)}, u32[]{:S(2)}) %collective-permute-start.47) | collective-permute-done | bytes 524320 | tf_op jit(solution)/shard_map/ppermute | solution.py:68
  259.2 13.9 %fusion = bf16[1,512,4096]{2,1,0:T(8,128)(2,1)} fusion(bf16[2048,4096]{1,0:T(8,128)(2,1)} %all-gather.2.cloned.1.call-done, bf16[512,512]{1,0:T(8,128)(2,1)S(1)} %get-tuple-element.90, bf16[512,512]{1,0:T(8,128)(2,1)} %get-tuple-element.91, bf16[512,512]{1,0:T(8,128)(2,1)} %get-tuple-element.92, bf16[512,512]{1,0:T(8,128)(2,1)S(1)} %get-tuple-element.89), kind=kOutput, calls=%fused_computation.1 | convolution fusion | flops 8600420352 | bytes 23068672 | tf_op jit(solution)/shard_map/dot_general | solution.py:244
  (58 shorter events, 19.1 us)
Async XLA Ops:
  6.5 252.7 %all-gather.2.cloned.1.call-start = ((), (), s32[]{:S(2)}) async-start(), calls=%async_computation | async-start | bytes 17825792 | tf_op jit(solution)/shard_map/all_gather | solution.py:235
  6.5 7.9 %collective-permute-start.28 = (bf16[512,2048]{1,0:T(8,128)(2,1)}, bf16[512,2048]{1,0:T(8,128)(2,1)}, u32[]{:S(2)}, u32[]{:S(2)}) collective-permute-start(bf16[512,2048]{1,0:T(8,128)(2,1)} %bitcast.49), channel_id=1, source_target_pairs={{0,8},{8,0},{16,24},{24,16},{32,40},{40,32},{48,56},{56,48},{64,72... | collective-permute-start | bytes 6291464 | tf_op jit(solution)/shard_map/ppermute | solution.py:218
  7.9 5.5 %collective-permute-start.29 = (bf16[512,1024]{1,0:T(8,128)(2,1)}, bf16[512,1024]{1,0:T(8,128)(2,1)S(1)}, u32[]{:S(2)}, u32[]{:S(2)}) collective-permute-start(bf16[512,1024]{1,0:T(8,128)(2,1)} %bitcast.51), channel_id=1, source_target_pairs={{0,8},{8,0},{16,24},{24,16},{32,40},{40,32},{48,56},{56,48},{64,72... | collective-permute-start | bytes 3145736 | tf_op jit(solution)/shard_map/ppermute | solution.py:219
  13.4 1.0 copy-start
  18.7 18.8 %collective-permute-start.14 = (bf16[4,128,768]{2,1,0:T(8,128)(2,1)S(1)}, bf16[4,128,768]{2,1,0:T(8,128)(2,1)S(1)}, u32[]{:S(2)}, u32[]{:S(2)}) collective-permute-start(bf16[4,128,768]{2,1,0:T(8,128)(2,1)S(1)} %param.17), channel_id=1, source_target_pairs={{0,16},{8,24},{16,0},{24,8},{32,48},{40,56},{48,32},{56,40},{64,80... | collective-permute-start | bytes 2359304 | tf_op jit(solution)/shard_map/cond/branch_1_fun/ppermute | solution.py:64
  41.6 21.2 %collective-permute-start = (bf16[4,128,768]{2,1,0:T(8,128)(2,1)S(1)}, bf16[4,128,768]{2,1,0:T(8,128)(2,1)S(1)}, u32[]{:S(2)}, u32[]{:S(2)}) collective-permute-start(bf16[4,128,768]{2,1,0:T(8,128)(2,1)S(1)} %param.1), channel_id=1, source_target_pairs={{0,16},{8,24},{16,0},{24,8},{32,48},{40,56},{48,32},{56,40},{64,80... | collective-permute-start | bytes 2359304 | tf_op jit(solution)/shard_map/cond/branch_1_fun/ppermute | solution.py:64
  63.7 85.1 %collective-permute-start.32 = (bf16[128,768]{1,0:T(8,128)(2,1)}, bf16[128,768]{1,0:T(8,128)(2,1)S(1)}, u32[]{:S(2)}, u32[]{:S(2)}) collective-permute-start(bf16[128,768]{1,0:T(8,128)(2,1)} %get-tuple-element.102), channel_id=1, source_target_pairs={{0,6},{1,7},{2,0},{3,1},{4,2},{5,3},{6,4},{7,5},{8,14},{9,15},{10,... | collective-permute-start | bytes 589832 | tf_op jit(solution)/shard_map/ppermute | solution.py:68
  63.7 85.1 %collective-permute-start.31 = (bf16[128,768]{1,0:T(8,128)(2,1)}, bf16[128,768]{1,0:T(8,128)(2,1)S(1)}, u32[]{:S(2)}, u32[]{:S(2)}) collective-permute-start(bf16[128,768]{1,0:T(8,128)(2,1)} %get-tuple-element.103), channel_id=1, source_target_pairs={{0,4},{1,5},{2,6},{3,7},{4,0},{5,1},{6,2},{7,3},{8,12},{9,13},{10,... | collective-permute-start | bytes 589832 | tf_op jit(solution)/shard_map/ppermute | solution.py:68
  70.4 81.9 %collective-permute-start.30 = (bf16[128,768]{1,0:T(8,128)(2,1)}, bf16[128,768]{1,0:T(8,128)(2,1)}, u32[]{:S(2)}, u32[]{:S(2)}) collective-permute-start(bf16[128,768]{1,0:T(8,128)(2,1)} %get-tuple-element.104), channel_id=1, source_target_pairs={{0,2},{1,3},{2,4},{3,5},{4,6},{5,7},{6,0},{7,1},{8,10},{9,11},{10,... | collective-permute-start | bytes 589832 | tf_op jit(solution)/shard_map/ppermute | solution.py:68
  72.1 80.2 %collective-permute-start.38 = (bf16[128,768]{1,0:T(8,128)(2,1)}, bf16[128,768]{1,0:T(8,128)(2,1)}, u32[]{:S(2)}, u32[]{:S(2)}) collective-permute-start(bf16[128,768]{1,0:T(8,128)(2,1)} %get-tuple-element.96), channel_id=1, source_target_pairs={{0,6},{1,7},{2,0},{3,1},{4,2},{5,3},{6,4},{7,5},{8,14},{9,15},{10,... | collective-permute-start | bytes 589832 | tf_op jit(solution)/shard_map/ppermute | solution.py:68
  73.9 16.4 %collective-permute-start.13 = (bf16[4,128,768]{2,1,0:T(8,128)(2,1)S(1)}, bf16[4,128,768]{2,1,0:T(8,128)(2,1)S(1)}, u32[]{:S(2)}, u32[]{:S(2)}) collective-permute-start(bf16[4,128,768]{2,1,0:T(8,128)(2,1)S(1)} %param.15), channel_id=1, source_target_pairs={{0,112},{8,120},{16,96},{24,104},{32,80},{40,88},{48,64},{56,72},{... | collective-permute-start | bytes 2359304 | tf_op jit(solution)/shard_map/cond/branch_7_fun/ppermute | solution.py:64
  90.4 17.3 %collective-permute-start.23 = (bf16[4,128,768]{2,1,0:T(8,128)(2,1)S(1)}, bf16[4,128,768]{2,1,0:T(8,128)(2,1)S(1)}, u32[]{:S(2)}, u32[]{:S(2)}) collective-permute-start(bf16[4,128,768]{2,1,0:T(8,128)(2,1)S(1)} %param.27), channel_id=1, source_target_pairs={{0,48},{8,56},{16,32},{24,40},{32,16},{40,24},{48,0},{56,8},{64,11... | collective-permute-start | bytes 2359304 | tf_op jit(solution)/shard_map/cond/branch_3_fun/ppermute | solution.py:64
  108.0 44.9 %collective-permute-start.37 = (bf16[128,768]{1,0:T(8,128)(2,1)}, bf16[128,768]{1,0:T(8,128)(2,1)}, u32[]{:S(2)}, u32[]{:S(2)}) collective-permute-start(bf16[128,768]{1,0:T(8,128)(2,1)} %get-tuple-element.97), channel_id=1, source_target_pairs={{0,4},{1,5},{2,6},{3,7},{4,0},{5,1},{6,2},{7,3},{8,12},{9,13},{10,... | collective-permute-start | bytes 589832 | tf_op jit(solution)/shard_map/ppermute | solution.py:68
  148.8 8.0 %copy-start.1 = (bf16[128,768]{1,0:T(8,128)(2,1)}, bf16[128,768]{1,0:T(8,128)(2,1)S(1)}, u32[]{:S(2)}) copy-start(bf16[128,768]{1,0:T(8,128)(2,1)S(1)} %collective-permute-done.32.refs_3_.refs_6_) | copy-start | bytes 589828
  148.8 6.3 %collective-permute-start.36 = (bf16[128,768]{1,0:T(8,128)(2,1)}, bf16[128,768]{1,0:T(8,128)(2,1)}, u32[]{:S(2)}, u32[]{:S(2)}) collective-permute-start(bf16[128,768]{1,0:T(8,128)(2,1)} %get-tuple-element.98), channel_id=1, source_target_pairs={{0,2},{1,3},{2,4},{3,5},{4,6},{5,7},{6,0},{7,1},{8,10},{9,11},{10,... | collective-permute-start | bytes 589832 | tf_op jit(solution)/shard_map/ppermute | solution.py:68
  148.8 8.0 %copy-start.2 = (bf16[128,768]{1,0:T(8,128)(2,1)}, bf16[128,768]{1,0:T(8,128)(2,1)S(1)}, u32[]{:S(2)}) copy-start(bf16[128,768]{1,0:T(8,128)(2,1)S(1)} %collective-permute-done.31.refs_2_.refs_5_) | copy-start | bytes 589828
  148.8 8.0 %collective-permute-start.35 = (bf16[128,768]{1,0:T(8,128)(2,1)S(1)}, bf16[128,768]{1,0:T(8,128)(2,1)}, u32[]{:S(2)}, u32[]{:S(2)}) collective-permute-start(bf16[128,768]{1,0:T(8,128)(2,1)S(1)} %get-tuple-element.99), channel_id=1, source_target_pairs={{0,6},{1,7},{2,0},{3,1},{4,2},{5,3},{6,4},{7,5},{8,14},{9,15},{10,... | collective-permute-start | bytes 589832 | tf_op jit(solution)/shard_map/ppermute | solution.py:68
  152.3 8.5 %collective-permute-start.34 = (bf16[128,768]{1,0:T(8,128)(2,1)}, bf16[128,768]{1,0:T(8,128)(2,1)}, u32[]{:S(2)}, u32[]{:S(2)}) collective-permute-start(bf16[128,768]{1,0:T(8,128)(2,1)} %get-tuple-element.100), channel_id=1, source_target_pairs={{0,4},{1,5},{2,6},{3,7},{4,0},{5,1},{6,2},{7,3},{8,12},{9,13},{10,... | collective-permute-start | bytes 589832 | tf_op jit(solution)/shard_map/ppermute | solution.py:68
  152.3 13.1 %collective-permute-start.33 = (bf16[128,768]{1,0:T(8,128)(2,1)}, bf16[128,768]{1,0:T(8,128)(2,1)}, u32[]{:S(2)}, u32[]{:S(2)}) collective-permute-start(bf16[128,768]{1,0:T(8,128)(2,1)} %get-tuple-element.101), channel_id=1, source_target_pairs={{0,2},{1,3},{2,4},{3,5},{4,6},{5,7},{6,0},{7,1},{8,10},{9,11},{10,... | collective-permute-start | bytes 589832 | tf_op jit(solution)/shard_map/ppermute | solution.py:68
  152.9 16.4 %collective-permute-start.41 = (bf16[128,768]{1,0:T(8,128)(2,1)}, bf16[128,768]{1,0:T(8,128)(2,1)}, u32[]{:S(2)}, u32[]{:S(2)}) collective-permute-start(bf16[128,768]{1,0:T(8,128)(2,1)} %get-tuple-element.93), channel_id=1, source_target_pairs={{0,6},{1,7},{2,0},{3,1},{4,2},{5,3},{6,4},{7,5},{8,14},{9,15},{10,... | collective-permute-start | bytes 589832 | tf_op jit(solution)/shard_map/ppermute | solution.py:68
  155.1 15.0 %collective-permute-start.40 = (bf16[128,768]{1,0:T(8,128)(2,1)}, bf16[128,768]{1,0:T(8,128)(2,1)}, u32[]{:S(2)}, u32[]{:S(2)}) collective-permute-start(bf16[128,768]{1,0:T(8,128)(2,1)} %get-tuple-element.94), channel_id=1, source_target_pairs={{0,4},{1,5},{2,6},{3,7},{4,0},{5,1},{6,2},{7,3},{8,12},{9,13},{10,... | collective-permute-start | bytes 589832 | tf_op jit(solution)/shard_map/ppermute | solution.py:68
  156.8 16.6 %collective-permute-start.39 = (bf16[128,768]{1,0:T(8,128)(2,1)}, bf16[128,768]{1,0:T(8,128)(2,1)}, u32[]{:S(2)}, u32[]{:S(2)}) collective-permute-start(bf16[128,768]{1,0:T(8,128)(2,1)} %get-tuple-element.95), channel_id=1, source_target_pairs={{0,2},{1,3},{2,4},{3,5},{4,6},{5,7},{6,0},{7,1},{8,10},{9,11},{10,... | collective-permute-start | bytes 589832 | tf_op jit(solution)/shard_map/ppermute | solution.py:68
  158.4 18.0 %copy-start.5 = (s32[1,32]{1,0:T(1,128)S(1)}, s32[1,32]{1,0:T(1,128)}, u32[]{:S(2)}) copy-start(s32[1,32]{1,0:T(1,128)} %param.39) | copy-start | bytes 388
  160.8 16.4 %collective-permute-start.42 = (bf16[4,128,256]{2,1,0:T(8,128)(2,1)}, bf16[4,128,256]{2,1,0:T(8,128)(2,1)S(1)}, u32[]{:S(2)}, u32[]{:S(2)}) collective-permute-start(bf16[4,128,256]{2,1,0:T(8,128)(2,1)} %collect.4), channel_id=1, source_target_pairs={{0,1},{1,0},{2,3},{3,2},{4,5},{5,4},{6,7},{7,6},{8,9},{9,8},{10,11... | collective-permute-start | bytes 786440 | tf_op jit(solution)/shard_map/ppermute | solution.py:234
  165.5 11.8 %collective-permute-start.44 = (bf16[4,128,256]{2,1,0:T(8,128)(2,1)}, bf16[4,128,256]{2,1,0:T(8,128)(2,1)}, u32[]{:S(2)}, u32[]{:S(2)}) collective-permute-start(bf16[4,128,256]{2,1,0:T(8,128)(2,1)} %collect.6), channel_id=1, source_target_pairs={{0,1},{1,0},{2,3},{3,2},{4,5},{5,4},{6,7},{7,6},{8,9},{9,8},{10,11... | collective-permute-start | bytes 786440 | tf_op jit(solution)/shard_map/ppermute | solution.py:234
  169.4 7.8 %collective-permute-start.43 = (bf16[4,128,256]{2,1,0:T(8,128)(2,1)}, bf16[4,128,256]{2,1,0:T(8,128)(2,1)}, u32[]{:S(2)}, u32[]{:S(2)}) collective-permute-start(bf16[4,128,256]{2,1,0:T(8,128)(2,1)} %collect.5), channel_id=1, source_target_pairs={{0,1},{1,0},{2,3},{3,2},{4,5},{5,4},{6,7},{7,6},{8,9},{9,8},{10,11... | collective-permute-start | bytes 786440 | tf_op jit(solution)/shard_map/ppermute | solution.py:234
  175.0 10.1 %collective-permute-start.45 = (bf16[4,128,256]{2,1,0:T(8,128)(2,1)}, bf16[4,128,256]{2,1,0:T(8,128)(2,1)}, u32[]{:S(2)}, u32[]{:S(2)}) collective-permute-start(bf16[4,128,256]{2,1,0:T(8,128)(2,1)} %collect.7), channel_id=1, source_target_pairs={{0,1},{1,0},{2,3},{3,2},{4,5},{5,4},{6,7},{7,6},{8,9},{9,8},{10,11... | collective-permute-start | bytes 786440 | tf_op jit(solution)/shard_map/ppermute | solution.py:234
  177.2 7.9 %copy-start.4 = (bf16[4,128,256]{2,1,0:T(8,128)(2,1)}, bf16[4,128,256]{2,1,0:T(8,128)(2,1)S(1)}, u32[]{:S(2)}) copy-start(bf16[4,128,256]{2,1,0:T(8,128)(2,1)S(1)} %collective-permute-done.42.refs_16_) | copy-start | bytes 786436
  217.3 18.5 %collective-permute-start.46 = (bf16[512,512]{1,0:T(8,128)(2,1)}, bf16[512,512]{1,0:T(8,128)(2,1)S(1)}, u32[]{:S(2)}, u32[]{:S(2)}) collective-permute-start(bf16[512,512]{1,0:T(8,128)(2,1)} %get-tuple-element.86), channel_id=1, source_target_pairs={{0,2},{1,3},{2,4},{3,5},{4,6},{5,7},{6,0},{7,1},{8,10},{9,11},{10,... | collective-permute-start | bytes 1572872 | tf_op jit(solution)/shard_map/ppermute | solution.py:68
  217.3 38.5 %collective-permute-start.47 = (bf16[512,512]{1,0:T(8,128)(2,1)}, bf16[512,512]{1,0:T(8,128)(2,1)S(1)}, u32[]{:S(2)}, u32[]{:S(2)}) collective-permute-start(bf16[512,512]{1,0:T(8,128)(2,1)} %get-tuple-element.87), channel_id=1, source_target_pairs={{0,4},{1,5},{2,6},{3,7},{4,0},{5,1},{6,2},{7,3},{8,12},{9,13},{10,... | collective-permute-start | bytes 1572872 | tf_op jit(solution)/shard_map/ppermute | solution.py:68
  233.8 22.0 %collective-permute-start.48 = (bf16[512,512]{1,0:T(8,128)(2,1)}, bf16[512,512]{1,0:T(8,128)(2,1)S(1)}, u32[]{:S(2)}, u32[]{:S(2)}) collective-permute-start(bf16[512,512]{1,0:T(8,128)(2,1)} %get-tuple-element.88), channel_id=1, source_target_pairs={{0,6},{1,7},{2,0},{3,1},{4,2},{5,3},{6,4},{7,5},{8,14},{9,15},{10,... | collective-permute-start | bytes 1572872 | tf_op jit(solution)/shard_map/ppermute | solution.py:68
  255.8 0.8 copy-start.3
Sparse Core Ops, SparseCore 0:
  39.8 124.8 all-gather.1

commit v2 on v1

--- a/solution.py
+++ b/solution.py
@@ -194,6 +194,39 @@
     )(block, *came)
 
 
+def project_kernel(where_ref, *refs):
+    parts, w_ref, out_ref, rows = refs[:4], refs[4], refs[5], refs[6]
+
+    @pl.when(pl.program_id(0) == 0)
+    def _():
+        for k, part in enumerate(parts):
+            group = (where_ref[0] + GROUPS - k) % GROUPS
+            rows[:, pl.ds(pl.multiple_of(group * GQ, GQ), GQ)] = part[...]
+
+    out_ref[...] = jnp.dot(rows[...], w_ref[...], preferred_element_type=jnp.float32).astype(
+        out_ref.dtype
+    )
+
+
+def project(where, parts, weight):
+    depth, cols = weight.shape
+    count = parts[0].shape[0]
+    wide = 512
+    part = pl.BlockSpec((count, GQ), lambda i, w: (0, 0))
+    return pl.pallas_call(
+        project_kernel,
+        out_shape=jax.ShapeDtypeStruct((count, cols), weight.dtype),
+        grid_spec=pltpu.PrefetchScalarGridSpec(
+            num_scalar_prefetch=1,
+            grid=(cols // wide,),
+            in_specs=[part] * 4 + [pl.BlockSpec((depth, wide), lambda i, w: (0, i))],
+            out_specs=pl.BlockSpec((count, wide), lambda i, w: (0, i)),
+            scratch_shapes=[pltpu.VMEM((count, depth), weight.dtype)],
+        ),
+        name="project",
+    )(where, *parts, weight)
+
+
 def tie_kernel(w_ref, token_ref, out_ref):
     out_ref[...] = w_ref[...]
 
@@ -236,13 +269,7 @@
 
     outs = attend(where, starts, blocks, pieces, other)
     parts = [outs[0]] + [z_shift(outs[k], k) for k in range(1, 4)]
-    stacked = jnp.stack(parts)
-    attended = jnp.concatenate(
-        [lax.dynamic_index_in_dim(stacked, (z + 4 - c) & 3, 0, keepdims=False) for c in range(4)],
-        axis=1,
-    )
-    out = jnp.dot(attended, weight, preferred_element_type=jnp.float32)
-    return out.astype(jnp.bfloat16)[None]
+    return project(where, parts, weight)[None]
 
 
 def solution(mesh):

time: 280 us -> 280 us (level)
  Pallas kernels: 45 us -> 60.8 us
  matrix products: 13.9 us -> 0 us
    pallas_call x0 -> x1, Pallas kernels: none -> 15.8 us  [project(): pl.pallas_call(project_kernel, out_shape=jax.ShapeDtypeStruct((count, col...]
    dot_general x1 -> x0, matrix products: 13.9 us -> none  [body(): out = jnp.dot(attended, weight, preferred_element_type=jnp.float32)]
  transfers between devices with their start and end apart: 26 -> 26, of which waited for: 9 -> 9; matrix products, arithmetic and copies ran while one was open for 3% -> 2% of each run, Pallas kernels for 14% -> 14%
where the time goes in v2:
time: 280 us; the launch traced here: 279 us
  waiting for transfers between devices  99.9 us (36%)
  starting transfers between devices  94 us (34%)
  Pallas kernels  60.8 us (22%)
  between operations  16 us (6%)
  local copies, waits for them, and re-layouts  6.94 us (2%)
    ppermute x15, starting transfers between devices, z_shift(): lax.ppermute(x, 'seq', [(s, (s // 2 + k) % 4 * 2 + s % 2) for s in range(...  75 us
    ppermute x4, waiting for transfers between devices, moves(): yield (lambda x, code=code: lax.ppermute(x, 'dp', flip(code << 1)))  65 us
    pallas_call x1, Pallas kernels, attend(): pl.pallas_call(attend_kernel, grid=(1,), out_shape=[jax.ShapeDtypeStruct(...  32.1 us
    ppermute x15, waiting for transfers between devices, z_shift(): lax.ppermute(x, 'seq', [(s, (s // 2 + k) % 4 * 2 + s % 2) for s in range(...  24.1 us
    pallas_call x1, Pallas kernels, project(): pl.pallas_call(project_kernel, out_shape=jax.ShapeDtypeStruct((count, col...  15.8 us
    ppermute x4, starting transfers between devices, body(): other.append(lax.ppermute(mine, 'seq', [(s, s ^ 1) for s in range(8)]))  9 us
    ppermute x4, starting transfers between devices, moves(): yield (lambda x, code=code: lax.ppermute(x, 'dp', flip(code << 1)))  8.63 us
    ppermute x4, waiting for transfers between devices, body(): other.append(lax.ppermute(mine, 'seq', [(s, s ^ 1) for s in range(8)]))  7.92 us
  transfers between devices with their start and end apart: 26, of which 9 were waited for; matrix products, arithmetic and copies ran while one was open for 2% of the time, Pallas kernels for 14%

profile of v2, /device:TPU:1, one launch (start us, length us, event | category | flops | bytes accessed | tf_op | source)
XLA Modules:
  0.0 279.3 jit_solution(2706973847120214016)
XLA Ops:
  7.9 1.5 fusion
  10.7 2.8 collective-permute-done.29.ks_ref
  14.4 4.3 %prep.1 = (bf16[4,128,768]{2,1,0:T(8,128)(2,1)S(1)}, bf16[4,128,768]{2,1,0:T(8,128)(2,1)S(1)}, bf16[4,128,768]{2,1,0:T(8,128)(2,1)S(1)}, bf16[4,128,768]{2,1,0:T(8,128)(2,1)S(1)}) custom-call(s32[2]{0:T(128)} %pad_add_fusion.z_ref.where_ref, s32[1,4]{1,0:T(1,128)} %marks_ref.1, bf16[512,2048]{1,0:T(8,128)(2,1)} %bitcast.36, ...), custom_call_target="tpu_custom_call" | custom-call | tf_op jit(solution)/shard_map/prep/pallas_call | solution.py:44
  18.7 18.9 %conditional.6 = (bf16[4,128,768]{2,1,0:T(8,128)(2,1)S(1)}) conditional(s32[]{:T(128)} %bitcast.8, bf16[4,128,768]{2,1,0:T(8,128)(2,1)S(1)} %get-tuple-element.83, bf16[4,128,768]{2,1,0:T(8,128)(2,1)S(1)} %get-tuple-element.83, bf16[4,128,768]{2,1,0:T(8,128)(2,1)S(1)} %get-tuple-element.83, ...), branch_computations={%region_17.0_spmd, %region_18.0_spmd, %region_19.0_spmd, %region_2... | conditional | bytes 4718640 | solution.py:260
  20.1 17.4 %collective-permute-done.14 = bf16[4,128,768]{2,1,0:T(8,128)(2,1)S(1)} collective-permute-done((bf16[4,128,768]{2,1,0:T(8,128)(2,1)S(1)}, bf16[4,128,768]{2,1,0:T(8,128)(2,1)S(1)}, u32[]{:S(2)}, u32[]{:S(2)}) %collective-permute-start.14) | collective-permute-done | bytes 786464 | tf_op jit(solution)/shard_map/cond/branch_1_fun/ppermute | solution.py:64
  37.6 2.1 tie.1
  41.5 21.2 %conditional.4 = (bf16[4,128,768]{2,1,0:T(8,128)(2,1)S(1)}) conditional(s32[]{:T(128)} %bitcast.4, bf16[4,128,768]{2,1,0:T(8,128)(2,1)S(1)} %get-tuple-element.81, bf16[4,128,768]{2,1,0:T(8,128)(2,1)S(1)} %get-tuple-element.81, bf16[4,128,768]{2,1,0:T(8,128)(2,1)S(1)} %get-tuple-element.81, ...), branch_computations={%region_1.0_spmd, %region_2.0_spmd, %region_3.0_spmd, %region_4.0_... | conditional | bytes 4718640 | solution.py:260
  42.9 19.7 %collective-permute-done = bf16[4,128,768]{2,1,0:T(8,128)(2,1)S(1)} collective-permute-done((bf16[4,128,768]{2,1,0:T(8,128)(2,1)S(1)}, bf16[4,128,768]{2,1,0:T(8,128)(2,1)S(1)}, u32[]{:S(2)}, u32[]{:S(2)}) %collective-permute-start) | collective-permute-done | bytes 786464 | tf_op jit(solution)/shard_map/cond/branch_1_fun/ppermute | solution.py:64
  63.6 6.7 %collective-permute-start.31 = (bf16[128,768]{1,0:T(8,128)(2,1)}, bf16[128,768]{1,0:T(8,128)(2,1)S(1)}, u32[]{:S(2)}, u32[]{:S(2)}) collective-permute-start(bf16[128,768]{1,0:T(8,128)(2,1)} %get-tuple-element.99), channel_id=1, source_target_pairs={{0,4},{1,5},{2,6},{3,7},{4,0},{5,1},{6,2},{7,3},{8,12},{9,13},{10,... | collective-permute-start | bytes 589832 | tf_op jit(solution)/shard_map/ppermute | solution.py:68
  72.0 1.8 collective-permute-start.38
  73.8 16.4 %conditional.5 = (bf16[4,128,768]{2,1,0:T(8,128)(2,1)S(1)}) conditional(s32[]{:T(128)} %bitcast.7, bf16[4,128,768]{2,1,0:T(8,128)(2,1)S(1)} %get-tuple-element.82, bf16[4,128,768]{2,1,0:T(8,128)(2,1)S(1)} %get-tuple-element.82, bf16[4,128,768]{2,1,0:T(8,128)(2,1)S(1)} %get-tuple-element.82, ...), branch_computations={%region_9.0_spmd, %region_10.0_spmd, %region_11.0_spmd, %region_12... | conditional | bytes 4718640 | solution.py:260
  73.8 4.6 %collective-permute-start.13 = (bf16[4,128,768]{2,1,0:T(8,128)(2,1)S(1)}, bf16[4,128,768]{2,1,0:T(8,128)(2,1)S(1)}, u32[]{:S(2)}, u32[]{:S(2)}) collective-permute-start(bf16[4,128,768]{2,1,0:T(8,128)(2,1)S(1)} %param.15), channel_id=1, source_target_pairs={{0,112},{8,120},{16,96},{24,104},{32,80},{40,88},{48,64},{56,72},{... | collective-permute-start | bytes 2359304 | tf_op jit(solution)/shard_map/cond/branch_7_fun/ppermute | solution.py:64
  78.4 11.8 %collective-permute-done.13 = bf16[4,128,768]{2,1,0:T(8,128)(2,1)S(1)} collective-permute-done((bf16[4,128,768]{2,1,0:T(8,128)(2,1)S(1)}, bf16[4,128,768]{2,1,0:T(8,128)(2,1)S(1)}, u32[]{:S(2)}, u32[]{:S(2)}) %collective-permute-start.13) | collective-permute-done | bytes 786464 | tf_op jit(solution)/shard_map/cond/branch_7_fun/ppermute | solution.py:64
  90.3 17.6 %conditional.7 = (bf16[4,128,768]{2,1,0:T(8,128)(2,1)S(1)}) conditional(s32[]{:T(128)} %bitcast.9, bf16[4,128,768]{2,1,0:T(8,128)(2,1)S(1)} %get-tuple-element.84, bf16[4,128,768]{2,1,0:T(8,128)(2,1)S(1)} %get-tuple-element.84, bf16[4,128,768]{2,1,0:T(8,128)(2,1)S(1)} %get-tuple-element.84, ...), branch_computations={%region_25.0_spmd, %region_26.0_spmd, %region_27.0_spmd, %region_2... | conditional | bytes 4718640 | solution.py:260
  91.6 16.1 %collective-permute-done.23 = bf16[4,128,768]{2,1,0:T(8,128)(2,1)S(1)} collective-permute-done((bf16[4,128,768]{2,1,0:T(8,128)(2,1)S(1)}, bf16[4,128,768]{2,1,0:T(8,128)(2,1)S(1)}, u32[]{:S(2)}, u32[]{:S(2)}) %collective-permute-start.23) | collective-permute-done | bytes 786464 | tf_op jit(solution)/shard_map/cond/branch_3_fun/ppermute | solution.py:64
  107.9 40.0 %collective-permute-start.37 = (bf16[128,768]{1,0:T(8,128)(2,1)}, bf16[128,768]{1,0:T(8,128)(2,1)}, u32[]{:S(2)}, u32[]{:S(2)}) collective-permute-start(bf16[128,768]{1,0:T(8,128)(2,1)} %get-tuple-element.93), channel_id=1, source_target_pairs={{0,4},{1,5},{2,6},{3,7},{4,0},{5,1},{6,2},{7,3},{8,12},{9,13},{10,... | collective-permute-start | bytes 589832 | tf_op jit(solution)/shard_map/ppermute | solution.py:68
  148.8 2.7 collective-permute-start.35
  152.9 2.1 collective-permute-start.41
  155.0 1.7 collective-permute-start.40
  156.8 1.6 collect.4
  158.4 1.6 collect.6
  160.8 4.6 %collective-permute-start.42 = (bf16[4,128,256]{2,1,0:T(8,128)(2,1)}, bf16[4,128,256]{2,1,0:T(8,128)(2,1)S(1)}, u32[]{:S(2)}, u32[]{:S(2)}) collective-permute-start(bf16[4,128,256]{2,1,0:T(8,128)(2,1)} %collect.4), channel_id=1, source_target_pairs={{0,1},{1,0},{2,3},{3,2},{4,5},{5,4},{6,7},{7,6},{8,9},{9,8},{10,11... | collective-permute-start | bytes 786440 | tf_op jit(solution)/shard_map/ppermute | solution.py:267
  165.4 2.3 collective-permute-start.44
  167.7 1.6 collect.5
  170.0 3.3 %collective-permute-done.39.refs_1_.refs_13_ = bf16[128,768]{1,0:T(8,128)(2,1)} collective-permute-done((bf16[128,768]{1,0:T(8,128)(2,1)}, bf16[128,768]{1,0:T(8,128)(2,1)}, u32[]{:S(2)}, u32[]{:S(2)}) %collective-permute-start.39) | collective-permute-done | bytes 196640 | tf_op jit(solution)/shard_map/ppermute | solution.py:68
  173.3 1.6 collect.7
  177.2 7.9 %collective-permute-done.45.refs_19_ = bf16[4,128,256]{2,1,0:T(8,128)(2,1)} collective-permute-done((bf16[4,128,256]{2,1,0:T(8,128)(2,1)}, bf16[4,128,256]{2,1,0:T(8,128)(2,1)}, u32[]{:S(2)}, u32[]{:S(2)}) %collective-permute-start.45) | collective-permute-done | bytes 262176 | tf_op jit(solution)/shard_map/ppermute | solution.py:267
  185.1 32.1 %attend.1 = (bf16[512,512]{1,0:T(8,128)(2,1)}, bf16[512,512]{1,0:T(8,128)(2,1)}, bf16[512,512]{1,0:T(8,128)(2,1)}, bf16[512,512]{1,0:T(8,128)(2,1)}) custom-call(s32[2]{0:T(128)} %pad_add_fusion.z_ref.where_ref, s32[1,32]{1,0:T(1,128)} %bitcast.39, bf16[4,128,768]{2,1,0:T(8,128)(2,1)S(1)} %get-tuple-element.105.refs_0_, ...), custom_call_target="tpu_custom_call" | custom-call | tf_op jit(solution)/shard_map/attend/pallas_call | solution.py:162
  217.2 16.5 %collective-permute-start.47 = (bf16[512,512]{1,0:T(8,128)(2,1)}, bf16[512,512]{1,0:T(8,128)(2,1)S(1)}, u32[]{:S(2)}, u32[]{:S(2)}) collective-permute-start(bf16[512,512]{1,0:T(8,128)(2,1)} %get-tuple-element.87), channel_id=1, source_target_pairs={{0,4},{1,5},{2,6},{3,7},{4,0},{5,1},{6,2},{7,3},{8,12},{9,13},{10,... | collective-permute-start | bytes 1572872 | tf_op jit(solution)/shard_map/ppermute | solution.py:68
  233.7 2.0 collective-permute-start.48
  235.7 20.0 %collective-permute-done.47.refs_2_ = bf16[512,512]{1,0:T(8,128)(2,1)S(1)} collective-permute-done((bf16[512,512]{1,0:T(8,128)(2,1)}, bf16[512,512]{1,0:T(8,128)(2,1)S(1)}, u32[]{:S(2)}, u32[]{:S(2)}) %collective-permute-start.47) | collective-permute-done | bytes 524320 | tf_op jit(solution)/shard_map/ppermute | solution.py:68
  256.7 15.8 %project.1 = bf16[512,4096]{1,0:T(8,128)(2,1)} custom-call(s32[2]{0:T(128)} %pad_add_fusion.z_ref.where_ref, bf16[512,512]{1,0:T(8,128)(2,1)} %get-tuple-element.85.refs_0_, bf16[512,512]{1,0:T(8,128)(2,1)} %copy-done.3, bf16[512,512]{1,0:T(8,128)(2,1)} %copy-done.4, bf16[512,512]{1,0:T(8,128)(2,1)} %copy-done.5, ...), custom_call_target="tpu_custom_call" | custom-call | tf_op jit(solution)/shard_map/project/pallas_call | solution.py:216
  (60 shorter events, 16.7 us)
Async XLA Ops:
  6.5 249.2 %all-gather.2.cloned.1.call-start = ((), (), s32[]{:S(2)}) async-start(), calls=%async_computation | async-start | bytes 17825792 | tf_op jit(solution)/shard_map/all_gather | solution.py:268
  6.5 7.9 %collective-permute-start.28 = (bf16[512,2048]{1,0:T(8,128)(2,1)}, bf16[512,2048]{1,0:T(8,128)(2,1)}, u32[]{:S(2)}, u32[]{:S(2)}) collective-permute-start(bf16[512,2048]{1,0:T(8,128)(2,1)} %bitcast.35), channel_id=1, source_target_pairs={{0,8},{8,0},{16,24},{24,16},{32,40},{40,32},{48,56},{56,48},{64,72... | collective-permute-start | bytes 6291464 | tf_op jit(solution)/shard_map/ppermute | solution.py:251
  7.9 5.5 %collective-permute-start.29 = (bf16[512,1024]{1,0:T(8,128)(2,1)}, bf16[512,1024]{1,0:T(8,128)(2,1)S(1)}, u32[]{:S(2)}, u32[]{:S(2)}) collective-permute-start(bf16[512,1024]{1,0:T(8,128)(2,1)} %bitcast.37), channel_id=1, source_target_pairs={{0,8},{8,0},{16,24},{24,16},{32,40},{40,32},{48,56},{56,48},{64,72... | collective-permute-start | bytes 3145736 | tf_op jit(solution)/shard_map/ppermute | solution.py:252
  13.4 1.0 copy-start
  18.7 18.8 %collective-permute-start.14 = (bf16[4,128,768]{2,1,0:T(8,128)(2,1)S(1)}, bf16[4,128,768]{2,1,0:T(8,128)(2,1)S(1)}, u32[]{:S(2)}, u32[]{:S(2)}) collective-permute-start(bf16[4,128,768]{2,1,0:T(8,128)(2,1)S(1)} %param.17), channel_id=1, source_target_pairs={{0,16},{8,24},{16,0},{24,8},{32,48},{40,56},{48,32},{56,40},{64,80... | collective-permute-start | bytes 2359304 | tf_op jit(solution)/shard_map/cond/branch_1_fun/ppermute | solution.py:64
  41.5 21.1 %collective-permute-start = (bf16[4,128,768]{2,1,0:T(8,128)(2,1)S(1)}, bf16[4,128,768]{2,1,0:T(8,128)(2,1)S(1)}, u32[]{:S(2)}, u32[]{:S(2)}) collective-permute-start(bf16[4,128,768]{2,1,0:T(8,128)(2,1)S(1)} %param.1), channel_id=1, source_target_pairs={{0,16},{8,24},{16,0},{24,8},{32,48},{40,56},{48,32},{56,40},{64,80... | collective-permute-start | bytes 2359304 | tf_op jit(solution)/shard_map/cond/branch_1_fun/ppermute | solution.py:64
  63.6 85.1 %collective-permute-start.32 = (bf16[128,768]{1,0:T(8,128)(2,1)}, bf16[128,768]{1,0:T(8,128)(2,1)S(1)}, u32[]{:S(2)}, u32[]{:S(2)}) collective-permute-start(bf16[128,768]{1,0:T(8,128)(2,1)} %get-tuple-element.98), channel_id=1, source_target_pairs={{0,6},{1,7},{2,0},{3,1},{4,2},{5,3},{6,4},{7,5},{8,14},{9,15},{10,... | collective-permute-start | bytes 589832 | tf_op jit(solution)/shard_map/ppermute | solution.py:68
  63.6 85.2 %collective-permute-start.31 = (bf16[128,768]{1,0:T(8,128)(2,1)}, bf16[128,768]{1,0:T(8,128)(2,1)S(1)}, u32[]{:S(2)}, u32[]{:S(2)}) collective-permute-start(bf16[128,768]{1,0:T(8,128)(2,1)} %get-tuple-element.99), channel_id=1, source_target_pairs={{0,4},{1,5},{2,6},{3,7},{4,0},{5,1},{6,2},{7,3},{8,12},{9,13},{10,... | collective-permute-start | bytes 589832 | tf_op jit(solution)/shard_map/ppermute | solution.py:68
  70.3 82.0 %collective-permute-start.30 = (bf16[128,768]{1,0:T(8,128)(2,1)}, bf16[128,768]{1,0:T(8,128)(2,1)}, u32[]{:S(2)}, u32[]{:S(2)}) collective-permute-start(bf16[128,768]{1,0:T(8,128)(2,1)} %get-tuple-element.100), channel_id=1, source_target_pairs={{0,2},{1,3},{2,4},{3,5},{4,6},{5,7},{6,0},{7,1},{8,10},{9,11},{10,... | collective-permute-start | bytes 589832 | tf_op jit(solution)/shard_map/ppermute | solution.py:68
  72.0 80.3 %collective-permute-start.38 = (bf16[128,768]{1,0:T(8,128)(2,1)}, bf16[128,768]{1,0:T(8,128)(2,1)}, u32[]{:S(2)}, u32[]{:S(2)}) collective-permute-start(bf16[128,768]{1,0:T(8,128)(2,1)} %get-tuple-element.92), channel_id=1, source_target_pairs={{0,6},{1,7},{2,0},{3,1},{4,2},{5,3},{6,4},{7,5},{8,14},{9,15},{10,... | collective-permute-start | bytes 589832 | tf_op jit(solution)/shard_map/ppermute | solution.py:68
  73.8 16.4 %collective-permute-start.13 = (bf16[4,128,768]{2,1,0:T(8,128)(2,1)S(1)}, bf16[4,128,768]{2,1,0:T(8,128)(2,1)S(1)}, u32[]{:S(2)}, u32[]{:S(2)}) collective-permute-start(bf16[4,128,768]{2,1,0:T(8,128)(2,1)S(1)} %param.15), channel_id=1, source_target_pairs={{0,112},{8,120},{16,96},{24,104},{32,80},{40,88},{48,64},{56,72},{... | collective-permute-start | bytes 2359304 | tf_op jit(solution)/shard_map/cond/branch_7_fun/ppermute | solution.py:64
  90.3 17.3 %collective-permute-start.23 = (bf16[4,128,768]{2,1,0:T(8,128)(2,1)S(1)}, bf16[4,128,768]{2,1,0:T(8,128)(2,1)S(1)}, u32[]{:S(2)}, u32[]{:S(2)}) collective-permute-start(bf16[4,128,768]{2,1,0:T(8,128)(2,1)S(1)} %param.27), channel_id=1, source_target_pairs={{0,48},{8,56},{16,32},{24,40},{32,16},{40,24},{48,0},{56,8},{64,11... | collective-permute-start | bytes 2359304 | tf_op jit(solution)/shard_map/cond/branch_3_fun/ppermute | solution.py:64
  107.9 68.4 %copy-start.7 = (s32[1,32]{1,0:T(1,128)S(1)}, s32[1,32]{1,0:T(1,128)}, u32[]{:S(2)}) copy-start(s32[1,32]{1,0:T(1,128)} %param.39) | copy-start | bytes 388
  107.9 45.0 %collective-permute-start.37 = (bf16[128,768]{1,0:T(8,128)(2,1)}, bf16[128,768]{1,0:T(8,128)(2,1)}, u32[]{:S(2)}, u32[]{:S(2)}) collective-permute-start(bf16[128,768]{1,0:T(8,128)(2,1)} %get-tuple-element.93), channel_id=1, source_target_pairs={{0,4},{1,5},{2,6},{3,7},{4,0},{5,1},{6,2},{7,3},{8,12},{9,13},{10,... | collective-permute-start | bytes 589832 | tf_op jit(solution)/shard_map/ppermute | solution.py:68
  148.7 8.0 %copy-start.1 = (bf16[128,768]{1,0:T(8,128)(2,1)}, bf16[128,768]{1,0:T(8,128)(2,1)S(1)}, u32[]{:S(2)}) copy-start(bf16[128,768]{1,0:T(8,128)(2,1)S(1)} %collective-permute-done.32.refs_3_.refs_6_) | copy-start | bytes 589828
  148.7 6.3 %collective-permute-start.36 = (bf16[128,768]{1,0:T(8,128)(2,1)}, bf16[128,768]{1,0:T(8,128)(2,1)}, u32[]{:S(2)}, u32[]{:S(2)}) collective-permute-start(bf16[128,768]{1,0:T(8,128)(2,1)} %get-tuple-element.94), channel_id=1, source_target_pairs={{0,2},{1,3},{2,4},{3,5},{4,6},{5,7},{6,0},{7,1},{8,10},{9,11},{10,... | collective-permute-start | bytes 589832 | tf_op jit(solution)/shard_map/ppermute | solution.py:68
  148.8 8.0 %copy-start.2 = (bf16[128,768]{1,0:T(8,128)(2,1)}, bf16[128,768]{1,0:T(8,128)(2,1)S(1)}, u32[]{:S(2)}) copy-start(bf16[128,768]{1,0:T(8,128)(2,1)S(1)} %collective-permute-done.31.refs_2_.refs_5_) | copy-start | bytes 589828
  148.8 8.0 %collective-permute-start.35 = (bf16[128,768]{1,0:T(8,128)(2,1)S(1)}, bf16[128,768]{1,0:T(8,128)(2,1)}, u32[]{:S(2)}, u32[]{:S(2)}) collective-permute-start(bf16[128,768]{1,0:T(8,128)(2,1)S(1)} %get-tuple-element.95), channel_id=1, source_target_pairs={{0,6},{1,7},{2,0},{3,1},{4,2},{5,3},{6,4},{7,5},{8,14},{9,15},{10,... | collective-permute-start | bytes 589832 | tf_op jit(solution)/shard_map/ppermute | solution.py:68
  152.3 8.5 %collective-permute-start.34 = (bf16[128,768]{1,0:T(8,128)(2,1)}, bf16[128,768]{1,0:T(8,128)(2,1)}, u32[]{:S(2)}, u32[]{:S(2)}) collective-permute-start(bf16[128,768]{1,0:T(8,128)(2,1)} %get-tuple-element.96), channel_id=1, source_target_pairs={{0,4},{1,5},{2,6},{3,7},{4,0},{5,1},{6,2},{7,3},{8,12},{9,13},{10,... | collective-permute-start | bytes 589832 | tf_op jit(solution)/shard_map/ppermute | solution.py:68
  152.3 13.1 %collective-permute-start.33 = (bf16[128,768]{1,0:T(8,128)(2,1)}, bf16[128,768]{1,0:T(8,128)(2,1)}, u32[]{:S(2)}, u32[]{:S(2)}) collective-permute-start(bf16[128,768]{1,0:T(8,128)(2,1)} %get-tuple-element.97), channel_id=1, source_target_pairs={{0,2},{1,3},{2,4},{3,5},{4,6},{5,7},{6,0},{7,1},{8,10},{9,11},{10,... | collective-permute-start | bytes 589832 | tf_op jit(solution)/shard_map/ppermute | solution.py:68
  152.9 16.4 %collective-permute-start.41 = (bf16[128,768]{1,0:T(8,128)(2,1)}, bf16[128,768]{1,0:T(8,128)(2,1)}, u32[]{:S(2)}, u32[]{:S(2)}) collective-permute-start(bf16[128,768]{1,0:T(8,128)(2,1)} %get-tuple-element.89), channel_id=1, source_target_pairs={{0,6},{1,7},{2,0},{3,1},{4,2},{5,3},{6,4},{7,5},{8,14},{9,15},{10,... | collective-permute-start | bytes 589832 | tf_op jit(solution)/shard_map/ppermute | solution.py:68
  155.0 14.9 %collective-permute-start.40 = (bf16[128,768]{1,0:T(8,128)(2,1)}, bf16[128,768]{1,0:T(8,128)(2,1)}, u32[]{:S(2)}, u32[]{:S(2)}) collective-permute-start(bf16[128,768]{1,0:T(8,128)(2,1)} %get-tuple-element.90), channel_id=1, source_target_pairs={{0,4},{1,5},{2,6},{3,7},{4,0},{5,1},{6,2},{7,3},{8,12},{9,13},{10,... | collective-permute-start | bytes 589832 | tf_op jit(solution)/shard_map/ppermute | solution.py:68
  156.7 16.6 %collective-permute-start.39 = (bf16[128,768]{1,0:T(8,128)(2,1)}, bf16[128,768]{1,0:T(8,128)(2,1)}, u32[]{:S(2)}, u32[]{:S(2)}) collective-permute-start(bf16[128,768]{1,0:T(8,128)(2,1)} %get-tuple-element.91), channel_id=1, source_target_pairs={{0,2},{1,3},{2,4},{3,5},{4,6},{5,7},{6,0},{7,1},{8,10},{9,11},{10,... | collective-permute-start | bytes 589832 | tf_op jit(solution)/shard_map/ppermute | solution.py:68
  160.8 16.4 %collective-permute-start.42 = (bf16[4,128,256]{2,1,0:T(8,128)(2,1)}, bf16[4,128,256]{2,1,0:T(8,128)(2,1)S(1)}, u32[]{:S(2)}, u32[]{:S(2)}) collective-permute-start(bf16[4,128,256]{2,1,0:T(8,128)(2,1)} %collect.4), channel_id=1, source_target_pairs={{0,1},{1,0},{2,3},{3,2},{4,5},{5,4},{6,7},{7,6},{8,9},{9,8},{10,11... | collective-permute-start | bytes 786440 | tf_op jit(solution)/shard_map/ppermute | solution.py:267
  165.4 11.8 %collective-permute-start.44 = (bf16[4,128,256]{2,1,0:T(8,128)(2,1)}, bf16[4,128,256]{2,1,0:T(8,128)(2,1)}, u32[]{:S(2)}, u32[]{:S(2)}) collective-permute-start(bf16[4,128,256]{2,1,0:T(8,128)(2,1)} %collect.6), channel_id=1, source_target_pairs={{0,1},{1,0},{2,3},{3,2},{4,5},{5,4},{6,7},{7,6},{8,9},{9,8},{10,11... | collective-permute-start | bytes 786440 | tf_op jit(solution)/shard_map/ppermute | solution.py:267
  169.3 7.9 %collective-permute-start.43 = (bf16[4,128,256]{2,1,0:T(8,128)(2,1)}, bf16[4,128,256]{2,1,0:T(8,128)(2,1)}, u32[]{:S(2)}, u32[]{:S(2)}) collective-permute-start(bf16[4,128,256]{2,1,0:T(8,128)(2,1)} %collect.5), channel_id=1, source_target_pairs={{0,1},{1,0},{2,3},{3,2},{4,5},{5,4},{6,7},{7,6},{8,9},{9,8},{10,11... | collective-permute-start | bytes 786440 | tf_op jit(solution)/shard_map/ppermute | solution.py:267
  174.9 10.1 %collective-permute-start.45 = (bf16[4,128,256]{2,1,0:T(8,128)(2,1)}, bf16[4,128,256]{2,1,0:T(8,128)(2,1)}, u32[]{:S(2)}, u32[]{:S(2)}) collective-permute-start(bf16[4,128,256]{2,1,0:T(8,128)(2,1)} %collect.7), channel_id=1, source_target_pairs={{0,1},{1,0},{2,3},{3,2},{4,5},{5,4},{6,7},{7,6},{8,9},{9,8},{10,11... | collective-permute-start | bytes 786440 | tf_op jit(solution)/shard_map/ppermute | solution.py:267
  177.1 7.9 %copy-start.6 = (bf16[4,128,256]{2,1,0:T(8,128)(2,1)}, bf16[4,128,256]{2,1,0:T(8,128)(2,1)S(1)}, u32[]{:S(2)}) copy-start(bf16[4,128,256]{2,1,0:T(8,128)(2,1)S(1)} %collective-permute-done.42.refs_16_) | copy-start | bytes 786436
  217.2 18.5 %collective-permute-start.46 = (bf16[512,512]{1,0:T(8,128)(2,1)}, bf16[512,512]{1,0:T(8,128)(2,1)S(1)}, u32[]{:S(2)}, u32[]{:S(2)}) collective-permute-start(bf16[512,512]{1,0:T(8,128)(2,1)} %get-tuple-element.86), channel_id=1, source_target_pairs={{0,2},{1,3},{2,4},{3,5},{4,6},{5,7},{6,0},{7,1},{8,10},{9,11},{10,... | collective-permute-start | bytes 1572872 | tf_op jit(solution)/shard_map/ppermute | solution.py:68
  217.2 38.5 %collective-permute-start.47 = (bf16[512,512]{1,0:T(8,128)(2,1)}, bf16[512,512]{1,0:T(8,128)(2,1)S(1)}, u32[]{:S(2)}, u32[]{:S(2)}) collective-permute-start(bf16[512,512]{1,0:T(8,128)(2,1)} %get-tuple-element.87), channel_id=1, source_target_pairs={{0,4},{1,5},{2,6},{3,7},{4,0},{5,1},{6,2},{7,3},{8,12},{9,13},{10,... | collective-permute-start | bytes 1572872 | tf_op jit(solution)/shard_map/ppermute | solution.py:68
  233.7 22.0 %collective-permute-start.48 = (bf16[512,512]{1,0:T(8,128)(2,1)}, bf16[512,512]{1,0:T(8,128)(2,1)S(1)}, u32[]{:S(2)}, u32[]{:S(2)}) collective-permute-start(bf16[512,512]{1,0:T(8,128)(2,1)} %get-tuple-element.88), channel_id=1, source_target_pairs={{0,6},{1,7},{2,0},{3,1},{4,2},{5,3},{6,4},{7,5},{8,14},{9,15},{10,... | collective-permute-start | bytes 1572872 | tf_op jit(solution)/shard_map/ppermute | solution.py:68
  235.7 20.0 %copy-start.3 = (bf16[512,512]{1,0:T(8,128)(2,1)}, bf16[512,512]{1,0:T(8,128)(2,1)S(1)}, u32[]{:S(2)}) copy-start(bf16[512,512]{1,0:T(8,128)(2,1)S(1)} %collective-permute-done.46.refs_1_) | copy-start | bytes 1572868
  (2 other events, 1.8 us)
Sparse Core Ops, SparseCore 0:
  39.8 124.8 all-gather.1

commit v3 on v2

--- a/solution.py
+++ b/solution.py
@@ -18,6 +18,9 @@
 CHAINS = 1
 NB = 32
 NEG = -1e30
+COLS_A = 1536
+WIDE = 512
+XC = [list(range(8)), list(range(8, 16))]
 
 
 def prep_kernel(z_ref, marks_ref, q_ref, qs_ref, k_ref, ks_ref, *out_refs):
@@ -195,53 +198,102 @@
 
 
 def project_kernel(where_ref, *refs):
-    parts, w_ref, out_ref, rows = refs[:4], refs[4], refs[5], refs[6]
-
-    @pl.when(pl.program_id(0) == 0)
+    parts, pieces, b_ref, out_ref = refs[:4], refs[4:9], refs[9], refs[10]
+    rows, rows_b = refs[11:]
+    y, core = where_ref[2], where_ref[3]
+    step = pl.program_id(0)
+
+    @pl.when(step == 0)
     def _():
         for k, part in enumerate(parts):
             group = (where_ref[0] + GROUPS - k) % GROUPS
             rows[:, pl.ds(pl.multiple_of(group * GQ, GQ), GQ)] = part[...]
-
-    out_ref[...] = jnp.dot(rows[...], w_ref[...], preferred_element_type=jnp.float32).astype(
-        out_ref.dtype
-    )
-
-
-def project(where, parts, weight):
-    depth, cols = weight.shape
+        for n in range(16):
+            head = n % 2 * 8 + n // 2
+            rows_b[:, n * HEAD_DIM : (n + 1) * HEAD_DIM] = rows[
+                :, head * HEAD_DIM : (head + 1) * HEAD_DIM
+            ]
+
+    @pl.when(step < COLS_A // WIDE)
+    def _():
+        far = (1 - y) * 1024
+        firsts = (
+            y * 1024,
+            far + core * 512,
+            far + core * 512 + 256,
+            far + (1 - core) * 512,
+            far + (1 - core) * 512 + 256,
+        )
+        total = None
+        for first, piece in zip(firsts, pieces):
+            depth = piece.shape[0]
+            mine = rows[:, pl.ds(pl.multiple_of(first, 256), depth)]
+            product = jnp.dot(mine, piece[...], preferred_element_type=jnp.float32)
+            total = product if total is None else total + product
+        out_ref[...] = total.astype(out_ref.dtype)
+
+    @pl.when(step >= COLS_A // WIDE)
+    def _():
+        out_ref[...] = jnp.dot(
+            rows_b[...], b_ref[...], preferred_element_type=jnp.float32
+        ).astype(out_ref.dtype)
+
+
+def project(where, parts, pieces, b):
+    depth = b.shape[0]
     count = parts[0].shape[0]
-    wide = 512
+    steps_a = COLS_A // WIDE
     part = pl.BlockSpec((count, GQ), lambda i, w: (0, 0))
+    a_specs = [
+        pl.BlockSpec((piece.shape[0], WIDE), lambda i, w: (0, jnp.minimum(i, steps_a - 1)))
+        for piece in pieces
+    ]
+    b_spec = pl.BlockSpec((depth, WIDE), lambda i, w: (0, jnp.maximum(i - steps_a, 0)))
+    cols = COLS_A + b.shape[1]
     return pl.pallas_call(
         project_kernel,
-        out_shape=jax.ShapeDtypeStruct((count, cols), weight.dtype),
+        out_shape=jax.ShapeDtypeStruct((count, cols), b.dtype),
         grid_spec=pltpu.PrefetchScalarGridSpec(
             num_scalar_prefetch=1,
-            grid=(cols // wide,),
-            in_specs=[part] * 4 + [pl.BlockSpec((depth, wide), lambda i, w: (0, i))],
-            out_specs=pl.BlockSpec((count, wide), lambda i, w: (0, i)),
-            scratch_shapes=[pltpu.VMEM((count, depth), weight.dtype)],
+            grid=(cols // WIDE,),
+            in_specs=[part] * 4 + a_specs + [b_spec],
+            out_specs=pl.BlockSpec((count, WIDE), lambda i, w: (0, i)),
+            scratch_shapes=[pltpu.VMEM((count, depth), b.dtype)] * 2,
         ),
         name="project",
-    )(where, *parts, weight)
-
-
-def tie_kernel(w_ref, token_ref, out_ref):
-    out_ref[...] = w_ref[...]
-
-
-def tie(weight, token):
-    rows, cols = weight.shape
-    spec = pl.BlockSpec((rows, cols // 2), lambda i: (0, i))
+    )(where, *parts, *pieces, b)
+
+
+def tie_kernel(where_ref, own_ref, far_ref, token_ref, out_ref):
+    rows = own_ref.shape[0]
+    y = where_ref[2]
+    out_ref[pl.ds(pl.multiple_of(y * rows, rows), rows), :] = own_ref[...]
+    out_ref[pl.ds(pl.multiple_of((1 - y) * rows, rows), rows), :] = far_ref[...]
+
+
+def tie(where, own, far, token):
+    rows, cols = own.shape
+    half = pl.BlockSpec((rows, cols // 2), lambda i, w: (0, i))
     return pl.pallas_call(
         tie_kernel,
-        grid=(2,),
-        out_shape=jax.ShapeDtypeStruct(weight.shape, weight.dtype),
-        in_specs=[spec, pl.BlockSpec(memory_space=pl.ANY)],
-        out_specs=spec,
+        out_shape=jax.ShapeDtypeStruct((2 * rows, cols), own.dtype),
+        grid_spec=pltpu.PrefetchScalarGridSpec(
+            num_scalar_prefetch=1,
+            grid=(2,),
+            in_specs=[half, half, pl.BlockSpec(memory_space=pl.ANY)],
+            out_specs=pl.BlockSpec((2 * rows, cols // 2), lambda i, w: (0, i)),
+        ),
         name="tie",
-    )(weight, token)
+    )(where, own, far, token)
+
+
+def y_shift(x, k):
+    moves = []
+    for dp in range(16):
+        for seq in range(8):
+            y = (seq % 2 * 2 + dp // 8 + k) % 4
+            moves.append((dp * 8 + seq, (y % 2 * 8 + dp % 8) * 8 + seq // 2 * 2 + y // 2))
+    return lax.ppermute(x, ("dp", "seq"), moves)
 
 
 def body(queries, keys_values, doc_blocks, route_plan, out_weight):
@@ -250,7 +302,13 @@
     q, kv = queries[0], keys_values[0]
     qs = lax.ppermute(q, "dp", flip(1))
     kvs = lax.ppermute(kv, "dp", flip(1))
-    where = jnp.stack([z, h]).astype(jnp.int32)
+    dp = lax.axis_index("dp")
+    core = dp & 1
+    where = jnp.stack([z, h, dp >> 3, core]).astype(jnp.int32)
+    own_a = lax.all_gather(
+        out_weight[:, :COLS_A], "dp", axis=0, axis_index_groups=XC, tiled=True
+    )
+    far = lax.ppermute(out_weight[:, COLS_A:], "dp", flip(8))
     docs = doc_blocks[0]
     starts = jnp.sum((docs[None, :] < docs[:, None]).astype(jnp.int32), axis=1)[None]
     blocks = list(prep(where, route_plan, q, qs, kv, kvs))
@@ -265,11 +323,18 @@
         pieces += came
         mine = collect(block, came)
         other.append(lax.ppermute(mine, "seq", [(s, s ^ 1) for s in range(8)]))
-    weight = lax.all_gather(tie(out_weight, blocks[2]), "dp", axis=0, tiled=True)
+    both = tie(where, out_weight[:, COLS_A:], far, blocks[3])
+    weight_b = lax.all_gather(both, "dp", axis=0, axis_index_groups=XC, tiled=True)
+    weight_a = [own_a]
+    for n, shift in enumerate((-1, 1)):
+        rows = lax.dynamic_slice_in_dim(own_a, core * 512 + n * 256, 256, 0)
+        weight_a.append(y_shift(rows, shift))
+    for n in range(2):
+        weight_a.append(lax.ppermute(weight_a[1 + n], "dp", flip(1)))
 
     outs = attend(where, starts, blocks, pieces, other)
     parts = [outs[0]] + [z_shift(outs[k], k) for k in range(1, 4)]
-    return project(where, parts, weight)[None]
+    return project(where, parts, weight_a, weight_b)[None]
 
 
 def solution(mesh):

time: 280 us -> 295 us (1.054)
  waiting for transfers between devices: 99.9 us -> 140 us
  starting transfers between devices: 94 us -> 59.2 us
  local copies, waits for them, and re-layouts: 6.94 us -> 14 us
    ppermute x4, waiting for transfers between devices: 65 us -> 109 us  [moves(): yield (lambda x, code=code: lax.ppermute(x, 'dp', flip(code << 1)))]
    ppermute x15, starting transfers between devices: 75 us -> 32.2 us  [z_shift(): lax.ppermute(x, 'seq', [(s, (s // 2 + k) % 4 * 2 + s % 2) for s in range(...]
    ppermute x0 -> x5, starting transfers between devices: none -> 14.5 us  [the longest x2 11.7 us: body(): weight_a.append(lax.ppermute(weight_a[1 + n], 'dp', flip(1)))]
    ppermute x4, waiting for transfers between devices: 7.92 us -> 0.01 us  [body(): other.append(lax.ppermute(mine, 'seq', [(s, s ^ 1) for s in range(8)]))]
    ppermute x15, waiting for transfers between devices: 24.1 us -> 31.4 us  [z_shift(): lax.ppermute(x, 'seq', [(s, (s // 2 + k) % 4 * 2 + s % 2) for s in range(...]
    slice x0 -> x2, local copies, waits for them, and re-layouts: none -> 3.74 us  [the longest x1 1.98 us: body(): both = tie(where, out_weight[:, COLS_A:], far, blocks[3])]
    ppermute x4, starting transfers between devices: 8.63 us -> 5.08 us  [moves(): yield (lambda x, code=code: lax.ppermute(x, 'dp', flip(code << 1)))]
    ppermute x4, starting transfers between devices: 9 us -> 5.83 us  [body(): other.append(lax.ppermute(mine, 'seq', [(s, s ^ 1) for s in range(8)]))]
  transfers between devices with their start and end apart: 26 -> 32, of which waited for: 9 -> 11; matrix products, arithmetic and copies ran while one was open for 2% -> 4% of each run, Pallas kernels for 14% -> 16%
where the time goes in v3:
time: 295 us; the launch traced here: 294 us
  waiting for transfers between devices  140 us (47%)
  Pallas kernels  62.9 us (21%)
  starting transfers between devices  59.2 us (20%)
  between operations  16.1 us (5%)
  local copies, waits for them, and re-layouts  14 us (5%)
    ppermute x4, waiting for transfers between devices, moves(): yield (lambda x, code=code: lax.ppermute(x, 'dp', flip(code << 1)))  109 us
    ppermute x15, starting transfers between devices, z_shift(): lax.ppermute(x, 'seq', [(s, (s // 2 + k) % 4 * 2 + s % 2) for s in range(...  32.2 us
    pallas_call x1, Pallas kernels, attend(): pl.pallas_call(attend_kernel, grid=(1,), out_shape=[jax.ShapeDtypeStruct(...  32.1 us
    ppermute x15, waiting for transfers between devices, z_shift(): lax.ppermute(x, 'seq', [(s, (s // 2 + k) % 4 * 2 + s % 2) for s in range(...  31.4 us
    pallas_call x1, Pallas kernels, project(): pl.pallas_call(project_kernel, out_shape=jax.ShapeDtypeStruct((count, col...  17.1 us
    ppermute x2, starting transfers between devices, body(): weight_a.append(lax.ppermute(weight_a[1 + n], 'dp', flip(1)))  11.7 us
    pallas_call x4, Pallas kernels, collect(): pl.pallas_call(collect_kernel, grid=(1,), out_shape=jax.ShapeDtypeStruct(...  6.58 us
  transfers between devices with their start and end apart: 32, of which 11 were waited for; matrix products, arithmetic and copies ran while one was open for 4% of the time, Pallas kernels for 16%

profile of v3, /device:TPU:1, one launch (start us, length us, event | category | flops | bytes accessed | tf_op | source)
XLA Modules:
  0.0 294.4 jit_solution(14747513062770104087)
XLA Ops:
  6.5 1.8 slice.71
  9.9 2.0 slice.72.own_ref
  17.0 4.3 %prep.1 = (bf16[4,128,768]{2,1,0:T(8,128)(2,1)S(1)}, bf16[4,128,768]{2,1,0:T(8,128)(2,1)S(1)}, bf16[4,128,768]{2,1,0:T(8,128)(2,1)S(1)}, bf16[4,128,768]{2,1,0:T(8,128)(2,1)S(1)}) custom-call(s32[4]{0:T(128)} %pad_add_fusion.z_ref.where_ref, s32[1,4]{1,0:T(1,128)} %marks_ref.1, bf16[512,2048]{1,0:T(8,128)(2,1)} %bitcast.38, ...), custom_call_target="tpu_custom_call" | custom-call | tf_op jit(solution)/shard_map/prep/pallas_call | solution.py:47
  21.3 32.9 %conditional.7 = (bf16[4,128,768]{2,1,0:T(8,128)(2,1)S(1)}) conditional(s32[]{:T(128)} %bitcast.11, bf16[4,128,768]{2,1,0:T(8,128)(2,1)S(1)} %get-tuple-element.84, bf16[4,128,768]{2,1,0:T(8,128)(2,1)S(1)} %get-tuple-element.84, bf16[4,128,768]{2,1,0:T(8,128)(2,1)S(1)} %get-tuple-element.84, ...), branch_computations={%region_25.0_spmd, %region_26.0_spmd, %region_27.0_spmd, %region_2... | conditional | bytes 4718640 | solution.py:318
  21.4 2.5 collective-permute-start.23
  23.9 30.2 %collective-permute-done.23 = bf16[4,128,768]{2,1,0:T(8,128)(2,1)S(1)} collective-permute-done((bf16[4,128,768]{2,1,0:T(8,128)(2,1)S(1)}, bf16[4,128,768]{2,1,0:T(8,128)(2,1)S(1)}, u32[]{:S(2)}, u32[]{:S(2)}) %collective-permute-start.23) | collective-permute-done | bytes 786464 | tf_op jit(solution)/shard_map/cond/branch_3_fun/ppermute | solution.py:67
  54.2 2.8 tie.1
  59.9 5.0 %collective-permute-start.40 = (bf16[128,768]{1,0:T(8,128)(2,1)}, bf16[128,768]{1,0:T(8,128)(2,1)S(1)}, u32[]{:S(2)}, u32[]{:S(2)}) collective-permute-start(bf16[128,768]{1,0:T(8,128)(2,1)} %get-tuple-element.92), channel_id=1, source_target_pairs={{0,4},{1,5},{2,6},{3,7},{4,0},{5,1},{6,2},{7,3},{8,12},{9,13},{10,... | collective-permute-start | bytes 589832 | tf_op jit(solution)/shard_map/ppermute | solution.py:71
  64.9 2.0 collective-permute-start.41
  66.9 29.9 %conditional.6 = (bf16[4,128,768]{2,1,0:T(8,128)(2,1)S(1)}) conditional(s32[]{:T(128)} %bitcast.10, bf16[4,128,768]{2,1,0:T(8,128)(2,1)S(1)} %get-tuple-element.83, bf16[4,128,768]{2,1,0:T(8,128)(2,1)S(1)} %get-tuple-element.83, bf16[4,128,768]{2,1,0:T(8,128)(2,1)S(1)} %get-tuple-element.83, ...), branch_computations={%region_17.0_spmd, %region_18.0_spmd, %region_19.0_spmd, %region_2... | conditional | bytes 4718640 | solution.py:318
  67.4 29.4 %collective-permute-done.14 = bf16[4,128,768]{2,1,0:T(8,128)(2,1)S(1)} collective-permute-done((bf16[4,128,768]{2,1,0:T(8,128)(2,1)S(1)}, bf16[4,128,768]{2,1,0:T(8,128)(2,1)S(1)}, u32[]{:S(2)}, u32[]{:S(2)}) %collective-permute-start.14) | collective-permute-done | bytes 786464 | tf_op jit(solution)/shard_map/cond/branch_1_fun/ppermute | solution.py:67
  97.7 35.8 %conditional.5 = (bf16[4,128,768]{2,1,0:T(8,128)(2,1)S(1)}) conditional(s32[]{:T(128)} %bitcast.9, bf16[4,128,768]{2,1,0:T(8,128)(2,1)S(1)} %get-tuple-element.82, bf16[4,128,768]{2,1,0:T(8,128)(2,1)S(1)} %get-tuple-element.82, bf16[4,128,768]{2,1,0:T(8,128)(2,1)S(1)} %get-tuple-element.82, ...), branch_computations={%region_9.0_spmd, %region_10.0_spmd, %region_11.0_spmd, %region_12... | conditional | bytes 4718640 | solution.py:318
  98.4 35.1 %collective-permute-done.13 = bf16[4,128,768]{2,1,0:T(8,128)(2,1)S(1)} collective-permute-done((bf16[4,128,768]{2,1,0:T(8,128)(2,1)S(1)}, bf16[4,128,768]{2,1,0:T(8,128)(2,1)S(1)}, u32[]{:S(2)}, u32[]{:S(2)}) %collective-permute-start.13) | collective-permute-done | bytes 786464 | tf_op jit(solution)/shard_map/cond/branch_7_fun/ppermute | solution.py:67
  133.6 15.9 %conditional.4 = (bf16[4,128,768]{2,1,0:T(8,128)(2,1)S(1)}) conditional(s32[]{:T(128)} %bitcast.6, bf16[4,128,768]{2,1,0:T(8,128)(2,1)S(1)} %get-tuple-element.81, bf16[4,128,768]{2,1,0:T(8,128)(2,1)S(1)} %get-tuple-element.81, bf16[4,128,768]{2,1,0:T(8,128)(2,1)S(1)} %get-tuple-element.81, ...), branch_computations={%region_1.0_spmd, %region_2.0_spmd, %region_3.0_spmd, %region_4.0_... | conditional | bytes 4718640 | solution.py:318
  134.9 14.2 %collective-permute-done = bf16[4,128,768]{2,1,0:T(8,128)(2,1)S(1)} collective-permute-done((bf16[4,128,768]{2,1,0:T(8,128)(2,1)S(1)}, bf16[4,128,768]{2,1,0:T(8,128)(2,1)S(1)}, u32[]{:S(2)}, u32[]{:S(2)}) %collective-permute-start) | collective-permute-done | bytes 786464 | tf_op jit(solution)/shard_map/cond/branch_1_fun/ppermute | solution.py:67
  150.4 2.6 constant_dynamic-slice_fusion
  155.3 14.5 %collective-permute-start.38 = (bf16[128,768]{1,0:T(8,128)(2,1)S(1)}, bf16[128,768]{1,0:T(8,128)(2,1)}, u32[]{:S(2)}, u32[]{:S(2)}) collective-permute-start(bf16[128,768]{1,0:T(8,128)(2,1)S(1)} %copy-done.9), channel_id=1, source_target_pairs={{0,6},{1,7},{2,0},{3,1},{4,2},{5,3},{6,4},{7,5},{8,14},{9,15},{10,... | collective-permute-start | bytes 589832 | tf_op jit(solution)/shard_map/ppermute | solution.py:71
  172.4 3.2 %collective-permute-start.35 = (bf16[128,768]{1,0:T(8,128)(2,1)}, bf16[128,768]{1,0:T(8,128)(2,1)}, u32[]{:S(2)}, u32[]{:S(2)}) collective-permute-start(bf16[128,768]{1,0:T(8,128)(2,1)} %get-tuple-element.97), channel_id=1, source_target_pairs={{0,6},{1,7},{2,0},{3,1},{4,2},{5,3},{6,4},{7,5},{8,14},{9,15},{10,... | collective-permute-start | bytes 589832 | tf_op jit(solution)/shard_map/ppermute | solution.py:71
  175.6 2.8 collective-permute-done.33.refs_1_.refs_7_
  178.4 1.6 collect.7
  185.4 1.6 collect.6
  187.1 1.7 collect.5
  188.7 1.7 collective-permute-start.44
  190.4 2.1 collective-permute-done.32.refs_3_.refs_6_
  193.7 1.7 collect.4
  195.4 1.7 collective-permute-start.42
  197.1 11.6 %collective-permute-start.51 = (bf16[256,1536]{1,0:T(8,128)(2,1)}, bf16[256,1536]{1,0:T(8,128)(2,1)}, u32[]{:S(2)}, u32[]{:S(2)}) collective-permute-start(bf16[256,1536]{1,0:T(8,128)(2,1)} %collective-permute-done.49.refs_5_), channel_id=1, source_target_pairs={{0,8},{8,0},{16,24},{24,16},{32,40},{40,32},{48,56},{56,48},{64,72... | collective-permute-start | bytes 2359304 | tf_op jit(solution)/shard_map/ppermute | solution.py:333
  210.2 32.1 %attend.1 = (bf16[512,512]{1,0:T(8,128)(2,1)}, bf16[512,512]{1,0:T(8,128)(2,1)}, bf16[512,512]{1,0:T(8,128)(2,1)}, bf16[512,512]{1,0:T(8,128)(2,1)}) custom-call(s32[4]{0:T(128)} %pad_add_fusion.z_ref.where_ref, s32[1,32]{1,0:T(1,128)} %bitcast.41, bf16[4,128,768]{2,1,0:T(8,128)(2,1)S(1)} %get-tuple-element.107.refs_0_, ...), custom_call_target="tpu_custom_call" | custom-call | tf_op jit(solution)/shard_map/attend/pallas_call | solution.py:165
  242.4 3.4 %collective-permute-start.47 = (bf16[512,512]{1,0:T(8,128)(2,1)}, bf16[512,512]{1,0:T(8,128)(2,1)S(1)}, u32[]{:S(2)}, u32[]{:S(2)}) collective-permute-start(bf16[512,512]{1,0:T(8,128)(2,1)} %get-tuple-element.87), channel_id=1, source_target_pairs={{0,4},{1,5},{2,6},{3,7},{4,0},{5,1},{6,2},{7,3},{8,12},{9,13},{10,... | collective-permute-start | bytes 1572872 | tf_op jit(solution)/shard_map/ppermute | solution.py:71
  245.7 11.7 %collective-permute-done.46.refs_1_ = bf16[512,512]{1,0:T(8,128)(2,1)S(1)} collective-permute-done((bf16[512,512]{1,0:T(8,128)(2,1)}, bf16[512,512]{1,0:T(8,128)(2,1)S(1)}, u32[]{:S(2)}, u32[]{:S(2)}) %collective-permute-start.46) | collective-permute-done | bytes 524320 | tf_op jit(solution)/shard_map/ppermute | solution.py:71
  257.4 12.2 %collective-permute-done.47.refs_2_ = bf16[512,512]{1,0:T(8,128)(2,1)S(1)} collective-permute-done((bf16[512,512]{1,0:T(8,128)(2,1)}, bf16[512,512]{1,0:T(8,128)(2,1)S(1)}, u32[]{:S(2)}, u32[]{:S(2)}) %collective-permute-start.47) | collective-permute-done | bytes 524320 | tf_op jit(solution)/shard_map/ppermute | solution.py:71
  270.5 17.1 %project.1 = bf16[512,4096]{1,0:T(8,128)(2,1)} custom-call(s32[4]{0:T(128)} %pad_add_fusion.z_ref.where_ref, bf16[512,512]{1,0:T(8,128)(2,1)} %get-tuple-element.85.refs_0_, bf16[512,512]{1,0:T(8,128)(2,1)} %copy-done.5, bf16[512,512]{1,0:T(8,128)(2,1)} %copy-done.6, bf16[512,512]{1,0:T(8,128)(2,1)} %copy-done.7, ...), custom_call_target="tpu_custom_call" | custom-call | tf_op jit(solution)/shard_map/project/pallas_call | solution.py:253
  (82 shorter events, 25.6 us)
Async XLA Ops:
  6.5 143.8 %all-gather.3.cloned.1.call-start = ((), (), s32[]{:S(2)}) async-start(), calls=%async_computation | async-start | bytes 3538944 | tf_op jit(solution)/shard_map/all_gather | solution.py:308
  8.3 261.3 %all-gather.5.cloned.1.call-start = ((), (), s32[]{:S(2)}) async-start(), calls=%async_computation.1 | async-start | bytes 11796480 | tf_op jit(solution)/shard_map/all_gather | solution.py:327
  8.4 8.6 %collective-permute-start.28 = (bf16[512,2048]{1,0:T(8,128)(2,1)}, bf16[512,2048]{1,0:T(8,128)(2,1)}, u32[]{:S(2)}, u32[]{:S(2)}) collective-permute-start(bf16[512,2048]{1,0:T(8,128)(2,1)} %bitcast.37), channel_id=1, source_target_pairs={{0,8},{8,0},{16,24},{24,16},{32,40},{40,32},{48,56},{56,48},{64,72... | collective-permute-start | bytes 6291464 | tf_op jit(solution)/shard_map/ppermute | solution.py:303
  9.8 6.2 %collective-permute-start.29 = (bf16[512,1024]{1,0:T(8,128)(2,1)}, bf16[512,1024]{1,0:T(8,128)(2,1)S(1)}, u32[]{:S(2)}, u32[]{:S(2)}) collective-permute-start(bf16[512,1024]{1,0:T(8,128)(2,1)} %bitcast.39), channel_id=1, source_target_pairs={{0,8},{8,0},{16,24},{24,16},{32,40},{40,32},{48,56},{56,48},{64,72... | collective-permute-start | bytes 3145736 | tf_op jit(solution)/shard_map/ppermute | solution.py:304
  11.9 42.3 %collective-permute-start.53 = (bf16[128,2560]{1,0:T(8,128)(2,1)}, bf16[128,2560]{1,0:T(8,128)(2,1)}, u32[]{:S(2)}, u32[]{:S(2)}) collective-permute-start(bf16[128,2560]{1,0:T(8,128)(2,1)} %slice.72.own_ref), channel_id=1, source_target_pairs={{0,64},{8,72},{16,80},{24,88},{32,96},{40,104},{48,112},{56,120},{... | collective-permute-start | bytes 1966088 | tf_op jit(solution)/shard_map/ppermute | solution.py:311
  21.4 32.8 %collective-permute-start.23 = (bf16[4,128,768]{2,1,0:T(8,128)(2,1)S(1)}, bf16[4,128,768]{2,1,0:T(8,128)(2,1)S(1)}, u32[]{:S(2)}, u32[]{:S(2)}) collective-permute-start(bf16[4,128,768]{2,1,0:T(8,128)(2,1)S(1)} %param.27), channel_id=1, source_target_pairs={{0,48},{8,56},{16,32},{24,40},{32,16},{40,24},{48,0},{56,8},{64,11... | collective-permute-start | bytes 2359304 | tf_op jit(solution)/shard_map/cond/branch_3_fun/ppermute | solution.py:67
  59.9 93.1 %collective-permute-start.39 = (bf16[128,768]{1,0:T(8,128)(2,1)}, bf16[128,768]{1,0:T(8,128)(2,1)S(1)}, u32[]{:S(2)}, u32[]{:S(2)}) collective-permute-start(bf16[128,768]{1,0:T(8,128)(2,1)} %get-tuple-element.93), channel_id=1, source_target_pairs={{0,2},{1,3},{2,4},{3,5},{4,6},{5,7},{6,0},{7,1},{8,10},{9,11},{10,... | collective-permute-start | bytes 589832 | tf_op jit(solution)/shard_map/ppermute | solution.py:71
  59.9 93.2 %collective-permute-start.40 = (bf16[128,768]{1,0:T(8,128)(2,1)}, bf16[128,768]{1,0:T(8,128)(2,1)S(1)}, u32[]{:S(2)}, u32[]{:S(2)}) collective-permute-start(bf16[128,768]{1,0:T(8,128)(2,1)} %get-tuple-element.92), channel_id=1, source_target_pairs={{0,4},{1,5},{2,6},{3,7},{4,0},{5,1},{6,2},{7,3},{8,12},{9,13},{10,... | collective-permute-start | bytes 589832 | tf_op jit(solution)/shard_map/ppermute | solution.py:71
  64.9 90.4 %collective-permute-start.41 = (bf16[128,768]{1,0:T(8,128)(2,1)}, bf16[128,768]{1,0:T(8,128)(2,1)}, u32[]{:S(2)}, u32[]{:S(2)}) collective-permute-start(bf16[128,768]{1,0:T(8,128)(2,1)} %get-tuple-element.91), channel_id=1, source_target_pairs={{0,6},{1,7},{2,0},{3,1},{4,2},{5,3},{6,4},{7,5},{8,14},{9,15},{10,... | collective-permute-start | bytes 589832 | tf_op jit(solution)/shard_map/ppermute | solution.py:71
  66.9 29.9 %collective-permute-start.14 = (bf16[4,128,768]{2,1,0:T(8,128)(2,1)S(1)}, bf16[4,128,768]{2,1,0:T(8,128)(2,1)S(1)}, u32[]{:S(2)}, u32[]{:S(2)}) collective-permute-start(bf16[4,128,768]{2,1,0:T(8,128)(2,1)S(1)} %param.17), channel_id=1, source_target_pairs={{0,16},{8,24},{16,0},{24,8},{32,48},{40,56},{48,32},{56,40},{64,80... | collective-permute-start | bytes 2359304 | tf_op jit(solution)/shard_map/cond/branch_1_fun/ppermute | solution.py:67
  97.7 72.1 %collective-permute-start.36 = (bf16[128,768]{1,0:T(8,128)(2,1)}, bf16[128,768]{1,0:T(8,128)(2,1)}, u32[]{:S(2)}, u32[]{:S(2)}) collective-permute-start(bf16[128,768]{1,0:T(8,128)(2,1)} %get-tuple-element.96), channel_id=1, source_target_pairs={{0,2},{1,3},{2,4},{3,5},{4,6},{5,7},{6,0},{7,1},{8,10},{9,11},{10,... | collective-permute-start | bytes 589832 | tf_op jit(solution)/shard_map/ppermute | solution.py:71
  97.7 35.8 %collective-permute-start.13 = (bf16[4,128,768]{2,1,0:T(8,128)(2,1)S(1)}, bf16[4,128,768]{2,1,0:T(8,128)(2,1)S(1)}, u32[]{:S(2)}, u32[]{:S(2)}) collective-permute-start(bf16[4,128,768]{2,1,0:T(8,128)(2,1)S(1)} %param.15), channel_id=1, source_target_pairs={{0,112},{8,120},{16,96},{24,104},{32,80},{40,88},{48,64},{56,72},{... | collective-permute-start | bytes 2359304 | tf_op jit(solution)/shard_map/cond/branch_7_fun/ppermute | solution.py:67
  133.6 15.6 %collective-permute-start = (bf16[4,128,768]{2,1,0:T(8,128)(2,1)S(1)}, bf16[4,128,768]{2,1,0:T(8,128)(2,1)S(1)}, u32[]{:S(2)}, u32[]{:S(2)}) collective-permute-start(bf16[4,128,768]{2,1,0:T(8,128)(2,1)S(1)} %param.1), channel_id=1, source_target_pairs={{0,16},{8,24},{16,0},{24,8},{32,48},{40,56},{48,32},{56,40},{64,80... | collective-permute-start | bytes 2359304 | tf_op jit(solution)/shard_map/cond/branch_1_fun/ppermute | solution.py:67
  149.4 20.4 %collective-permute-start.37 = (bf16[128,768]{1,0:T(8,128)(2,1)}, bf16[128,768]{1,0:T(8,128)(2,1)}, u32[]{:S(2)}, u32[]{:S(2)}) collective-permute-start(bf16[128,768]{1,0:T(8,128)(2,1)} %get-tuple-element.95), channel_id=1, source_target_pairs={{0,4},{1,5},{2,6},{3,7},{4,0},{5,1},{6,2},{7,3},{8,12},{9,13},{10,... | collective-permute-start | bytes 589832 | tf_op jit(solution)/shard_map/ppermute | solution.py:71
  153.0 44.1 %collective-permute-start.49 = (bf16[256,1536]{1,0:T(8,128)(2,1)}, bf16[256,1536]{1,0:T(8,128)(2,1)}, u32[]{:S(2)}, u32[]{:S(2)}) collective-permute-start(bf16[256,1536]{1,0:T(8,128)(2,1)} %get-tuple-element.90), channel_id=1, source_target_pairs={{0,65},{1,64},{2,67},{3,66},{4,69},{5,68},{6,71},{7,70},{8,73},{9,... | collective-permute-start | bytes 2359304 | tf_op jit(solution)/shard_map/ppermute | solution.py:296
  153.1 55.7 %collective-permute-start.50 = (bf16[256,1536]{1,0:T(8,128)(2,1)}, bf16[256,1536]{1,0:T(8,128)(2,1)}, u32[]{:S(2)}, u32[]{:S(2)}) collective-permute-start(bf16[256,1536]{1,0:T(8,128)(2,1)} %get-tuple-element.89), channel_id=1, source_target_pairs={{0,64},{1,65},{2,66},{3,67},{4,68},{5,69},{6,70},{7,71},{8,72},{9,... | collective-permute-start | bytes 2359304 | tf_op jit(solution)/shard_map/ppermute | solution.py:296
  155.3 17.1 %collective-permute-start.38 = (bf16[128,768]{1,0:T(8,128)(2,1)S(1)}, bf16[128,768]{1,0:T(8,128)(2,1)}, u32[]{:S(2)}, u32[]{:S(2)}) collective-permute-start(bf16[128,768]{1,0:T(8,128)(2,1)S(1)} %copy-done.9), channel_id=1, source_target_pairs={{0,6},{1,7},{2,0},{3,1},{4,2},{5,3},{6,4},{7,5},{8,14},{9,15},{10,... | collective-permute-start | bytes 589832 | tf_op jit(solution)/shard_map/ppermute | solution.py:71
  169.8 8.6 %collective-permute-start.33 = (bf16[128,768]{1,0:T(8,128)(2,1)S(1)}, bf16[128,768]{1,0:T(8,128)(2,1)}, u32[]{:S(2)}, u32[]{:S(2)}) collective-permute-start(bf16[128,768]{1,0:T(8,128)(2,1)S(1)} %get-tuple-element.99), channel_id=1, source_target_pairs={{0,2},{1,3},{2,4},{3,5},{4,6},{5,7},{6,0},{7,1},{8,10},{9,11},{10,... | collective-permute-start | bytes 589832 | tf_op jit(solution)/shard_map/ppermute | solution.py:71
  169.8 10.3 %collective-permute-start.34 = (bf16[128,768]{1,0:T(8,128)(2,1)}, bf16[128,768]{1,0:T(8,128)(2,1)}, u32[]{:S(2)}, u32[]{:S(2)}) collective-permute-start(bf16[128,768]{1,0:T(8,128)(2,1)} %get-tuple-element.98), channel_id=1, source_target_pairs={{0,4},{1,5},{2,6},{3,7},{4,0},{5,1},{6,2},{7,3},{8,12},{9,13},{10,... | collective-permute-start | bytes 589832 | tf_op jit(solution)/shard_map/ppermute | solution.py:71
  172.4 9.6 %collective-permute-start.35 = (bf16[128,768]{1,0:T(8,128)(2,1)}, bf16[128,768]{1,0:T(8,128)(2,1)}, u32[]{:S(2)}, u32[]{:S(2)}) collective-permute-start(bf16[128,768]{1,0:T(8,128)(2,1)} %get-tuple-element.97), channel_id=1, source_target_pairs={{0,6},{1,7},{2,0},{3,1},{4,2},{5,3},{6,4},{7,5},{8,14},{9,15},{10,... | collective-permute-start | bytes 589832 | tf_op jit(solution)/shard_map/ppermute | solution.py:71
  178.4 6.0 %collective-permute-start.30 = (bf16[128,768]{1,0:T(8,128)(2,1)}, bf16[128,768]{1,0:T(8,128)(2,1)}, u32[]{:S(2)}, u32[]{:S(2)}) collective-permute-start(bf16[128,768]{1,0:T(8,128)(2,1)} %get-tuple-element.102), channel_id=1, source_target_pairs={{0,2},{1,3},{2,4},{3,5},{4,6},{5,7},{6,0},{7,1},{8,10},{9,11},{10,... | collective-permute-start | bytes 589832 | tf_op jit(solution)/shard_map/ppermute | solution.py:71
  180.0 15.4 %collective-permute-start.45 = (bf16[4,128,256]{2,1,0:T(8,128)(2,1)}, bf16[4,128,256]{2,1,0:T(8,128)(2,1)}, u32[]{:S(2)}, u32[]{:S(2)}) collective-permute-start(bf16[4,128,256]{2,1,0:T(8,128)(2,1)} %collect.7), channel_id=1, source_target_pairs={{0,1},{1,0},{2,3},{3,2},{4,5},{5,4},{6,7},{7,6},{8,9},{9,8},{10,11... | collective-permute-start | bytes 786440 | tf_op jit(solution)/shard_map/ppermute | solution.py:325
  182.0 6.7 %collective-permute-start.31 = (bf16[128,768]{1,0:T(8,128)(2,1)}, bf16[128,768]{1,0:T(8,128)(2,1)S(1)}, u32[]{:S(2)}, u32[]{:S(2)}) collective-permute-start(bf16[128,768]{1,0:T(8,128)(2,1)} %get-tuple-element.101), channel_id=1, source_target_pairs={{0,4},{1,5},{2,6},{3,7},{4,0},{5,1},{6,2},{7,3},{8,12},{9,13},{10,... | collective-permute-start | bytes 589832 | tf_op jit(solution)/shard_map/ppermute | solution.py:71
  184.4 8.0 %collective-permute-start.32 = (bf16[128,768]{1,0:T(8,128)(2,1)}, bf16[128,768]{1,0:T(8,128)(2,1)S(1)}, u32[]{:S(2)}, u32[]{:S(2)}) collective-permute-start(bf16[128,768]{1,0:T(8,128)(2,1)} %get-tuple-element.100), channel_id=1, source_target_pairs={{0,6},{1,7},{2,0},{3,1},{4,2},{5,3},{6,4},{7,5},{8,14},{9,15},{10,... | collective-permute-start | bytes 589832 | tf_op jit(solution)/shard_map/ppermute | solution.py:71
  188.7 20.8 %collective-permute-start.44 = (bf16[4,128,256]{2,1,0:T(8,128)(2,1)}, bf16[4,128,256]{2,1,0:T(8,128)(2,1)}, u32[]{:S(2)}, u32[]{:S(2)}) collective-permute-start(bf16[4,128,256]{2,1,0:T(8,128)(2,1)} %collect.6), channel_id=1, source_target_pairs={{0,1},{1,0},{2,3},{3,2},{4,5},{5,4},{6,7},{7,6},{8,9},{9,8},{10,11... | collective-permute-start | bytes 786440 | tf_op jit(solution)/shard_map/ppermute | solution.py:325
  192.5 17.1 %collective-permute-start.43 = (bf16[4,128,256]{2,1,0:T(8,128)(2,1)}, bf16[4,128,256]{2,1,0:T(8,128)(2,1)}, u32[]{:S(2)}, u32[]{:S(2)}) collective-permute-start(bf16[4,128,256]{2,1,0:T(8,128)(2,1)} %collect.5), channel_id=1, source_target_pairs={{0,1},{1,0},{2,3},{3,2},{4,5},{5,4},{6,7},{7,6},{8,9},{9,8},{10,11... | collective-permute-start | bytes 786440 | tf_op jit(solution)/shard_map/ppermute | solution.py:325
  195.4 14.1 %collective-permute-start.42 = (bf16[4,128,256]{2,1,0:T(8,128)(2,1)}, bf16[4,128,256]{2,1,0:T(8,128)(2,1)S(1)}, u32[]{:S(2)}, u32[]{:S(2)}) collective-permute-start(bf16[4,128,256]{2,1,0:T(8,128)(2,1)} %collect.4), channel_id=1, source_target_pairs={{0,1},{1,0},{2,3},{3,2},{4,5},{5,4},{6,7},{7,6},{8,9},{9,8},{10,11... | collective-permute-start | bytes 786440 | tf_op jit(solution)/shard_map/ppermute | solution.py:325
  197.1 72.5 %collective-permute-start.51 = (bf16[256,1536]{1,0:T(8,128)(2,1)}, bf16[256,1536]{1,0:T(8,128)(2,1)}, u32[]{:S(2)}, u32[]{:S(2)}) collective-permute-start(bf16[256,1536]{1,0:T(8,128)(2,1)} %collective-permute-done.49.refs_5_), channel_id=1, source_target_pairs={{0,8},{8,0},{16,24},{24,16},{32,40},{40,32},{48,56},{56,48},{64,72... | collective-permute-start | bytes 2359304 | tf_op jit(solution)/shard_map/ppermute | solution.py:333
  208.7 60.9 %collective-permute-start.52 = (bf16[256,1536]{1,0:T(8,128)(2,1)}, bf16[256,1536]{1,0:T(8,128)(2,1)}, u32[]{:S(2)}, u32[]{:S(2)}) collective-permute-start(bf16[256,1536]{1,0:T(8,128)(2,1)} %collective-permute-done.50.refs_6_), channel_id=1, source_target_pairs={{0,8},{8,0},{16,24},{24,16},{32,40},{40,32},{48,56},{56,48},{64,72... | collective-permute-start | bytes 2359304 | tf_op jit(solution)/shard_map/ppermute | solution.py:333
  242.4 15.0 %collective-permute-start.46 = (bf16[512,512]{1,0:T(8,128)(2,1)}, bf16[512,512]{1,0:T(8,128)(2,1)S(1)}, u32[]{:S(2)}, u32[]{:S(2)}) collective-permute-start(bf16[512,512]{1,0:T(8,128)(2,1)} %get-tuple-element.86), channel_id=1, source_target_pairs={{0,2},{1,3},{2,4},{3,5},{4,6},{5,7},{6,0},{7,1},{8,10},{9,11},{10,... | collective-permute-start | bytes 1572872 | tf_op jit(solution)/shard_map/ppermute | solution.py:71
  242.4 27.2 %collective-permute-start.47 = (bf16[512,512]{1,0:T(8,128)(2,1)}, bf16[512,512]{1,0:T(8,128)(2,1)S(1)}, u32[]{:S(2)}, u32[]{:S(2)}) collective-permute-start(bf16[512,512]{1,0:T(8,128)(2,1)} %get-tuple-element.87), channel_id=1, source_target_pairs={{0,4},{1,5},{2,6},{3,7},{4,0},{5,1},{6,2},{7,3},{8,12},{9,13},{10,... | collective-permute-start | bytes 1572872 | tf_op jit(solution)/shard_map/ppermute | solution.py:71
  245.7 23.8 %collective-permute-start.48 = (bf16[512,512]{1,0:T(8,128)(2,1)}, bf16[512,512]{1,0:T(8,128)(2,1)S(1)}, u32[]{:S(2)}, u32[]{:S(2)}) collective-permute-start(bf16[512,512]{1,0:T(8,128)(2,1)} %get-tuple-element.88), channel_id=1, source_target_pairs={{0,6},{1,7},{2,0},{3,1},{4,2},{5,3},{6,4},{7,5},{8,14},{9,15},{10,... | collective-permute-start | bytes 1572872 | tf_op jit(solution)/shard_map/ppermute | solution.py:71
  (11 other events, 108.0 us)
Sparse Core Ops, SparseCore 0:
  9.0 43.9 all-gather.2
  57.2 78.5 all-gather.4

commit v4 on v2

--- a/solution.py
+++ b/solution.py
@@ -18,6 +18,7 @@
 CHAINS = 1
 NB = 32
 NEG = -1e30
+XC = [list(range(8)), list(range(8, 16))]
 
 
 def prep_kernel(z_ref, marks_ref, q_ref, qs_ref, k_ref, ks_ref, *out_refs):
@@ -201,7 +202,11 @@
     def _():
         for k, part in enumerate(parts):
             group = (where_ref[0] + GROUPS - k) % GROUPS
-            rows[:, pl.ds(pl.multiple_of(group * GQ, GQ), GQ)] = part[...]
+            for g in range(GROUPS):
+                head = group * GROUPS + g
+                place = head % 8 * 2 + head // 8
+                cols = pl.ds(pl.multiple_of(place * HEAD_DIM, HEAD_DIM), HEAD_DIM)
+                rows[:, cols] = part[:, g * HEAD_DIM : (g + 1) * HEAD_DIM]
 
     out_ref[...] = jnp.dot(rows[...], w_ref[...], preferred_element_type=jnp.float32).astype(
         out_ref.dtype
@@ -227,21 +232,43 @@
     )(where, *parts, weight)
 
 
-def tie_kernel(w_ref, token_ref, out_ref):
-    out_ref[...] = w_ref[...]
-
-
-def tie(weight, token):
-    rows, cols = weight.shape
-    spec = pl.BlockSpec((rows, cols // 2), lambda i: (0, i))
+def tie_kernel(where_ref, own_ref, lo_ref, hi_ref, token_ref, out_ref):
+    rows = own_ref.shape[0]
+    y = where_ref[2]
+    far = pl.multiple_of((1 - y) * rows, rows)
+    out_ref[pl.ds(pl.multiple_of(y * rows, rows), rows), :] = own_ref[...]
+    out_ref[pl.ds(far, rows // 2), :] = lo_ref[...]
+    out_ref[pl.ds(pl.multiple_of(far + rows // 2, rows // 2), rows // 2), :] = hi_ref[...]
+
+
+def tie(where, own, lo, hi, token):
+    rows, cols = own.shape
+    half = pl.BlockSpec((rows // 2, cols // 4), lambda i, w: (0, i))
     return pl.pallas_call(
         tie_kernel,
-        grid=(2,),
-        out_shape=jax.ShapeDtypeStruct(weight.shape, weight.dtype),
-        in_specs=[spec, pl.BlockSpec(memory_space=pl.ANY)],
-        out_specs=spec,
+        out_shape=jax.ShapeDtypeStruct((2 * rows, cols), own.dtype),
+        grid_spec=pltpu.PrefetchScalarGridSpec(
+            num_scalar_prefetch=1,
+            grid=(4,),
+            in_specs=[
+                pl.BlockSpec((rows, cols // 4), lambda i, w: (0, i)),
+                half,
+                half,
+                pl.BlockSpec(memory_space=pl.ANY),
+            ],
+            out_specs=pl.BlockSpec((2 * rows, cols // 4), lambda i, w: (0, i)),
+        ),
         name="tie",
-    )(weight, token)
+    )(where, own, lo, hi, token)
+
+
+def y_shift(x, k):
+    moves = []
+    for dp in range(16):
+        for seq in range(8):
+            y = (seq % 2 * 2 + dp // 8 + k) % 4
+            moves.append((dp * 8 + seq, (y % 2 * 8 + dp % 8) * 8 + seq // 2 * 2 + y // 2))
+    return lax.ppermute(x, ("dp", "seq"), moves)
 
 
 def body(queries, keys_values, doc_blocks, route_plan, out_weight):
@@ -250,7 +277,11 @@
     q, kv = queries[0], keys_values[0]
     qs = lax.ppermute(q, "dp", flip(1))
     kvs = lax.ppermute(kv, "dp", flip(1))
-    where = jnp.stack([z, h]).astype(jnp.int32)
+    where = jnp.stack([z, h, lax.axis_index("dp") >> 3]).astype(jnp.int32)
+    far = []
+    for n, shift in enumerate((1, -1)):
+        rows = out_weight[n * 64 : (n + 1) * 64]
+        far.append(y_shift(rows, shift))
     docs = doc_blocks[0]
     starts = jnp.sum((docs[None, :] < docs[:, None]).astype(jnp.int32), axis=1)[None]
     blocks = list(prep(where, route_plan, q, qs, kv, kvs))
@@ -265,7 +296,8 @@
         pieces += came
         mine = collect(block, came)
         other.append(lax.ppermute(mine, "seq", [(s, s ^ 1) for s in range(8)]))
-    weight = lax.all_gather(tie(out_weight, blocks[2]), "dp", axis=0, tiled=True)
+    both = tie(where, out_weight, *far, blocks[3])
+    weight = lax.all_gather(both, "dp", axis=0, axis_index_groups=XC, tiled=True)
 
     outs = attend(where, starts, blocks, pieces, other)
     parts = [outs[0]] + [z_shift(outs[k], k) for k in range(1, 4)]

time: 280 us -> 268 us (0.957)
  the two profiles are of different devices: /device:TPU:1 before, /device:TPU:2 now
where the time goes in v4:
time: 268 us
  waiting for transfers between devices  137 us (51%)
  Pallas kernels  62.1 us (23%)
  starting transfers between devices  42.2 us (16%)
  between operations  16.1 us (6%)
  local copies, waits for them, and re-layouts  8.27 us (3%)
    ppermute x4, waiting for transfers between devices, moves(): yield (lambda x, code=code: lax.ppermute(x, 'dp', flip(code << 1)))  108 us
    pallas_call x1, Pallas kernels, attend(): pl.pallas_call(attend_kernel, grid=(1,), out_shape=[jax.ShapeDtypeStruct(...  30.5 us
    ppermute x15, waiting for transfers between devices, z_shift(): lax.ppermute(x, 'seq', [(s, (s // 2 + k) % 4 * 2 + s % 2) for s in range(...  21.4 us
    ppermute x15, starting transfers between devices, z_shift(): lax.ppermute(x, 'seq', [(s, (s // 2 + k) % 4 * 2 + s % 2) for s in range(...  20.2 us
    pallas_call x1, Pallas kernels, project(): pl.pallas_call(project_kernel, out_shape=jax.ShapeDtypeStruct((count, col...  16.3 us
    ppermute x4, starting transfers between devices, body(): other.append(lax.ppermute(mine, 'seq', [(s, s ^ 1) for s in range(8)]))  10.8 us
    ppermute x4, waiting for transfers between devices, body(): other.append(lax.ppermute(mine, 'seq', [(s, s ^ 1) for s in range(8)]))  8.24 us
    ppermute x4, starting transfers between devices, moves(): yield (lambda x, code=code: lax.ppermute(x, 'dp', flip(code << 1)))  7.72 us
  transfers between devices with their start and end apart: 28, of which 11 were waited for; matrix products, arithmetic and copies ran while one was open for 3% of the time, Pallas kernels for 15%

profile of v4, /device:TPU:2, one launch (start us, length us, event | category | flops | bytes accessed | tf_op | source)
XLA Modules:
  0.0 267.6 jit_solution(5839879339176008478)
XLA Ops:
  7.1 2.3 fusion
  9.3 3.0 %collective-permute-start.50 = (bf16[64,4096]{1,0:T(8,128)(2,1)}, bf16[64,4096]{1,0:T(8,128)(2,1)}, u32[]{:S(2)}, u32[]{:S(2)}) collective-permute-start(bf16[64,4096]{1,0:T(8,128)(2,1)} %get-tuple-element.89), channel_id=1, source_target_pairs={{0,65},{1,64},{2,67},{3,66},{4,69},{5,68},{6,71},{7,70},{8,73},{9,... | collective-permute-start | bytes 1572872 | tf_op jit(solution)/shard_map/ppermute | solution.py:271
  15.4 4.3 %prep.1 = (bf16[4,128,768]{2,1,0:T(8,128)(2,1)S(1)}, bf16[4,128,768]{2,1,0:T(8,128)(2,1)S(1)}, bf16[4,128,768]{2,1,0:T(8,128)(2,1)S(1)}, bf16[4,128,768]{2,1,0:T(8,128)(2,1)S(1)}) custom-call(s32[3]{0:T(128)} %pad_add_fusion.z_ref.where_ref, s32[1,4]{1,0:T(1,128)} %marks_ref.1, bf16[512,2048]{1,0:T(8,128)(2,1)} %bitcast.37, ...), custom_call_target="tpu_custom_call" | custom-call | tf_op jit(solution)/shard_map/prep/pallas_call | solution.py:45
  19.7 19.3 %conditional.7 = (bf16[4,128,768]{2,1,0:T(8,128)(2,1)S(1)}) conditional(s32[]{:T(128)} %bitcast.10, bf16[4,128,768]{2,1,0:T(8,128)(2,1)S(1)} %get-tuple-element.84, bf16[4,128,768]{2,1,0:T(8,128)(2,1)S(1)} %get-tuple-element.84, bf16[4,128,768]{2,1,0:T(8,128)(2,1)S(1)} %get-tuple-element.84, ...), branch_computations={%region_25.0_spmd, %region_26.0_spmd, %region_27.0_spmd, %region_2... | conditional | bytes 4718640 | solution.py:291
  21.3 17.7 %collective-permute-done.23 = bf16[4,128,768]{2,1,0:T(8,128)(2,1)S(1)} collective-permute-done((bf16[4,128,768]{2,1,0:T(8,128)(2,1)S(1)}, bf16[4,128,768]{2,1,0:T(8,128)(2,1)S(1)}, u32[]{:S(2)}, u32[]{:S(2)}) %collective-permute-start.23) | collective-permute-done | bytes 786464 | tf_op jit(solution)/shard_map/cond/branch_3_fun/ppermute | solution.py:65
  39.1 4.4 %tie.1 = bf16[256,4096]{1,0:T(8,128)(2,1)} custom-call(s32[3]{0:T(128)} %pad_add_fusion.z_ref.where_ref, bf16[128,4096]{1,0:T(8,128)(2,1)} %own_ref.1, bf16[64,4096]{1,0:T(8,128)(2,1)} %collective-permute-done.49.lo_ref, bf16[64,4096]{1,0:T(8,128)(2,1)} %collective-permute-done.50.hi_ref, bf16[4,128,768]{2,1,0:T(8,128)(2,1)S(1)} %get-tuple-element.110.refs_0_.refs_3_.token_ref), custom_call_target="tpu_custom_call" | custom-call | tf_op jit(solution)/shard_map/tie/pallas_call | solution.py:247
  45.4 23.9 %conditional.4 = (bf16[4,128,768]{2,1,0:T(8,128)(2,1)S(1)}) conditional(s32[]{:T(128)} %bitcast.5, bf16[4,128,768]{2,1,0:T(8,128)(2,1)S(1)} %get-tuple-element.81, bf16[4,128,768]{2,1,0:T(8,128)(2,1)S(1)} %get-tuple-element.81, bf16[4,128,768]{2,1,0:T(8,128)(2,1)S(1)} %get-tuple-element.81, ...), branch_computations={%region_1.0_spmd, %region_2.0_spmd, %region_3.0_spmd, %region_4.0_... | conditional | bytes 4718640 | solution.py:291
  45.4 1.8 collective-permute-start
  47.2 22.0 %collective-permute-done = bf16[4,128,768]{2,1,0:T(8,128)(2,1)S(1)} collective-permute-done((bf16[4,128,768]{2,1,0:T(8,128)(2,1)S(1)}, bf16[4,128,768]{2,1,0:T(8,128)(2,1)S(1)}, u32[]{:S(2)}, u32[]{:S(2)}) %collective-permute-start) | collective-permute-done | bytes 786464 | tf_op jit(solution)/shard_map/cond/branch_1_fun/ppermute | solution.py:65
  73.7 2.0 collective-permute-start.41
  75.7 37.1 %conditional.5 = (bf16[4,128,768]{2,1,0:T(8,128)(2,1)S(1)}) conditional(s32[]{:T(128)} %bitcast.8, bf16[4,128,768]{2,1,0:T(8,128)(2,1)S(1)} %get-tuple-element.82, bf16[4,128,768]{2,1,0:T(8,128)(2,1)S(1)} %get-tuple-element.82, bf16[4,128,768]{2,1,0:T(8,128)(2,1)S(1)} %get-tuple-element.82, ...), branch_computations={%region_9.0_spmd, %region_10.0_spmd, %region_11.0_spmd, %region_12... | conditional | bytes 4718640 | solution.py:291
  75.7 2.5 collective-permute-start.13
  78.2 34.6 %collective-permute-done.13 = bf16[4,128,768]{2,1,0:T(8,128)(2,1)S(1)} collective-permute-done((bf16[4,128,768]{2,1,0:T(8,128)(2,1)S(1)}, bf16[4,128,768]{2,1,0:T(8,128)(2,1)S(1)}, u32[]{:S(2)}, u32[]{:S(2)}) %collective-permute-start.13) | collective-permute-done | bytes 786464 | tf_op jit(solution)/shard_map/cond/branch_7_fun/ppermute | solution.py:65
  112.8 35.5 %conditional.6 = (bf16[4,128,768]{2,1,0:T(8,128)(2,1)S(1)}) conditional(s32[]{:T(128)} %bitcast.9, bf16[4,128,768]{2,1,0:T(8,128)(2,1)S(1)} %get-tuple-element.83, bf16[4,128,768]{2,1,0:T(8,128)(2,1)S(1)} %get-tuple-element.83, bf16[4,128,768]{2,1,0:T(8,128)(2,1)S(1)} %get-tuple-element.83, ...), branch_computations={%region_17.0_spmd, %region_18.0_spmd, %region_19.0_spmd, %region_2... | conditional | bytes 4718640 | solution.py:291
  112.9 1.9 collective-permute-start.14
  114.7 33.4 %collective-permute-done.14 = bf16[4,128,768]{2,1,0:T(8,128)(2,1)S(1)} collective-permute-done((bf16[4,128,768]{2,1,0:T(8,128)(2,1)S(1)}, bf16[4,128,768]{2,1,0:T(8,128)(2,1)S(1)}, u32[]{:S(2)}, u32[]{:S(2)}) %collective-permute-start.14) | collective-permute-done | bytes 786464 | tf_op jit(solution)/shard_map/cond/branch_1_fun/ppermute | solution.py:65
  148.3 2.6 collective-permute-start.40
  152.1 2.8 %collective-permute-start.35 = (bf16[128,768]{1,0:T(8,128)(2,1)S(1)}, bf16[128,768]{1,0:T(8,128)(2,1)}, u32[]{:S(2)}, u32[]{:S(2)}) collective-permute-start(bf16[128,768]{1,0:T(8,128)(2,1)S(1)} %get-tuple-element.97), channel_id=1, source_target_pairs={{0,6},{1,7},{2,0},{3,1},{4,2},{5,3},{6,4},{7,5},{8,14},{9,15},{10,... | collective-permute-start | bytes 589832 | tf_op jit(solution)/shard_map/ppermute | solution.py:69
  157.7 2.4 collective-permute-start.38
  160.1 2.9 %collective-permute-done.39.refs_1_.refs_13_ = bf16[128,768]{1,0:T(8,128)(2,1)} collective-permute-done((bf16[128,768]{1,0:T(8,128)(2,1)}, bf16[128,768]{1,0:T(8,128)(2,1)}, u32[]{:S(2)}, u32[]{:S(2)}) %collective-permute-start.39) | collective-permute-done | bytes 196640 | tf_op jit(solution)/shard_map/ppermute | solution.py:69
  163.0 1.8 collective-permute-start.37
  166.4 1.6 collect.7
  168.1 7.2 %collective-permute-start.42 = (bf16[4,128,256]{2,1,0:T(8,128)(2,1)}, bf16[4,128,256]{2,1,0:T(8,128)(2,1)S(1)}, u32[]{:S(2)}, u32[]{:S(2)}) collective-permute-start(bf16[4,128,256]{2,1,0:T(8,128)(2,1)} %collect.4), channel_id=1, source_target_pairs={{0,1},{1,0},{2,3},{3,2},{4,5},{5,4},{6,7},{7,6},{8,9},{9,8},{10,11... | collective-permute-start | bytes 786440 | tf_op jit(solution)/shard_map/ppermute | solution.py:298
  177.0 3.4 %collective-permute-start.43 = (bf16[4,128,256]{2,1,0:T(8,128)(2,1)}, bf16[4,128,256]{2,1,0:T(8,128)(2,1)}, u32[]{:S(2)}, u32[]{:S(2)}) collective-permute-start(bf16[4,128,256]{2,1,0:T(8,128)(2,1)} %collect.5), channel_id=1, source_target_pairs={{0,1},{1,0},{2,3},{3,2},{4,5},{5,4},{6,7},{7,6},{8,9},{9,8},{10,11... | collective-permute-start | bytes 786440 | tf_op jit(solution)/shard_map/ppermute | solution.py:298
  180.4 1.6 collect.6
  182.9 2.6 collective-permute-done.45.refs_19_
  185.5 2.8 %collective-permute-done.43.refs_17_ = bf16[4,128,256]{2,1,0:T(8,128)(2,1)} collective-permute-done((bf16[4,128,256]{2,1,0:T(8,128)(2,1)}, bf16[4,128,256]{2,1,0:T(8,128)(2,1)}, u32[]{:S(2)}, u32[]{:S(2)}) %collective-permute-start.43) | collective-permute-done | bytes 262176 | tf_op jit(solution)/shard_map/ppermute | solution.py:298
  188.3 2.8 %collective-permute-done.44.refs_18_ = bf16[4,128,256]{2,1,0:T(8,128)(2,1)} collective-permute-done((bf16[4,128,256]{2,1,0:T(8,128)(2,1)}, bf16[4,128,256]{2,1,0:T(8,128)(2,1)}, u32[]{:S(2)}, u32[]{:S(2)}) %collective-permute-start.44) | collective-permute-done | bytes 262176 | tf_op jit(solution)/shard_map/ppermute | solution.py:298
  191.2 30.5 %attend.1 = (bf16[512,512]{1,0:T(8,128)(2,1)}, bf16[512,512]{1,0:T(8,128)(2,1)}, bf16[512,512]{1,0:T(8,128)(2,1)}, bf16[512,512]{1,0:T(8,128)(2,1)}) custom-call(s32[3]{0:T(128)} %pad_add_fusion.z_ref.where_ref, s32[1,32]{1,0:T(1,128)} %bitcast.40, bf16[4,128,768]{2,1,0:T(8,128)(2,1)S(1)} %get-tuple-element.107.refs_0_, ...), custom_call_target="tpu_custom_call" | custom-call | tf_op jit(solution)/shard_map/attend/pallas_call | solution.py:163
  222.8 2.4 collective-permute-start.47
  226.3 16.8 %collective-permute-done.46.refs_1_ = bf16[512,512]{1,0:T(8,128)(2,1)S(1)} collective-permute-done((bf16[512,512]{1,0:T(8,128)(2,1)}, bf16[512,512]{1,0:T(8,128)(2,1)S(1)}, u32[]{:S(2)}, u32[]{:S(2)}) %collective-permute-start.46) | collective-permute-done | bytes 524320 | tf_op jit(solution)/shard_map/ppermute | solution.py:69
  244.5 16.3 %project.1 = bf16[512,4096]{1,0:T(8,128)(2,1)} custom-call(s32[3]{0:T(128)} %pad_add_fusion.z_ref.where_ref, bf16[512,512]{1,0:T(8,128)(2,1)} %get-tuple-element.85.refs_0_, bf16[512,512]{1,0:T(8,128)(2,1)} %copy-done.3, bf16[512,512]{1,0:T(8,128)(2,1)} %copy-done.4, bf16[512,512]{1,0:T(8,128)(2,1)} %copy-done.5, ...), custom_call_target="tpu_custom_call" | custom-call | tf_op jit(solution)/shard_map/project/pallas_call | solution.py:221
  (67 shorter events, 20.8 us)
Async XLA Ops:
  6.5 237.2 %all-gather.2.cloned.1.call-start = ((), (), s32[]{:S(2)}) async-start(), calls=%async_computation | async-start | bytes 18874368 | tf_op jit(solution)/shard_map/all_gather | solution.py:300
  6.5 8.8 %collective-permute-start.28 = (bf16[512,2048]{1,0:T(8,128)(2,1)}, bf16[512,2048]{1,0:T(8,128)(2,1)}, u32[]{:S(2)}, u32[]{:S(2)}) collective-permute-start(bf16[512,2048]{1,0:T(8,128)(2,1)} %bitcast.36), channel_id=1, source_target_pairs={{0,8},{8,0},{16,24},{24,16},{32,40},{40,32},{48,56},{56,48},{64,72... | collective-permute-start | bytes 6291464 | tf_op jit(solution)/shard_map/ppermute | solution.py:278
  6.5 7.8 %collective-permute-start.29 = (bf16[512,1024]{1,0:T(8,128)(2,1)}, bf16[512,1024]{1,0:T(8,128)(2,1)S(1)}, u32[]{:S(2)}, u32[]{:S(2)}) collective-permute-start(bf16[512,1024]{1,0:T(8,128)(2,1)} %bitcast.38), channel_id=1, source_target_pairs={{0,8},{8,0},{16,24},{24,16},{32,40},{40,32},{48,56},{56,48},{64,72... | collective-permute-start | bytes 3145736 | tf_op jit(solution)/shard_map/ppermute | solution.py:279
  9.3 29.7 %collective-permute-start.50 = (bf16[64,4096]{1,0:T(8,128)(2,1)}, bf16[64,4096]{1,0:T(8,128)(2,1)}, u32[]{:S(2)}, u32[]{:S(2)}) collective-permute-start(bf16[64,4096]{1,0:T(8,128)(2,1)} %get-tuple-element.89), channel_id=1, source_target_pairs={{0,65},{1,64},{2,67},{3,66},{4,69},{5,68},{6,71},{7,70},{8,73},{9,... | collective-permute-start | bytes 1572872 | tf_op jit(solution)/shard_map/ppermute | solution.py:271
  12.3 26.7 %collective-permute-start.49 = (bf16[64,4096]{1,0:T(8,128)(2,1)}, bf16[64,4096]{1,0:T(8,128)(2,1)}, u32[]{:S(2)}, u32[]{:S(2)}) collective-permute-start(bf16[64,4096]{1,0:T(8,128)(2,1)} %get-tuple-element.90), channel_id=1, source_target_pairs={{0,64},{1,65},{2,66},{3,67},{4,68},{5,69},{6,70},{7,71},{8,72},{9,... | collective-permute-start | bytes 1572872 | tf_op jit(solution)/shard_map/ppermute | solution.py:271
  19.7 19.2 %collective-permute-start.23 = (bf16[4,128,768]{2,1,0:T(8,128)(2,1)S(1)}, bf16[4,128,768]{2,1,0:T(8,128)(2,1)S(1)}, u32[]{:S(2)}, u32[]{:S(2)}) collective-permute-start(bf16[4,128,768]{2,1,0:T(8,128)(2,1)S(1)} %param.27), channel_id=1, source_target_pairs={{0,48},{8,56},{16,32},{24,40},{32,16},{40,24},{48,0},{56,8},{64,11... | collective-permute-start | bytes 2359304 | tf_op jit(solution)/shard_map/cond/branch_3_fun/ppermute | solution.py:65
  45.4 23.8 %collective-permute-start = (bf16[4,128,768]{2,1,0:T(8,128)(2,1)S(1)}, bf16[4,128,768]{2,1,0:T(8,128)(2,1)S(1)}, u32[]{:S(2)}, u32[]{:S(2)}) collective-permute-start(bf16[4,128,768]{2,1,0:T(8,128)(2,1)S(1)} %param.1), channel_id=1, source_target_pairs={{0,16},{8,24},{16,0},{24,8},{32,48},{40,56},{48,32},{56,40},{64,80... | collective-permute-start | bytes 2359304 | tf_op jit(solution)/shard_map/cond/branch_1_fun/ppermute | solution.py:65
  70.2 81.6 %collective-permute-start.32 = (bf16[128,768]{1,0:T(8,128)(2,1)}, bf16[128,768]{1,0:T(8,128)(2,1)S(1)}, u32[]{:S(2)}, u32[]{:S(2)}) collective-permute-start(bf16[128,768]{1,0:T(8,128)(2,1)} %get-tuple-element.100), channel_id=1, source_target_pairs={{0,6},{1,7},{2,0},{3,1},{4,2},{5,3},{6,4},{7,5},{8,14},{9,15},{10,... | collective-permute-start | bytes 589832 | tf_op jit(solution)/shard_map/ppermute | solution.py:69
  70.2 81.9 %collective-permute-start.31 = (bf16[128,768]{1,0:T(8,128)(2,1)}, bf16[128,768]{1,0:T(8,128)(2,1)S(1)}, u32[]{:S(2)}, u32[]{:S(2)}) collective-permute-start(bf16[128,768]{1,0:T(8,128)(2,1)} %get-tuple-element.101), channel_id=1, source_target_pairs={{0,4},{1,5},{2,6},{3,7},{4,0},{5,1},{6,2},{7,3},{8,12},{9,13},{10,... | collective-permute-start | bytes 589832 | tf_op jit(solution)/shard_map/ppermute | solution.py:69
  71.5 84.4 %collective-permute-start.30 = (bf16[128,768]{1,0:T(8,128)(2,1)}, bf16[128,768]{1,0:T(8,128)(2,1)}, u32[]{:S(2)}, u32[]{:S(2)}) collective-permute-start(bf16[128,768]{1,0:T(8,128)(2,1)} %get-tuple-element.102), channel_id=1, source_target_pairs={{0,2},{1,3},{2,4},{3,5},{4,6},{5,7},{6,0},{7,1},{8,10},{9,11},{10,... | collective-permute-start | bytes 589832 | tf_op jit(solution)/shard_map/ppermute | solution.py:69
  73.7 82.1 %collective-permute-start.41 = (bf16[128,768]{1,0:T(8,128)(2,1)}, bf16[128,768]{1,0:T(8,128)(2,1)}, u32[]{:S(2)}, u32[]{:S(2)}) collective-permute-start(bf16[128,768]{1,0:T(8,128)(2,1)} %get-tuple-element.91), channel_id=1, source_target_pairs={{0,6},{1,7},{2,0},{3,1},{4,2},{5,3},{6,4},{7,5},{8,14},{9,15},{10,... | collective-permute-start | bytes 589832 | tf_op jit(solution)/shard_map/ppermute | solution.py:69
  75.7 37.1 %collective-permute-start.13 = (bf16[4,128,768]{2,1,0:T(8,128)(2,1)S(1)}, bf16[4,128,768]{2,1,0:T(8,128)(2,1)S(1)}, u32[]{:S(2)}, u32[]{:S(2)}) collective-permute-start(bf16[4,128,768]{2,1,0:T(8,128)(2,1)S(1)} %param.15), channel_id=1, source_target_pairs={{0,112},{8,120},{16,96},{24,104},{32,80},{40,88},{48,64},{56,72},{... | collective-permute-start | bytes 2359304 | tf_op jit(solution)/shard_map/cond/branch_7_fun/ppermute | solution.py:65
  112.9 35.2 %collective-permute-start.14 = (bf16[4,128,768]{2,1,0:T(8,128)(2,1)S(1)}, bf16[4,128,768]{2,1,0:T(8,128)(2,1)S(1)}, u32[]{:S(2)}, u32[]{:S(2)}) collective-permute-start(bf16[4,128,768]{2,1,0:T(8,128)(2,1)S(1)} %param.17), channel_id=1, source_target_pairs={{0,16},{8,24},{16,0},{24,8},{32,48},{40,56},{48,32},{56,40},{64,80... | collective-permute-start | bytes 2359304 | tf_op jit(solution)/shard_map/cond/branch_1_fun/ppermute | solution.py:65
  148.3 9.4 %collective-permute-start.40 = (bf16[128,768]{1,0:T(8,128)(2,1)}, bf16[128,768]{1,0:T(8,128)(2,1)}, u32[]{:S(2)}, u32[]{:S(2)}) collective-permute-start(bf16[128,768]{1,0:T(8,128)(2,1)} %get-tuple-element.92), channel_id=1, source_target_pairs={{0,4},{1,5},{2,6},{3,7},{4,0},{5,1},{6,2},{7,3},{8,12},{9,13},{10,... | collective-permute-start | bytes 589832 | tf_op jit(solution)/shard_map/ppermute | solution.py:69
  151.7 13.0 %copy-start.1 = (bf16[128,768]{1,0:T(8,128)(2,1)}, bf16[128,768]{1,0:T(8,128)(2,1)S(1)}, u32[]{:S(2)}) copy-start(bf16[128,768]{1,0:T(8,128)(2,1)S(1)} %collective-permute-done.32.refs_3_.refs_6_) | copy-start | bytes 589828
  151.7 11.3 %collective-permute-start.39 = (bf16[128,768]{1,0:T(8,128)(2,1)}, bf16[128,768]{1,0:T(8,128)(2,1)}, u32[]{:S(2)}, u32[]{:S(2)}) collective-permute-start(bf16[128,768]{1,0:T(8,128)(2,1)} %get-tuple-element.93), channel_id=1, source_target_pairs={{0,2},{1,3},{2,4},{3,5},{4,6},{5,7},{6,0},{7,1},{8,10},{9,11},{10,... | collective-permute-start | bytes 589832 | tf_op jit(solution)/shard_map/ppermute | solution.py:69
  152.1 12.7 %copy-start.2 = (bf16[128,768]{1,0:T(8,128)(2,1)}, bf16[128,768]{1,0:T(8,128)(2,1)S(1)}, u32[]{:S(2)}) copy-start(bf16[128,768]{1,0:T(8,128)(2,1)S(1)} %collective-permute-done.31.refs_2_.refs_5_) | copy-start | bytes 589828
  152.1 12.6 %collective-permute-start.35 = (bf16[128,768]{1,0:T(8,128)(2,1)S(1)}, bf16[128,768]{1,0:T(8,128)(2,1)}, u32[]{:S(2)}, u32[]{:S(2)}) collective-permute-start(bf16[128,768]{1,0:T(8,128)(2,1)S(1)} %get-tuple-element.97), channel_id=1, source_target_pairs={{0,6},{1,7},{2,0},{3,1},{4,2},{5,3},{6,4},{7,5},{8,14},{9,15},{10,... | collective-permute-start | bytes 589832 | tf_op jit(solution)/shard_map/ppermute | solution.py:69
  155.8 12.2 %collective-permute-start.34 = (bf16[128,768]{1,0:T(8,128)(2,1)}, bf16[128,768]{1,0:T(8,128)(2,1)}, u32[]{:S(2)}, u32[]{:S(2)}) collective-permute-start(bf16[128,768]{1,0:T(8,128)(2,1)} %get-tuple-element.98), channel_id=1, source_target_pairs={{0,4},{1,5},{2,6},{3,7},{4,0},{5,1},{6,2},{7,3},{8,12},{9,13},{10,... | collective-permute-start | bytes 589832 | tf_op jit(solution)/shard_map/ppermute | solution.py:69
  155.8 19.4 %collective-permute-start.33 = (bf16[128,768]{1,0:T(8,128)(2,1)}, bf16[128,768]{1,0:T(8,128)(2,1)}, u32[]{:S(2)}, u32[]{:S(2)}) collective-permute-start(bf16[128,768]{1,0:T(8,128)(2,1)} %get-tuple-element.99), channel_id=1, source_target_pairs={{0,2},{1,3},{2,4},{3,5},{4,6},{5,7},{6,0},{7,1},{8,10},{9,11},{10,... | collective-permute-start | bytes 589832 | tf_op jit(solution)/shard_map/ppermute | solution.py:69
  157.7 19.2 %collective-permute-start.38 = (bf16[128,768]{1,0:T(8,128)(2,1)}, bf16[128,768]{1,0:T(8,128)(2,1)}, u32[]{:S(2)}, u32[]{:S(2)}) collective-permute-start(bf16[128,768]{1,0:T(8,128)(2,1)} %get-tuple-element.94), channel_id=1, source_target_pairs={{0,6},{1,7},{2,0},{3,1},{4,2},{5,3},{6,4},{7,5},{8,14},{9,15},{10,... | collective-permute-start | bytes 589832 | tf_op jit(solution)/shard_map/ppermute | solution.py:69
  163.0 17.4 %collective-permute-start.37 = (bf16[128,768]{1,0:T(8,128)(2,1)}, bf16[128,768]{1,0:T(8,128)(2,1)}, u32[]{:S(2)}, u32[]{:S(2)}) collective-permute-start(bf16[128,768]{1,0:T(8,128)(2,1)} %get-tuple-element.95), channel_id=1, source_target_pairs={{0,4},{1,5},{2,6},{3,7},{4,0},{5,1},{6,2},{7,3},{8,12},{9,13},{10,... | collective-permute-start | bytes 589832 | tf_op jit(solution)/shard_map/ppermute | solution.py:69
  164.8 15.6 %collective-permute-start.36 = (bf16[128,768]{1,0:T(8,128)(2,1)}, bf16[128,768]{1,0:T(8,128)(2,1)}, u32[]{:S(2)}, u32[]{:S(2)}) collective-permute-start(bf16[128,768]{1,0:T(8,128)(2,1)} %get-tuple-element.96), channel_id=1, source_target_pairs={{0,2},{1,3},{2,4},{3,5},{4,6},{5,7},{6,0},{7,1},{8,10},{9,11},{10,... | collective-permute-start | bytes 589832 | tf_op jit(solution)/shard_map/ppermute | solution.py:69
  166.4 15.7 %copy-start.8 = (s32[1,32]{1,0:T(1,128)S(1)}, s32[1,32]{1,0:T(1,128)}, u32[]{:S(2)}) copy-start(s32[1,32]{1,0:T(1,128)} %param.39) | copy-start | bytes 388
  168.1 14.8 %collective-permute-start.42 = (bf16[4,128,256]{2,1,0:T(8,128)(2,1)}, bf16[4,128,256]{2,1,0:T(8,128)(2,1)S(1)}, u32[]{:S(2)}, u32[]{:S(2)}) collective-permute-start(bf16[4,128,256]{2,1,0:T(8,128)(2,1)} %collect.4), channel_id=1, source_target_pairs={{0,1},{1,0},{2,3},{3,2},{4,5},{5,4},{6,7},{7,6},{8,9},{9,8},{10,11... | collective-permute-start | bytes 786440 | tf_op jit(solution)/shard_map/ppermute | solution.py:298
  175.3 10.3 %collective-permute-start.45 = (bf16[4,128,256]{2,1,0:T(8,128)(2,1)}, bf16[4,128,256]{2,1,0:T(8,128)(2,1)}, u32[]{:S(2)}, u32[]{:S(2)}) collective-permute-start(bf16[4,128,256]{2,1,0:T(8,128)(2,1)} %collect.7), channel_id=1, source_target_pairs={{0,1},{1,0},{2,3},{3,2},{4,5},{5,4},{6,7},{7,6},{8,9},{9,8},{10,11... | collective-permute-start | bytes 786440 | tf_op jit(solution)/shard_map/ppermute | solution.py:298
  177.0 11.4 %collective-permute-start.43 = (bf16[4,128,256]{2,1,0:T(8,128)(2,1)}, bf16[4,128,256]{2,1,0:T(8,128)(2,1)}, u32[]{:S(2)}, u32[]{:S(2)}) collective-permute-start(bf16[4,128,256]{2,1,0:T(8,128)(2,1)} %collect.5), channel_id=1, source_target_pairs={{0,1},{1,0},{2,3},{3,2},{4,5},{5,4},{6,7},{7,6},{8,9},{9,8},{10,11... | collective-permute-start | bytes 786440 | tf_op jit(solution)/shard_map/ppermute | solution.py:298
  182.0 9.1 %collective-permute-start.44 = (bf16[4,128,256]{2,1,0:T(8,128)(2,1)}, bf16[4,128,256]{2,1,0:T(8,128)(2,1)}, u32[]{:S(2)}, u32[]{:S(2)}) collective-permute-start(bf16[4,128,256]{2,1,0:T(8,128)(2,1)} %collect.6), channel_id=1, source_target_pairs={{0,1},{1,0},{2,3},{3,2},{4,5},{5,4},{6,7},{7,6},{8,9},{9,8},{10,11... | collective-permute-start | bytes 786440 | tf_op jit(solution)/shard_map/ppermute | solution.py:298
  182.9 8.2 %copy-start.6 = (bf16[4,128,256]{2,1,0:T(8,128)(2,1)}, bf16[4,128,256]{2,1,0:T(8,128)(2,1)S(1)}, u32[]{:S(2)}) copy-start(bf16[4,128,256]{2,1,0:T(8,128)(2,1)S(1)} %collective-permute-done.42.refs_16_) | copy-start | bytes 786436
  221.7 21.4 %collective-permute-start.46 = (bf16[512,512]{1,0:T(8,128)(2,1)}, bf16[512,512]{1,0:T(8,128)(2,1)S(1)}, u32[]{:S(2)}, u32[]{:S(2)}) collective-permute-start(bf16[512,512]{1,0:T(8,128)(2,1)} %get-tuple-element.86), channel_id=1, source_target_pairs={{0,2},{1,3},{2,4},{3,5},{4,6},{5,7},{6,0},{7,1},{8,10},{9,11},{10,... | collective-permute-start | bytes 1572872 | tf_op jit(solution)/shard_map/ppermute | solution.py:69
  222.8 20.3 %collective-permute-start.47 = (bf16[512,512]{1,0:T(8,128)(2,1)}, bf16[512,512]{1,0:T(8,128)(2,1)S(1)}, u32[]{:S(2)}, u32[]{:S(2)}) collective-permute-start(bf16[512,512]{1,0:T(8,128)(2,1)} %get-tuple-element.87), channel_id=1, source_target_pairs={{0,4},{1,5},{2,6},{3,7},{4,0},{5,1},{6,2},{7,3},{8,12},{9,13},{10,... | collective-permute-start | bytes 1572872 | tf_op jit(solution)/shard_map/ppermute | solution.py:69
  225.2 18.6 %collective-permute-start.48 = (bf16[512,512]{1,0:T(8,128)(2,1)}, bf16[512,512]{1,0:T(8,128)(2,1)S(1)}, u32[]{:S(2)}, u32[]{:S(2)}) collective-permute-start(bf16[512,512]{1,0:T(8,128)(2,1)} %get-tuple-element.88), channel_id=1, source_target_pairs={{0,6},{1,7},{2,0},{3,1},{4,2},{5,3},{6,4},{7,5},{8,14},{9,15},{10,... | collective-permute-start | bytes 1572872 | tf_op jit(solution)/shard_map/ppermute | solution.py:69
  (5 other events, 9.4 us)
Sparse Core Ops, SparseCore 0:
  43.7 106.2 all-gather.1

commit v5 on v3

--- a/solution.py
+++ b/solution.py
@@ -18,7 +18,7 @@
 CHAINS = 1
 NB = 32
 NEG = -1e30
-COLS_A = 1536
+COLS_A = 2048
 WIDE = 512
 XC = [list(range(8)), list(range(8, 16))]
 
@@ -264,27 +264,42 @@
     )(where, *parts, *pieces, b)
 
 
-def tie_kernel(where_ref, own_ref, far_ref, token_ref, out_ref):
-    rows = own_ref.shape[0]
+def tie_kernel(where_ref, a_ref, b_ref, lo_ref, hi_ref, token_ref, one_ref, both_ref):
+    rows = b_ref.shape[0]
     y = where_ref[2]
-    out_ref[pl.ds(pl.multiple_of(y * rows, rows), rows), :] = own_ref[...]
-    out_ref[pl.ds(pl.multiple_of((1 - y) * rows, rows), rows), :] = far_ref[...]
-
-
-def tie(where, own, far, token):
+    far = pl.multiple_of((1 - y) * rows, rows)
+    one_ref[...] = a_ref[...]
+    both_ref[pl.ds(pl.multiple_of(y * rows, rows), rows), :] = b_ref[...]
+    both_ref[pl.ds(far, rows // 2), :] = lo_ref[...]
+    both_ref[pl.ds(pl.multiple_of(far + rows // 2, rows // 2), rows // 2), :] = hi_ref[...]
+
+
+def tie(where, own, lo, hi, token):
     rows, cols = own.shape
-    half = pl.BlockSpec((rows, cols // 2), lambda i, w: (0, i))
+    half = cols // 2
+    wide = half // 2
+    thin = pl.BlockSpec((rows // 2, wide), lambda i, w: (0, i))
+    one = pl.BlockSpec((rows, wide), lambda i, w: (0, i))
     return pl.pallas_call(
         tie_kernel,
-        out_shape=jax.ShapeDtypeStruct((2 * rows, cols), own.dtype),
+        out_shape=[
+            jax.ShapeDtypeStruct((rows, half), own.dtype),
+            jax.ShapeDtypeStruct((2 * rows, half), own.dtype),
+        ],
         grid_spec=pltpu.PrefetchScalarGridSpec(
             num_scalar_prefetch=1,
             grid=(2,),
-            in_specs=[half, half, pl.BlockSpec(memory_space=pl.ANY)],
-            out_specs=pl.BlockSpec((2 * rows, cols // 2), lambda i, w: (0, i)),
+            in_specs=[
+                one,
+                pl.BlockSpec((rows, wide), lambda i, w: (0, i + 2)),
+                thin,
+                thin,
+                pl.BlockSpec(memory_space=pl.ANY),
+            ],
+            out_specs=[one, pl.BlockSpec((2 * rows, wide), lambda i, w: (0, i))],
         ),
         name="tie",
-    )(where, own, far, token)
+    )(where, own, own, lo, hi, token)
 
 
 def y_shift(x, k):
@@ -305,10 +320,10 @@
     dp = lax.axis_index("dp")
     core = dp & 1
     where = jnp.stack([z, h, dp >> 3, core]).astype(jnp.int32)
-    own_a = lax.all_gather(
-        out_weight[:, :COLS_A], "dp", axis=0, axis_index_groups=XC, tiled=True
-    )
-    far = lax.ppermute(out_weight[:, COLS_A:], "dp", flip(8))
+    far = []
+    for n, shift in enumerate((1, -1)):
+        rows = out_weight[n * 64 : (n + 1) * 64, COLS_A:]
+        far.append(y_shift(rows, shift))
     docs = doc_blocks[0]
     starts = jnp.sum((docs[None, :] < docs[:, None]).astype(jnp.int32), axis=1)[None]
     blocks = list(prep(where, route_plan, q, qs, kv, kvs))
@@ -323,7 +338,8 @@
         pieces += came
         mine = collect(block, came)
         other.append(lax.ppermute(mine, "seq", [(s, s ^ 1) for s in range(8)]))
-    both = tie(where, out_weight[:, COLS_A:], far, blocks[3])
+    one, both = tie(where, out_weight, *far, blocks[3])
+    own_a = lax.all_gather(one, "dp", axis=0, axis_index_groups=XC, tiled=True)
     weight_b = lax.all_gather(both, "dp", axis=0, axis_index_groups=XC, tiled=True)
     weight_a = [own_a]
     for n, shift in enumerate((-1, 1)):
@@ -333,7 +349,9 @@
         weight_a.append(lax.ppermute(weight_a[1 + n], "dp", flip(1)))
 
     outs = attend(where, starts, blocks, pieces, other)
-    parts = [outs[0]] + [z_shift(outs[k], k) for k in range(1, 4)]
+    parts = [outs[0]]
+    for k in range(1, 4):
+        parts.append(z_shift(outs[k], k))
     return project(where, parts, weight_a, weight_b)[None]
 
 

time: 295 us -> 305 us (1.034)
  the two profiles are of different devices: /device:TPU:1 before, /device:TPU:20 now
where the time goes in v5:
time: 305 us
  waiting for transfers between devices  148 us (49%)
  starting transfers between devices  63.9 us (21%)
  Pallas kernels  62.9 us (21%)
  between operations  16.1 us (5%)
  local copies, waits for them, and re-layouts  12.3 us (4%)
    ppermute x4, waiting for transfers between devices, moves(): yield (lambda x, code=code: lax.ppermute(x, 'dp', flip(code << 1)))  92.5 us
    ppermute x15, starting transfers between devices, z_shift(): lax.ppermute(x, 'seq', [(s, (s // 2 + k) % 4 * 2 + s % 2) for s in range(...  41.9 us
    pallas_call x1, Pallas kernels, attend(): pl.pallas_call(attend_kernel, grid=(1,), out_shape=[jax.ShapeDtypeStruct(...  32.2 us
    ppermute x15, waiting for transfers between devices, z_shift(): lax.ppermute(x, 'seq', [(s, (s // 2 + k) % 4 * 2 + s % 2) for s in range(...  30.9 us
    pallas_call x1, Pallas kernels, project(): pl.pallas_call(project_kernel, out_shape=jax.ShapeDtypeStruct((count, col...  16.9 us
    all_gather x1, waiting for transfers between devices, body(): own_a = lax.all_gather(one, 'dp', axis=0, axis_index_groups=XC, tiled=True)  13.2 us
    ppermute x4, waiting for transfers between devices, body(): other.append(lax.ppermute(mine, 'seq', [(s, s ^ 1) for s in range(8)]))  10.6 us
    ppermute x4, starting transfers between devices, moves(): yield (lambda x, code=code: lax.ppermute(x, 'dp', flip(code << 1)))  7.69 us
  transfers between devices with their start and end apart: 33, of which 16 were waited for; matrix products, arithmetic and copies ran while one was open for 3% of the time, Pallas kernels for 14%

profile of v5, /device:TPU:20, one launch (start us, length us, event | category | flops | bytes accessed | tf_op | source)
XLA Modules:
  0.0 304.8 jit_solution(15115161858123377486)
XLA Ops:
  14.6 4.3 %prep.1 = (bf16[4,128,768]{2,1,0:T(8,128)(2,1)S(1)}, bf16[4,128,768]{2,1,0:T(8,128)(2,1)S(1)}, bf16[4,128,768]{2,1,0:T(8,128)(2,1)S(1)}, bf16[4,128,768]{2,1,0:T(8,128)(2,1)S(1)}) custom-call(s32[4]{0:T(128)} %pad_add_fusion.z_ref.where_ref, s32[1,4]{1,0:T(1,128)} %marks_ref.1, bf16[512,2048]{1,0:T(8,128)(2,1)} %bitcast.38, ...), custom_call_target="tpu_custom_call" | custom-call | tf_op jit(solution)/shard_map/prep/pallas_call | solution.py:47
  18.9 20.0 %conditional.7 = (bf16[4,128,768]{2,1,0:T(8,128)(2,1)S(1)}) conditional(s32[]{:T(128)} %bitcast.11, bf16[4,128,768]{2,1,0:T(8,128)(2,1)S(1)} %get-tuple-element.86, bf16[4,128,768]{2,1,0:T(8,128)(2,1)S(1)} %get-tuple-element.86, bf16[4,128,768]{2,1,0:T(8,128)(2,1)S(1)} %get-tuple-element.86, ...), branch_computations={%region_25.0_spmd, %region_26.0_spmd, %region_27.0_spmd, %region_2... | conditional | bytes 4718640 | solution.py:333
  18.9 2.5 collective-permute-start.27
  21.5 17.3 %collective-permute-done.27 = bf16[4,128,768]{2,1,0:T(8,128)(2,1)S(1)} collective-permute-done((bf16[4,128,768]{2,1,0:T(8,128)(2,1)S(1)}, bf16[4,128,768]{2,1,0:T(8,128)(2,1)S(1)}, u32[]{:S(2)}, u32[]{:S(2)}) %collective-permute-start.27) | collective-permute-done | bytes 786464 | tf_op jit(solution)/shard_map/cond/branch_7_fun/ppermute | solution.py:67
  39.6 3.0 tie.1
  45.3 19.0 %conditional.4 = (bf16[4,128,768]{2,1,0:T(8,128)(2,1)S(1)}) conditional(s32[]{:T(128)} %bitcast.6, bf16[4,128,768]{2,1,0:T(8,128)(2,1)S(1)} %get-tuple-element.83, bf16[4,128,768]{2,1,0:T(8,128)(2,1)S(1)} %get-tuple-element.83, bf16[4,128,768]{2,1,0:T(8,128)(2,1)S(1)} %get-tuple-element.83, ...), branch_computations={%region_1.0_spmd, %region_2.0_spmd, %region_3.0_spmd, %region_4.0_... | conditional | bytes 4718640 | solution.py:333
  45.3 2.6 collective-permute-start.3
  47.9 16.3 %collective-permute-done.3 = bf16[4,128,768]{2,1,0:T(8,128)(2,1)S(1)} collective-permute-done((bf16[4,128,768]{2,1,0:T(8,128)(2,1)S(1)}, bf16[4,128,768]{2,1,0:T(8,128)(2,1)S(1)}, u32[]{:S(2)}, u32[]{:S(2)}) %collective-permute-start.3) | collective-permute-done | bytes 786464 | tf_op jit(solution)/shard_map/cond/branch_4_fun/ppermute | solution.py:67
  64.2 13.2 %all-gather.3.cloned.1.call-done.refs_4_ = bf16[1024,2048]{1,0:T(8,128)(2,1)} async-done(((bf16[128,2048]{1,0:T(8,128)(2,1)}), bf16[1024,2048]{1,0:T(8,128)(2,1)}) %all-gather.3.cloned.1.call-update) | async-done | bytes 4194320 | tf_op jit(solution)/shard_map/all_gather | solution.py:342
  77.4 3.1 %constant_dynamic-slice_fusion = (bf16[256,2048]{1,0:T(8,128)(2,1)}, bf16[256,2048]{1,0:T(8,128)(2,1)}) fusion(bf16[1024,2048]{1,0:T(8,128)(2,1)} %all-gather.3.cloned.1.call-done.refs_4_, s32[]{:T(128)S(6)} %select_n.7, s32[]{:T(128)S(6)} %select_n.6), kind=kLoop, calls=%fused_computation.14 | loop fusion | bytes 4194312 | tf_op jit(solution)/shard_map/dynamic_slice | solution.py:346
  81.7 3.4 %collective-permute-start.51 = (bf16[256,2048]{1,0:T(8,128)(2,1)}, bf16[256,2048]{1,0:T(8,128)(2,1)}, u32[]{:S(2)}, u32[]{:S(2)}) collective-permute-start(bf16[256,2048]{1,0:T(8,128)(2,1)} %get-tuple-element.94), channel_id=1, source_target_pairs={{0,65},{1,64},{2,67},{3,66},{4,69},{5,68},{6,71},{7,70},{8,73},{9,... | collective-permute-start | bytes 3145736 | tf_op jit(solution)/shard_map/ppermute | solution.py:311
  86.0 5.5 %collective-permute-start.32 = (bf16[128,768]{1,0:T(8,128)(2,1)}, bf16[128,768]{1,0:T(8,128)(2,1)S(1)}, u32[]{:S(2)}, u32[]{:S(2)}) collective-permute-start(bf16[128,768]{1,0:T(8,128)(2,1)} %get-tuple-element.106), channel_id=1, source_target_pairs={{0,6},{1,7},{2,0},{3,1},{4,2},{5,3},{6,4},{7,5},{8,14},{9,15},{10,... | collective-permute-start | bytes 589832 | tf_op jit(solution)/shard_map/ppermute | solution.py:71
  91.4 2.1 collective-permute-start.31
  93.6 33.4 %conditional.5 = (bf16[4,128,768]{2,1,0:T(8,128)(2,1)S(1)}) conditional(s32[]{:T(128)} %bitcast.9, bf16[4,128,768]{2,1,0:T(8,128)(2,1)S(1)} %get-tuple-element.84, bf16[4,128,768]{2,1,0:T(8,128)(2,1)S(1)} %get-tuple-element.84, bf16[4,128,768]{2,1,0:T(8,128)(2,1)S(1)} %get-tuple-element.84, ...), branch_computations={%region_9.0_spmd, %region_10.0_spmd, %region_11.0_spmd, %region_12... | conditional | bytes 4718640 | solution.py:333
  93.6 2.5 collective-permute-start.7
  96.0 30.8 %collective-permute-done.7 = bf16[4,128,768]{2,1,0:T(8,128)(2,1)S(1)} collective-permute-done((bf16[4,128,768]{2,1,0:T(8,128)(2,1)S(1)}, bf16[4,128,768]{2,1,0:T(8,128)(2,1)S(1)}, u32[]{:S(2)}, u32[]{:S(2)}) %collective-permute-start.7) | collective-permute-done | bytes 786464 | tf_op jit(solution)/shard_map/cond/branch_1_fun/ppermute | solution.py:67
  127.0 28.4 %conditional.6 = (bf16[4,128,768]{2,1,0:T(8,128)(2,1)S(1)}) conditional(s32[]{:T(128)} %bitcast.10, bf16[4,128,768]{2,1,0:T(8,128)(2,1)S(1)} %get-tuple-element.85, bf16[4,128,768]{2,1,0:T(8,128)(2,1)S(1)} %get-tuple-element.85, bf16[4,128,768]{2,1,0:T(8,128)(2,1)S(1)} %get-tuple-element.85, ...), branch_computations={%region_17.0_spmd, %region_18.0_spmd, %region_19.0_spmd, %region_2... | conditional | bytes 4718640 | solution.py:333
  127.1 28.1 %collective-permute-done.16 = bf16[4,128,768]{2,1,0:T(8,128)(2,1)S(1)} collective-permute-done((bf16[4,128,768]{2,1,0:T(8,128)(2,1)S(1)}, bf16[4,128,768]{2,1,0:T(8,128)(2,1)S(1)}, u32[]{:S(2)}, u32[]{:S(2)}) %collective-permute-start.16) | collective-permute-done | bytes 786464 | tf_op jit(solution)/shard_map/cond/branch_3_fun/ppermute | solution.py:67
  155.4 11.4 %collective-permute-start.30 = (bf16[128,768]{1,0:T(8,128)(2,1)}, bf16[128,768]{1,0:T(8,128)(2,1)}, u32[]{:S(2)}, u32[]{:S(2)}) collective-permute-start(bf16[128,768]{1,0:T(8,128)(2,1)} %get-tuple-element.108), channel_id=1, source_target_pairs={{0,2},{1,3},{2,4},{3,5},{4,6},{5,7},{6,0},{7,1},{8,10},{9,11},{10,... | collective-permute-start | bytes 589832 | tf_op jit(solution)/shard_map/ppermute | solution.py:71
  169.8 2.6 collective-permute-done.30.refs_1_.refs_4_
  172.4 2.5 collective-permute-start.39
  176.5 4.7 %collective-permute-start.34 = (bf16[128,768]{1,0:T(8,128)(2,1)}, bf16[128,768]{1,0:T(8,128)(2,1)}, u32[]{:S(2)}, u32[]{:S(2)}) collective-permute-start(bf16[128,768]{1,0:T(8,128)(2,1)} %get-tuple-element.104), channel_id=1, source_target_pairs={{0,4},{1,5},{2,6},{3,7},{4,0},{5,1},{6,2},{7,3},{8,12},{9,13},{10,... | collective-permute-start | bytes 589832 | tf_op jit(solution)/shard_map/ppermute | solution.py:71
  189.3 4.2 %collective-permute-start.37 = (bf16[128,768]{1,0:T(8,128)(2,1)}, bf16[128,768]{1,0:T(8,128)(2,1)S(1)}, u32[]{:S(2)}, u32[]{:S(2)}) collective-permute-start(bf16[128,768]{1,0:T(8,128)(2,1)} %get-tuple-element.101), channel_id=1, source_target_pairs={{0,4},{1,5},{2,6},{3,7},{4,0},{5,1},{6,2},{7,3},{8,12},{9,13},{10,... | collective-permute-start | bytes 589832 | tf_op jit(solution)/shard_map/ppermute | solution.py:71
  199.5 2.7 collective-permute-start.45
  203.1 2.7 collective-permute-start.43
  209.3 5.6 %collective-permute-done.43.refs_17_ = bf16[4,128,256]{2,1,0:T(8,128)(2,1)} collective-permute-done((bf16[4,128,256]{2,1,0:T(8,128)(2,1)}, bf16[4,128,256]{2,1,0:T(8,128)(2,1)}, u32[]{:S(2)}, u32[]{:S(2)}) %collective-permute-start.43) | collective-permute-done | bytes 262176 | tf_op jit(solution)/shard_map/ppermute | solution.py:340
  214.9 4.6 %collective-permute-done.44.refs_18_ = bf16[4,128,256]{2,1,0:T(8,128)(2,1)S(1)} collective-permute-done((bf16[4,128,256]{2,1,0:T(8,128)(2,1)}, bf16[4,128,256]{2,1,0:T(8,128)(2,1)S(1)}, u32[]{:S(2)}, u32[]{:S(2)}) %collective-permute-start.44) | collective-permute-done | bytes 262176 | tf_op jit(solution)/shard_map/ppermute | solution.py:340
  220.2 32.2 %attend.1 = (bf16[512,512]{1,0:T(8,128)(2,1)}, bf16[512,512]{1,0:T(8,128)(2,1)}, bf16[512,512]{1,0:T(8,128)(2,1)}, bf16[512,512]{1,0:T(8,128)(2,1)}) custom-call(s32[4]{0:T(128)} %pad_add_fusion.z_ref.where_ref, s32[1,32]{1,0:T(1,128)} %bitcast.41, bf16[4,128,768]{2,1,0:T(8,128)(2,1)S(1)} %get-tuple-element.113.refs_0_, ...), custom_call_target="tpu_custom_call" | custom-call | tf_op jit(solution)/shard_map/attend/pallas_call | solution.py:165
  253.3 2.2 collective-permute-start.47
  255.5 2.5 collective-permute-start.48
  258.0 21.6 %collective-permute-done.46.refs_1_ = bf16[512,512]{1,0:T(8,128)(2,1)S(1)} collective-permute-done((bf16[512,512]{1,0:T(8,128)(2,1)}, bf16[512,512]{1,0:T(8,128)(2,1)S(1)}, u32[]{:S(2)}, u32[]{:S(2)}) %collective-permute-start.46) | collective-permute-done | bytes 524320 | tf_op jit(solution)/shard_map/ppermute | solution.py:71
  281.0 16.9 %project.1 = bf16[512,4096]{1,0:T(8,128)(2,1)} custom-call(s32[4]{0:T(128)} %pad_add_fusion.z_ref.where_ref, bf16[512,512]{1,0:T(8,128)(2,1)} %get-tuple-element.87.refs_0_, bf16[512,512]{1,0:T(8,128)(2,1)} %copy-done.5, bf16[512,512]{1,0:T(8,128)(2,1)} %copy-done.6, bf16[512,512]{1,0:T(8,128)(2,1)} %copy-done.7, ...), custom_call_target="tpu_custom_call" | custom-call | tf_op jit(solution)/shard_map/project/pallas_call | solution.py:253
  (83 shorter events, 37.2 us)
Async XLA Ops:
  6.5 70.9 %all-gather.3.cloned.1.call-start = ((), (), s32[]{:S(2)}) async-start(), calls=%async_computation | async-start | bytes 4718592 | tf_op jit(solution)/shard_map/all_gather | solution.py:342
  6.5 8.0 %collective-permute-start.28 = (bf16[512,2048]{1,0:T(8,128)(2,1)}, bf16[512,2048]{1,0:T(8,128)(2,1)}, u32[]{:S(2)}, u32[]{:S(2)}) collective-permute-start(bf16[512,2048]{1,0:T(8,128)(2,1)} %bitcast.37), channel_id=1, source_target_pairs={{0,8},{8,0},{16,24},{24,16},{32,40},{40,32},{48,56},{56,48},{64,72... | collective-permute-start | bytes 6291464 | tf_op jit(solution)/shard_map/ppermute | solution.py:318
  8.9 29.9 %collective-permute-start.50 = (bf16[64,2048]{1,0:T(8,128)(2,1)}, bf16[64,2048]{1,0:T(8,128)(2,1)S(1)}, u32[]{:S(2)}, u32[]{:S(2)}) collective-permute-start(bf16[64,2048]{1,0:T(8,128)(2,1)} %get-tuple-element.95), channel_id=1, source_target_pairs={{0,65},{1,64},{2,67},{3,66},{4,69},{5,68},{6,71},{7,70},{8,73},{9,... | collective-permute-start | bytes 786440 | tf_op jit(solution)/shard_map/ppermute | solution.py:311
  9.4 29.5 %collective-permute-start.49 = (bf16[64,2048]{1,0:T(8,128)(2,1)}, bf16[64,2048]{1,0:T(8,128)(2,1)}, u32[]{:S(2)}, u32[]{:S(2)}) collective-permute-start(bf16[64,2048]{1,0:T(8,128)(2,1)} %get-tuple-element.96), channel_id=1, source_target_pairs={{0,64},{1,65},{2,66},{3,67},{4,68},{5,69},{6,70},{7,71},{8,72},{9,... | collective-permute-start | bytes 786440 | tf_op jit(solution)/shard_map/ppermute | solution.py:311
  18.9 19.9 %collective-permute-start.27 = (bf16[4,128,768]{2,1,0:T(8,128)(2,1)S(1)}, bf16[4,128,768]{2,1,0:T(8,128)(2,1)S(1)}, u32[]{:S(2)}, u32[]{:S(2)}) collective-permute-start(bf16[4,128,768]{2,1,0:T(8,128)(2,1)S(1)} %param.31), channel_id=1, source_target_pairs={{0,112},{8,120},{16,96},{24,104},{32,80},{40,88},{48,64},{56,72},{... | collective-permute-start | bytes 2359304 | tf_op jit(solution)/shard_map/cond/branch_7_fun/ppermute | solution.py:67
  42.6 237.7 %all-gather.5.cloned.1.call-start = ((), (), s32[]{:S(2)}) async-start(), calls=%async_computation.1 | async-start | bytes 9437184 | tf_op jit(solution)/shard_map/all_gather | solution.py:343
  45.3 18.9 %collective-permute-start.3 = (bf16[4,128,768]{2,1,0:T(8,128)(2,1)S(1)}, bf16[4,128,768]{2,1,0:T(8,128)(2,1)S(1)}, u32[]{:S(2)}, u32[]{:S(2)}) collective-permute-start(bf16[4,128,768]{2,1,0:T(8,128)(2,1)S(1)} %param.4), channel_id=1, source_target_pairs={{0,64},{8,72},{16,80},{24,88},{32,96},{40,104},{48,112},{56,120},{... | collective-permute-start | bytes 2359304 | tf_op jit(solution)/shard_map/cond/branch_4_fun/ppermute | solution.py:67
  80.5 106.9 %collective-permute-start.52 = (bf16[256,2048]{1,0:T(8,128)(2,1)}, bf16[256,2048]{1,0:T(8,128)(2,1)}, u32[]{:S(2)}, u32[]{:S(2)}) collective-permute-start(bf16[256,2048]{1,0:T(8,128)(2,1)} %get-tuple-element.93), channel_id=1, source_target_pairs={{0,64},{1,65},{2,66},{3,67},{4,68},{5,69},{6,70},{7,71},{8,72},{9,... | collective-permute-start | bytes 3145736 | tf_op jit(solution)/shard_map/ppermute | solution.py:311
  81.7 105.7 %collective-permute-start.51 = (bf16[256,2048]{1,0:T(8,128)(2,1)}, bf16[256,2048]{1,0:T(8,128)(2,1)}, u32[]{:S(2)}, u32[]{:S(2)}) collective-permute-start(bf16[256,2048]{1,0:T(8,128)(2,1)} %get-tuple-element.94), channel_id=1, source_target_pairs={{0,65},{1,64},{2,67},{3,66},{4,69},{5,68},{6,71},{7,70},{8,73},{9,... | collective-permute-start | bytes 3145736 | tf_op jit(solution)/shard_map/ppermute | solution.py:311
  86.0 80.9 %collective-permute-start.32 = (bf16[128,768]{1,0:T(8,128)(2,1)}, bf16[128,768]{1,0:T(8,128)(2,1)S(1)}, u32[]{:S(2)}, u32[]{:S(2)}) collective-permute-start(bf16[128,768]{1,0:T(8,128)(2,1)} %get-tuple-element.106), channel_id=1, source_target_pairs={{0,6},{1,7},{2,0},{3,1},{4,2},{5,3},{6,4},{7,5},{8,14},{9,15},{10,... | collective-permute-start | bytes 589832 | tf_op jit(solution)/shard_map/ppermute | solution.py:71
  91.4 75.5 %collective-permute-start.31 = (bf16[128,768]{1,0:T(8,128)(2,1)}, bf16[128,768]{1,0:T(8,128)(2,1)S(1)}, u32[]{:S(2)}, u32[]{:S(2)}) collective-permute-start(bf16[128,768]{1,0:T(8,128)(2,1)} %get-tuple-element.107), channel_id=1, source_target_pairs={{0,4},{1,5},{2,6},{3,7},{4,0},{5,1},{6,2},{7,3},{8,12},{9,13},{10,... | collective-permute-start | bytes 589832 | tf_op jit(solution)/shard_map/ppermute | solution.py:71
  93.6 33.3 %collective-permute-start.7 = (bf16[4,128,768]{2,1,0:T(8,128)(2,1)S(1)}, bf16[4,128,768]{2,1,0:T(8,128)(2,1)S(1)}, u32[]{:S(2)}, u32[]{:S(2)}) collective-permute-start(bf16[4,128,768]{2,1,0:T(8,128)(2,1)S(1)} %param.9), channel_id=1, source_target_pairs={{0,16},{8,24},{16,0},{24,8},{32,48},{40,56},{48,32},{56,40},{64,80... | collective-permute-start | bytes 2359304 | tf_op jit(solution)/shard_map/cond/branch_1_fun/ppermute | solution.py:67
  127.0 28.2 %collective-permute-start.16 = (bf16[4,128,768]{2,1,0:T(8,128)(2,1)S(1)}, bf16[4,128,768]{2,1,0:T(8,128)(2,1)S(1)}, u32[]{:S(2)}, u32[]{:S(2)}) collective-permute-start(bf16[4,128,768]{2,1,0:T(8,128)(2,1)S(1)} %param.19), channel_id=1, source_target_pairs={{0,48},{8,56},{16,32},{24,40},{32,16},{40,24},{48,0},{56,8},{64,11... | collective-permute-start | bytes 2359304 | tf_op jit(solution)/shard_map/cond/branch_3_fun/ppermute | solution.py:67
  155.4 17.0 %collective-permute-start.30 = (bf16[128,768]{1,0:T(8,128)(2,1)}, bf16[128,768]{1,0:T(8,128)(2,1)}, u32[]{:S(2)}, u32[]{:S(2)}) collective-permute-start(bf16[128,768]{1,0:T(8,128)(2,1)} %get-tuple-element.108), channel_id=1, source_target_pairs={{0,2},{1,3},{2,4},{3,5},{4,6},{5,7},{6,0},{7,1},{8,10},{9,11},{10,... | collective-permute-start | bytes 589832 | tf_op jit(solution)/shard_map/ppermute | solution.py:71
  166.9 8.0 %collective-permute-start.41 = (bf16[128,768]{1,0:T(8,128)(2,1)S(1)}, bf16[128,768]{1,0:T(8,128)(2,1)}, u32[]{:S(2)}, u32[]{:S(2)}) collective-permute-start(bf16[128,768]{1,0:T(8,128)(2,1)S(1)} %get-tuple-element.97), channel_id=1, source_target_pairs={{0,6},{1,7},{2,0},{3,1},{4,2},{5,3},{6,4},{7,5},{8,14},{9,15},{10,... | collective-permute-start | bytes 589832 | tf_op jit(solution)/shard_map/ppermute | solution.py:71
  167.0 9.5 %collective-permute-start.40 = (bf16[128,768]{1,0:T(8,128)(2,1)S(1)}, bf16[128,768]{1,0:T(8,128)(2,1)}, u32[]{:S(2)}, u32[]{:S(2)}) collective-permute-start(bf16[128,768]{1,0:T(8,128)(2,1)S(1)} %get-tuple-element.98), channel_id=1, source_target_pairs={{0,4},{1,5},{2,6},{3,7},{4,0},{5,1},{6,2},{7,3},{8,12},{9,13},{10,... | collective-permute-start | bytes 589832 | tf_op jit(solution)/shard_map/ppermute | solution.py:71
  172.4 9.7 %collective-permute-start.39 = (bf16[128,768]{1,0:T(8,128)(2,1)S(1)}, bf16[128,768]{1,0:T(8,128)(2,1)}, u32[]{:S(2)}, u32[]{:S(2)}) collective-permute-start(bf16[128,768]{1,0:T(8,128)(2,1)S(1)} %get-tuple-element.99), channel_id=1, source_target_pairs={{0,2},{1,3},{2,4},{3,5},{4,6},{5,7},{6,0},{7,1},{8,10},{9,11},{10,... | collective-permute-start | bytes 589832 | tf_op jit(solution)/shard_map/ppermute | solution.py:71
  174.9 9.8 %collective-permute-start.35 = (bf16[128,768]{1,0:T(8,128)(2,1)S(1)}, bf16[128,768]{1,0:T(8,128)(2,1)}, u32[]{:S(2)}, u32[]{:S(2)}) collective-permute-start(bf16[128,768]{1,0:T(8,128)(2,1)S(1)} %get-tuple-element.103), channel_id=1, source_target_pairs={{0,6},{1,7},{2,0},{3,1},{4,2},{5,3},{6,4},{7,5},{8,14},{9,15},{10,... | collective-permute-start | bytes 589832 | tf_op jit(solution)/shard_map/ppermute | solution.py:71
  176.5 10.5 %collective-permute-start.34 = (bf16[128,768]{1,0:T(8,128)(2,1)}, bf16[128,768]{1,0:T(8,128)(2,1)}, u32[]{:S(2)}, u32[]{:S(2)}) collective-permute-start(bf16[128,768]{1,0:T(8,128)(2,1)} %get-tuple-element.104), channel_id=1, source_target_pairs={{0,4},{1,5},{2,6},{3,7},{4,0},{5,1},{6,2},{7,3},{8,12},{9,13},{10,... | collective-permute-start | bytes 589832 | tf_op jit(solution)/shard_map/ppermute | solution.py:71
  182.1 7.2 %collective-permute-start.33 = (bf16[128,768]{1,0:T(8,128)(2,1)}, bf16[128,768]{1,0:T(8,128)(2,1)}, u32[]{:S(2)}, u32[]{:S(2)}) collective-permute-start(bf16[128,768]{1,0:T(8,128)(2,1)} %get-tuple-element.105), channel_id=1, source_target_pairs={{0,2},{1,3},{2,4},{3,5},{4,6},{5,7},{6,0},{7,1},{8,10},{9,11},{10,... | collective-permute-start | bytes 589832 | tf_op jit(solution)/shard_map/ppermute | solution.py:71
  184.6 8.9 %collective-permute-start.38 = (bf16[128,768]{1,0:T(8,128)(2,1)}, bf16[128,768]{1,0:T(8,128)(2,1)}, u32[]{:S(2)}, u32[]{:S(2)}) collective-permute-start(bf16[128,768]{1,0:T(8,128)(2,1)} %get-tuple-element.100), channel_id=1, source_target_pairs={{0,6},{1,7},{2,0},{3,1},{4,2},{5,3},{6,4},{7,5},{8,14},{9,15},{10,... | collective-permute-start | bytes 589832 | tf_op jit(solution)/shard_map/ppermute | solution.py:71
  187.0 20.4 %collective-permute-start.42 = (bf16[4,128,256]{2,1,0:T(8,128)(2,1)}, bf16[4,128,256]{2,1,0:T(8,128)(2,1)}, u32[]{:S(2)}, u32[]{:S(2)}) collective-permute-start(bf16[4,128,256]{2,1,0:T(8,128)(2,1)} %collect.4), channel_id=1, source_target_pairs={{0,1},{1,0},{2,3},{3,2},{4,5},{5,4},{6,7},{7,6},{8,9},{9,8},{10,11... | collective-permute-start | bytes 786440 | tf_op jit(solution)/shard_map/ppermute | solution.py:340
  187.4 92.8 %collective-permute-start.54 = (bf16[256,2048]{1,0:T(8,128)(2,1)}, bf16[256,2048]{1,0:T(8,128)(2,1)}, u32[]{:S(2)}, u32[]{:S(2)}) collective-permute-start(bf16[256,2048]{1,0:T(8,128)(2,1)} %collective-permute-done.52.refs_6_), channel_id=1, source_target_pairs={{0,8},{8,0},{16,24},{24,16},{32,40},{40,32},{48,56},{56,48},{64,72... | collective-permute-start | bytes 3145736 | tf_op jit(solution)/shard_map/ppermute | solution.py:349
  187.4 92.8 %collective-permute-start.53 = (bf16[256,2048]{1,0:T(8,128)(2,1)}, bf16[256,2048]{1,0:T(8,128)(2,1)}, u32[]{:S(2)}, u32[]{:S(2)}) collective-permute-start(bf16[256,2048]{1,0:T(8,128)(2,1)} %collective-permute-done.51.refs_5_), channel_id=1, source_target_pairs={{0,8},{8,0},{16,24},{24,16},{32,40},{40,32},{48,56},{56,48},{64,72... | collective-permute-start | bytes 3145736 | tf_op jit(solution)/shard_map/ppermute | solution.py:349
  189.3 10.2 %collective-permute-start.37 = (bf16[128,768]{1,0:T(8,128)(2,1)}, bf16[128,768]{1,0:T(8,128)(2,1)S(1)}, u32[]{:S(2)}, u32[]{:S(2)}) collective-permute-start(bf16[128,768]{1,0:T(8,128)(2,1)} %get-tuple-element.101), channel_id=1, source_target_pairs={{0,4},{1,5},{2,6},{3,7},{4,0},{5,1},{6,2},{7,3},{8,12},{9,13},{10,... | collective-permute-start | bytes 589832 | tf_op jit(solution)/shard_map/ppermute | solution.py:71
  193.5 9.6 %collective-permute-start.36 = (bf16[128,768]{1,0:T(8,128)(2,1)}, bf16[128,768]{1,0:T(8,128)(2,1)S(1)}, u32[]{:S(2)}, u32[]{:S(2)}) collective-permute-start(bf16[128,768]{1,0:T(8,128)(2,1)} %get-tuple-element.102), channel_id=1, source_target_pairs={{0,2},{1,3},{2,4},{3,5},{4,6},{5,7},{6,0},{7,1},{8,10},{9,11},{10,... | collective-permute-start | bytes 589832 | tf_op jit(solution)/shard_map/ppermute | solution.py:71
  199.5 9.8 %collective-permute-start.45 = (bf16[4,128,256]{2,1,0:T(8,128)(2,1)}, bf16[4,128,256]{2,1,0:T(8,128)(2,1)}, u32[]{:S(2)}, u32[]{:S(2)}) collective-permute-start(bf16[4,128,256]{2,1,0:T(8,128)(2,1)} %collect.7), channel_id=1, source_target_pairs={{0,1},{1,0},{2,3},{3,2},{4,5},{5,4},{6,7},{7,6},{8,9},{9,8},{10,11... | collective-permute-start | bytes 786440 | tf_op jit(solution)/shard_map/ppermute | solution.py:340
  203.1 11.9 %collective-permute-start.43 = (bf16[4,128,256]{2,1,0:T(8,128)(2,1)}, bf16[4,128,256]{2,1,0:T(8,128)(2,1)}, u32[]{:S(2)}, u32[]{:S(2)}) collective-permute-start(bf16[4,128,256]{2,1,0:T(8,128)(2,1)} %collect.5), channel_id=1, source_target_pairs={{0,1},{1,0},{2,3},{3,2},{4,5},{5,4},{6,7},{7,6},{8,9},{9,8},{10,11... | collective-permute-start | bytes 786440 | tf_op jit(solution)/shard_map/ppermute | solution.py:340
  207.5 12.1 %collective-permute-start.44 = (bf16[4,128,256]{2,1,0:T(8,128)(2,1)}, bf16[4,128,256]{2,1,0:T(8,128)(2,1)S(1)}, u32[]{:S(2)}, u32[]{:S(2)}) collective-permute-start(bf16[4,128,256]{2,1,0:T(8,128)(2,1)} %collect.6), channel_id=1, source_target_pairs={{0,1},{1,0},{2,3},{3,2},{4,5},{5,4},{6,7},{7,6},{8,9},{9,8},{10,11... | collective-permute-start | bytes 786440 | tf_op jit(solution)/shard_map/ppermute | solution.py:340
  252.4 27.2 %collective-permute-start.46 = (bf16[512,512]{1,0:T(8,128)(2,1)}, bf16[512,512]{1,0:T(8,128)(2,1)S(1)}, u32[]{:S(2)}, u32[]{:S(2)}) collective-permute-start(bf16[512,512]{1,0:T(8,128)(2,1)} %get-tuple-element.88), channel_id=1, source_target_pairs={{0,2},{1,3},{2,4},{3,5},{4,6},{5,7},{6,0},{7,1},{8,10},{9,11},{10,... | collective-permute-start | bytes 1572872 | tf_op jit(solution)/shard_map/ppermute | solution.py:71
  253.3 26.3 %collective-permute-start.47 = (bf16[512,512]{1,0:T(8,128)(2,1)}, bf16[512,512]{1,0:T(8,128)(2,1)S(1)}, u32[]{:S(2)}, u32[]{:S(2)}) collective-permute-start(bf16[512,512]{1,0:T(8,128)(2,1)} %get-tuple-element.89), channel_id=1, source_target_pairs={{0,4},{1,5},{2,6},{3,7},{4,0},{5,1},{6,2},{7,3},{8,12},{9,13},{10,... | collective-permute-start | bytes 1572872 | tf_op jit(solution)/shard_map/ppermute | solution.py:71
  255.5 24.7 %collective-permute-start.48 = (bf16[512,512]{1,0:T(8,128)(2,1)}, bf16[512,512]{1,0:T(8,128)(2,1)S(1)}, u32[]{:S(2)}, u32[]{:S(2)}) collective-permute-start(bf16[512,512]{1,0:T(8,128)(2,1)} %get-tuple-element.90), channel_id=1, source_target_pairs={{0,6},{1,7},{2,0},{3,1},{4,2},{5,3},{6,4},{7,5},{8,14},{9,15},{10,... | collective-permute-start | bytes 1572872 | tf_op jit(solution)/shard_map/ppermute | solution.py:71
  (12 other events, 99.4 us)
Sparse Core Ops, SparseCore 0:
  42.7 34.6 all-gather.2
  79.1 73.1 all-gather.4

commit v6 on v4

--- a/solution.py
+++ b/solution.py
@@ -243,20 +243,20 @@
 
 def tie(where, own, lo, hi, token):
     rows, cols = own.shape
-    half = pl.BlockSpec((rows // 2, cols // 4), lambda i, w: (0, i))
+    half = pl.BlockSpec((rows // 2, cols // 2), lambda i, w: (0, i))
     return pl.pallas_call(
         tie_kernel,
         out_shape=jax.ShapeDtypeStruct((2 * rows, cols), own.dtype),
         grid_spec=pltpu.PrefetchScalarGridSpec(
             num_scalar_prefetch=1,
-            grid=(4,),
+            grid=(2,),
             in_specs=[
-                pl.BlockSpec((rows, cols // 4), lambda i, w: (0, i)),
+                pl.BlockSpec((rows, cols // 2), lambda i, w: (0, i)),
                 half,
                 half,
                 pl.BlockSpec(memory_space=pl.ANY),
             ],
-            out_specs=pl.BlockSpec((2 * rows, cols // 4), lambda i, w: (0, i)),
+            out_specs=pl.BlockSpec((2 * rows, cols // 2), lambda i, w: (0, i)),
         ),
         name="tie",
     )(where, own, lo, hi, token)

time: 268 us -> 267 us (level)
  transfers between devices with their start and end apart: 28 -> 28, of which waited for: 11 -> 11; matrix products, arithmetic and copies ran while one was open for 3% -> 3% of each run, Pallas kernels for 15% -> 16%
where the time goes in v6:
time: 267 us; the launch traced here: 266 us
  waiting for transfers between devices  137 us (51%)
  Pallas kernels  60.9 us (23%)
  starting transfers between devices  42.2 us (16%)
  between operations  16.1 us (6%)
  local copies, waits for them, and re-layouts  8.27 us (3%)
    ppermute x4, waiting for transfers between devices, moves(): yield (lambda x, code=code: lax.ppermute(x, 'dp', flip(code << 1)))  108 us
    pallas_call x1, Pallas kernels, attend(): pl.pallas_call(attend_kernel, grid=(1,), out_shape=[jax.ShapeDtypeStruct(...  30.5 us
    ppermute x15, waiting for transfers between devices, z_shift(): lax.ppermute(x, 'seq', [(s, (s // 2 + k) % 4 * 2 + s % 2) for s in range(...  21.4 us
    ppermute x15, starting transfers between devices, z_shift(): lax.ppermute(x, 'seq', [(s, (s // 2 + k) % 4 * 2 + s % 2) for s in range(...  20.2 us
    pallas_call x1, Pallas kernels, project(): pl.pallas_call(project_kernel, out_shape=jax.ShapeDtypeStruct((count, col...  16.3 us
    ppermute x4, starting transfers between devices, body(): other.append(lax.ppermute(mine, 'seq', [(s, s ^ 1) for s in range(8)]))  10.8 us
    ppermute x4, waiting for transfers between devices, body(): other.append(lax.ppermute(mine, 'seq', [(s, s ^ 1) for s in range(8)]))  8.24 us
    ppermute x4, starting transfers between devices, moves(): yield (lambda x, code=code: lax.ppermute(x, 'dp', flip(code << 1)))  7.72 us
  transfers between devices with their start and end apart: 28, of which 11 were waited for; matrix products, arithmetic and copies ran while one was open for 3% of the time, Pallas kernels for 16%

profile of v6, /device:TPU:2, one launch (start us, length us, event | category | flops | bytes accessed | tf_op | source)
XLA Modules:
  0.0 266.4 jit_solution(5544136949398012165)
XLA Ops:
  7.1 2.3 fusion
  9.3 3.0 %collective-permute-start.50 = (bf16[64,4096]{1,0:T(8,128)(2,1)}, bf16[64,4096]{1,0:T(8,128)(2,1)}, u32[]{:S(2)}, u32[]{:S(2)}) collective-permute-start(bf16[64,4096]{1,0:T(8,128)(2,1)} %get-tuple-element.89), channel_id=1, source_target_pairs={{0,65},{1,64},{2,67},{3,66},{4,69},{5,68},{6,71},{7,70},{8,73},{9,... | collective-permute-start | bytes 1572872 | tf_op jit(solution)/shard_map/ppermute | solution.py:271
  15.4 4.3 %prep.1 = (bf16[4,128,768]{2,1,0:T(8,128)(2,1)S(1)}, bf16[4,128,768]{2,1,0:T(8,128)(2,1)S(1)}, bf16[4,128,768]{2,1,0:T(8,128)(2,1)S(1)}, bf16[4,128,768]{2,1,0:T(8,128)(2,1)S(1)}) custom-call(s32[3]{0:T(128)} %pad_add_fusion.z_ref.where_ref, s32[1,4]{1,0:T(1,128)} %marks_ref.1, bf16[512,2048]{1,0:T(8,128)(2,1)} %bitcast.37, ...), custom_call_target="tpu_custom_call" | custom-call | tf_op jit(solution)/shard_map/prep/pallas_call | solution.py:45
  19.7 19.3 %conditional.7 = (bf16[4,128,768]{2,1,0:T(8,128)(2,1)S(1)}) conditional(s32[]{:T(128)} %bitcast.10, bf16[4,128,768]{2,1,0:T(8,128)(2,1)S(1)} %get-tuple-element.84, bf16[4,128,768]{2,1,0:T(8,128)(2,1)S(1)} %get-tuple-element.84, bf16[4,128,768]{2,1,0:T(8,128)(2,1)S(1)} %get-tuple-element.84, ...), branch_computations={%region_25.0_spmd, %region_26.0_spmd, %region_27.0_spmd, %region_2... | conditional | bytes 4718640 | solution.py:291
  21.3 17.7 %collective-permute-done.23 = bf16[4,128,768]{2,1,0:T(8,128)(2,1)S(1)} collective-permute-done((bf16[4,128,768]{2,1,0:T(8,128)(2,1)S(1)}, bf16[4,128,768]{2,1,0:T(8,128)(2,1)S(1)}, u32[]{:S(2)}, u32[]{:S(2)}) %collective-permute-start.23) | collective-permute-done | bytes 786464 | tf_op jit(solution)/shard_map/cond/branch_3_fun/ppermute | solution.py:65
  39.1 3.3 %tie.1 = bf16[256,4096]{1,0:T(8,128)(2,1)} custom-call(s32[3]{0:T(128)} %pad_add_fusion.z_ref.where_ref, bf16[128,4096]{1,0:T(8,128)(2,1)} %own_ref.1, bf16[64,4096]{1,0:T(8,128)(2,1)} %collective-permute-done.49.lo_ref, bf16[64,4096]{1,0:T(8,128)(2,1)} %collective-permute-done.50.hi_ref, bf16[4,128,768]{2,1,0:T(8,128)(2,1)S(1)} %get-tuple-element.110.refs_0_.refs_3_.token_ref), custom_call_target="tpu_custom_call" | custom-call | tf_op jit(solution)/shard_map/tie/pallas_call | solution.py:247
  44.2 23.9 %conditional.4 = (bf16[4,128,768]{2,1,0:T(8,128)(2,1)S(1)}) conditional(s32[]{:T(128)} %bitcast.5, bf16[4,128,768]{2,1,0:T(8,128)(2,1)S(1)} %get-tuple-element.81, bf16[4,128,768]{2,1,0:T(8,128)(2,1)S(1)} %get-tuple-element.81, bf16[4,128,768]{2,1,0:T(8,128)(2,1)S(1)} %get-tuple-element.81, ...), branch_computations={%region_1.0_spmd, %region_2.0_spmd, %region_3.0_spmd, %region_4.0_... | conditional | bytes 4718640 | solution.py:291
  44.2 1.8 collective-permute-start
  46.1 22.0 %collective-permute-done = bf16[4,128,768]{2,1,0:T(8,128)(2,1)S(1)} collective-permute-done((bf16[4,128,768]{2,1,0:T(8,128)(2,1)S(1)}, bf16[4,128,768]{2,1,0:T(8,128)(2,1)S(1)}, u32[]{:S(2)}, u32[]{:S(2)}) %collective-permute-start) | collective-permute-done | bytes 786464 | tf_op jit(solution)/shard_map/cond/branch_1_fun/ppermute | solution.py:65
  72.5 2.0 collective-permute-start.41
  74.5 37.1 %conditional.5 = (bf16[4,128,768]{2,1,0:T(8,128)(2,1)S(1)}) conditional(s32[]{:T(128)} %bitcast.8, bf16[4,128,768]{2,1,0:T(8,128)(2,1)S(1)} %get-tuple-element.82, bf16[4,128,768]{2,1,0:T(8,128)(2,1)S(1)} %get-tuple-element.82, bf16[4,128,768]{2,1,0:T(8,128)(2,1)S(1)} %get-tuple-element.82, ...), branch_computations={%region_9.0_spmd, %region_10.0_spmd, %region_11.0_spmd, %region_12... | conditional | bytes 4718640 | solution.py:291
  74.5 2.5 collective-permute-start.13
  77.0 34.6 %collective-permute-done.13 = bf16[4,128,768]{2,1,0:T(8,128)(2,1)S(1)} collective-permute-done((bf16[4,128,768]{2,1,0:T(8,128)(2,1)S(1)}, bf16[4,128,768]{2,1,0:T(8,128)(2,1)S(1)}, u32[]{:S(2)}, u32[]{:S(2)}) %collective-permute-start.13) | collective-permute-done | bytes 786464 | tf_op jit(solution)/shard_map/cond/branch_7_fun/ppermute | solution.py:65
  111.7 35.5 %conditional.6 = (bf16[4,128,768]{2,1,0:T(8,128)(2,1)S(1)}) conditional(s32[]{:T(128)} %bitcast.9, bf16[4,128,768]{2,1,0:T(8,128)(2,1)S(1)} %get-tuple-element.83, bf16[4,128,768]{2,1,0:T(8,128)(2,1)S(1)} %get-tuple-element.83, bf16[4,128,768]{2,1,0:T(8,128)(2,1)S(1)} %get-tuple-element.83, ...), branch_computations={%region_17.0_spmd, %region_18.0_spmd, %region_19.0_spmd, %region_2... | conditional | bytes 4718640 | solution.py:291
  111.7 1.9 collective-permute-start.14
  113.5 33.4 %collective-permute-done.14 = bf16[4,128,768]{2,1,0:T(8,128)(2,1)S(1)} collective-permute-done((bf16[4,128,768]{2,1,0:T(8,128)(2,1)S(1)}, bf16[4,128,768]{2,1,0:T(8,128)(2,1)S(1)}, u32[]{:S(2)}, u32[]{:S(2)}) %collective-permute-start.14) | collective-permute-done | bytes 786464 | tf_op jit(solution)/shard_map/cond/branch_1_fun/ppermute | solution.py:65
  147.1 2.6 collective-permute-start.40
  150.9 2.8 %collective-permute-start.35 = (bf16[128,768]{1,0:T(8,128)(2,1)S(1)}, bf16[128,768]{1,0:T(8,128)(2,1)}, u32[]{:S(2)}, u32[]{:S(2)}) collective-permute-start(bf16[128,768]{1,0:T(8,128)(2,1)S(1)} %get-tuple-element.97), channel_id=1, source_target_pairs={{0,6},{1,7},{2,0},{3,1},{4,2},{5,3},{6,4},{7,5},{8,14},{9,15},{10,... | collective-permute-start | bytes 589832 | tf_op jit(solution)/shard_map/ppermute | solution.py:69
  156.6 2.4 collective-permute-start.38
  158.9 2.9 %collective-permute-done.39.refs_1_.refs_13_ = bf16[128,768]{1,0:T(8,128)(2,1)} collective-permute-done((bf16[128,768]{1,0:T(8,128)(2,1)}, bf16[128,768]{1,0:T(8,128)(2,1)}, u32[]{:S(2)}, u32[]{:S(2)}) %collective-permute-start.39) | collective-permute-done | bytes 196640 | tf_op jit(solution)/shard_map/ppermute | solution.py:69
  161.8 1.8 collective-permute-start.37
  165.2 1.6 collect.7
  166.9 7.2 %collective-permute-start.42 = (bf16[4,128,256]{2,1,0:T(8,128)(2,1)}, bf16[4,128,256]{2,1,0:T(8,128)(2,1)S(1)}, u32[]{:S(2)}, u32[]{:S(2)}) collective-permute-start(bf16[4,128,256]{2,1,0:T(8,128)(2,1)} %collect.4), channel_id=1, source_target_pairs={{0,1},{1,0},{2,3},{3,2},{4,5},{5,4},{6,7},{7,6},{8,9},{9,8},{10,11... | collective-permute-start | bytes 786440 | tf_op jit(solution)/shard_map/ppermute | solution.py:298
  175.8 3.4 %collective-permute-start.43 = (bf16[4,128,256]{2,1,0:T(8,128)(2,1)}, bf16[4,128,256]{2,1,0:T(8,128)(2,1)}, u32[]{:S(2)}, u32[]{:S(2)}) collective-permute-start(bf16[4,128,256]{2,1,0:T(8,128)(2,1)} %collect.5), channel_id=1, source_target_pairs={{0,1},{1,0},{2,3},{3,2},{4,5},{5,4},{6,7},{7,6},{8,9},{9,8},{10,11... | collective-permute-start | bytes 786440 | tf_op jit(solution)/shard_map/ppermute | solution.py:298
  179.2 1.6 collect.6
  181.7 2.6 collective-permute-done.45.refs_19_
  184.3 2.8 %collective-permute-done.43.refs_17_ = bf16[4,128,256]{2,1,0:T(8,128)(2,1)} collective-permute-done((bf16[4,128,256]{2,1,0:T(8,128)(2,1)}, bf16[4,128,256]{2,1,0:T(8,128)(2,1)}, u32[]{:S(2)}, u32[]{:S(2)}) %collective-permute-start.43) | collective-permute-done | bytes 262176 | tf_op jit(solution)/shard_map/ppermute | solution.py:298
  187.1 2.8 %collective-permute-done.44.refs_18_ = bf16[4,128,256]{2,1,0:T(8,128)(2,1)} collective-permute-done((bf16[4,128,256]{2,1,0:T(8,128)(2,1)}, bf16[4,128,256]{2,1,0:T(8,128)(2,1)}, u32[]{:S(2)}, u32[]{:S(2)}) %collective-permute-start.44) | collective-permute-done | bytes 262176 | tf_op jit(solution)/shard_map/ppermute | solution.py:298
  190.0 30.5 %attend.1 = (bf16[512,512]{1,0:T(8,128)(2,1)}, bf16[512,512]{1,0:T(8,128)(2,1)}, bf16[512,512]{1,0:T(8,128)(2,1)}, bf16[512,512]{1,0:T(8,128)(2,1)}) custom-call(s32[3]{0:T(128)} %pad_add_fusion.z_ref.where_ref, s32[1,32]{1,0:T(1,128)} %bitcast.40, bf16[4,128,768]{2,1,0:T(8,128)(2,1)S(1)} %get-tuple-element.107.refs_0_, ...), custom_call_target="tpu_custom_call" | custom-call | tf_op jit(solution)/shard_map/attend/pallas_call | solution.py:163
  221.6 2.4 collective-permute-start.47
  225.1 16.8 %collective-permute-done.46.refs_1_ = bf16[512,512]{1,0:T(8,128)(2,1)S(1)} collective-permute-done((bf16[512,512]{1,0:T(8,128)(2,1)}, bf16[512,512]{1,0:T(8,128)(2,1)S(1)}, u32[]{:S(2)}, u32[]{:S(2)}) %collective-permute-start.46) | collective-permute-done | bytes 524320 | tf_op jit(solution)/shard_map/ppermute | solution.py:69
  243.3 16.3 %project.1 = bf16[512,4096]{1,0:T(8,128)(2,1)} custom-call(s32[3]{0:T(128)} %pad_add_fusion.z_ref.where_ref, bf16[512,512]{1,0:T(8,128)(2,1)} %get-tuple-element.85.refs_0_, bf16[512,512]{1,0:T(8,128)(2,1)} %copy-done.3, bf16[512,512]{1,0:T(8,128)(2,1)} %copy-done.4, bf16[512,512]{1,0:T(8,128)(2,1)} %copy-done.5, ...), custom_call_target="tpu_custom_call" | custom-call | tf_op jit(solution)/shard_map/project/pallas_call | solution.py:221
  (67 shorter events, 20.8 us)
Async XLA Ops:
  6.5 236.0 %all-gather.2.cloned.1.call-start = ((), (), s32[]{:S(2)}) async-start(), calls=%async_computation | async-start | bytes 18874368 | tf_op jit(solution)/shard_map/all_gather | solution.py:300
  6.5 8.8 %collective-permute-start.28 = (bf16[512,2048]{1,0:T(8,128)(2,1)}, bf16[512,2048]{1,0:T(8,128)(2,1)}, u32[]{:S(2)}, u32[]{:S(2)}) collective-permute-start(bf16[512,2048]{1,0:T(8,128)(2,1)} %bitcast.36), channel_id=1, source_target_pairs={{0,8},{8,0},{16,24},{24,16},{32,40},{40,32},{48,56},{56,48},{64,72... | collective-permute-start | bytes 6291464 | tf_op jit(solution)/shard_map/ppermute | solution.py:278
  6.5 7.8 %collective-permute-start.29 = (bf16[512,1024]{1,0:T(8,128)(2,1)}, bf16[512,1024]{1,0:T(8,128)(2,1)S(1)}, u32[]{:S(2)}, u32[]{:S(2)}) collective-permute-start(bf16[512,1024]{1,0:T(8,128)(2,1)} %bitcast.38), channel_id=1, source_target_pairs={{0,8},{8,0},{16,24},{24,16},{32,40},{40,32},{48,56},{56,48},{64,72... | collective-permute-start | bytes 3145736 | tf_op jit(solution)/shard_map/ppermute | solution.py:279
  9.3 29.7 %collective-permute-start.50 = (bf16[64,4096]{1,0:T(8,128)(2,1)}, bf16[64,4096]{1,0:T(8,128)(2,1)}, u32[]{:S(2)}, u32[]{:S(2)}) collective-permute-start(bf16[64,4096]{1,0:T(8,128)(2,1)} %get-tuple-element.89), channel_id=1, source_target_pairs={{0,65},{1,64},{2,67},{3,66},{4,69},{5,68},{6,71},{7,70},{8,73},{9,... | collective-permute-start | bytes 1572872 | tf_op jit(solution)/shard_map/ppermute | solution.py:271
  12.3 26.7 %collective-permute-start.49 = (bf16[64,4096]{1,0:T(8,128)(2,1)}, bf16[64,4096]{1,0:T(8,128)(2,1)}, u32[]{:S(2)}, u32[]{:S(2)}) collective-permute-start(bf16[64,4096]{1,0:T(8,128)(2,1)} %get-tuple-element.90), channel_id=1, source_target_pairs={{0,64},{1,65},{2,66},{3,67},{4,68},{5,69},{6,70},{7,71},{8,72},{9,... | collective-permute-start | bytes 1572872 | tf_op jit(solution)/shard_map/ppermute | solution.py:271
  19.7 19.2 %collective-permute-start.23 = (bf16[4,128,768]{2,1,0:T(8,128)(2,1)S(1)}, bf16[4,128,768]{2,1,0:T(8,128)(2,1)S(1)}, u32[]{:S(2)}, u32[]{:S(2)}) collective-permute-start(bf16[4,128,768]{2,1,0:T(8,128)(2,1)S(1)} %param.27), channel_id=1, source_target_pairs={{0,48},{8,56},{16,32},{24,40},{32,16},{40,24},{48,0},{56,8},{64,11... | collective-permute-start | bytes 2359304 | tf_op jit(solution)/shard_map/cond/branch_3_fun/ppermute | solution.py:65
  44.2 23.8 %collective-permute-start = (bf16[4,128,768]{2,1,0:T(8,128)(2,1)S(1)}, bf16[4,128,768]{2,1,0:T(8,128)(2,1)S(1)}, u32[]{:S(2)}, u32[]{:S(2)}) collective-permute-start(bf16[4,128,768]{2,1,0:T(8,128)(2,1)S(1)} %param.1), channel_id=1, source_target_pairs={{0,16},{8,24},{16,0},{24,8},{32,48},{40,56},{48,32},{56,40},{64,80... | collective-permute-start | bytes 2359304 | tf_op jit(solution)/shard_map/cond/branch_1_fun/ppermute | solution.py:65
  69.0 81.6 %collective-permute-start.32 = (bf16[128,768]{1,0:T(8,128)(2,1)}, bf16[128,768]{1,0:T(8,128)(2,1)S(1)}, u32[]{:S(2)}, u32[]{:S(2)}) collective-permute-start(bf16[128,768]{1,0:T(8,128)(2,1)} %get-tuple-element.100), channel_id=1, source_target_pairs={{0,6},{1,7},{2,0},{3,1},{4,2},{5,3},{6,4},{7,5},{8,14},{9,15},{10,... | collective-permute-start | bytes 589832 | tf_op jit(solution)/shard_map/ppermute | solution.py:69
  69.0 81.9 %collective-permute-start.31 = (bf16[128,768]{1,0:T(8,128)(2,1)}, bf16[128,768]{1,0:T(8,128)(2,1)S(1)}, u32[]{:S(2)}, u32[]{:S(2)}) collective-permute-start(bf16[128,768]{1,0:T(8,128)(2,1)} %get-tuple-element.101), channel_id=1, source_target_pairs={{0,4},{1,5},{2,6},{3,7},{4,0},{5,1},{6,2},{7,3},{8,12},{9,13},{10,... | collective-permute-start | bytes 589832 | tf_op jit(solution)/shard_map/ppermute | solution.py:69
  70.3 84.4 %collective-permute-start.30 = (bf16[128,768]{1,0:T(8,128)(2,1)}, bf16[128,768]{1,0:T(8,128)(2,1)}, u32[]{:S(2)}, u32[]{:S(2)}) collective-permute-start(bf16[128,768]{1,0:T(8,128)(2,1)} %get-tuple-element.102), channel_id=1, source_target_pairs={{0,2},{1,3},{2,4},{3,5},{4,6},{5,7},{6,0},{7,1},{8,10},{9,11},{10,... | collective-permute-start | bytes 589832 | tf_op jit(solution)/shard_map/ppermute | solution.py:69
  72.5 82.1 %collective-permute-start.41 = (bf16[128,768]{1,0:T(8,128)(2,1)}, bf16[128,768]{1,0:T(8,128)(2,1)}, u32[]{:S(2)}, u32[]{:S(2)}) collective-permute-start(bf16[128,768]{1,0:T(8,128)(2,1)} %get-tuple-element.91), channel_id=1, source_target_pairs={{0,6},{1,7},{2,0},{3,1},{4,2},{5,3},{6,4},{7,5},{8,14},{9,15},{10,... | collective-permute-start | bytes 589832 | tf_op jit(solution)/shard_map/ppermute | solution.py:69
  74.5 37.1 %collective-permute-start.13 = (bf16[4,128,768]{2,1,0:T(8,128)(2,1)S(1)}, bf16[4,128,768]{2,1,0:T(8,128)(2,1)S(1)}, u32[]{:S(2)}, u32[]{:S(2)}) collective-permute-start(bf16[4,128,768]{2,1,0:T(8,128)(2,1)S(1)} %param.15), channel_id=1, source_target_pairs={{0,112},{8,120},{16,96},{24,104},{32,80},{40,88},{48,64},{56,72},{... | collective-permute-start | bytes 2359304 | tf_op jit(solution)/shard_map/cond/branch_7_fun/ppermute | solution.py:65
  111.7 35.2 %collective-permute-start.14 = (bf16[4,128,768]{2,1,0:T(8,128)(2,1)S(1)}, bf16[4,128,768]{2,1,0:T(8,128)(2,1)S(1)}, u32[]{:S(2)}, u32[]{:S(2)}) collective-permute-start(bf16[4,128,768]{2,1,0:T(8,128)(2,1)S(1)} %param.17), channel_id=1, source_target_pairs={{0,16},{8,24},{16,0},{24,8},{32,48},{40,56},{48,32},{56,40},{64,80... | collective-permute-start | bytes 2359304 | tf_op jit(solution)/shard_map/cond/branch_1_fun/ppermute | solution.py:65
  147.1 9.4 %collective-permute-start.40 = (bf16[128,768]{1,0:T(8,128)(2,1)}, bf16[128,768]{1,0:T(8,128)(2,1)}, u32[]{:S(2)}, u32[]{:S(2)}) collective-permute-start(bf16[128,768]{1,0:T(8,128)(2,1)} %get-tuple-element.92), channel_id=1, source_target_pairs={{0,4},{1,5},{2,6},{3,7},{4,0},{5,1},{6,2},{7,3},{8,12},{9,13},{10,... | collective-permute-start | bytes 589832 | tf_op jit(solution)/shard_map/ppermute | solution.py:69
  150.5 13.0 %copy-start.1 = (bf16[128,768]{1,0:T(8,128)(2,1)}, bf16[128,768]{1,0:T(8,128)(2,1)S(1)}, u32[]{:S(2)}) copy-start(bf16[128,768]{1,0:T(8,128)(2,1)S(1)} %collective-permute-done.32.refs_3_.refs_6_) | copy-start | bytes 589828
  150.5 11.3 %collective-permute-start.39 = (bf16[128,768]{1,0:T(8,128)(2,1)}, bf16[128,768]{1,0:T(8,128)(2,1)}, u32[]{:S(2)}, u32[]{:S(2)}) collective-permute-start(bf16[128,768]{1,0:T(8,128)(2,1)} %get-tuple-element.93), channel_id=1, source_target_pairs={{0,2},{1,3},{2,4},{3,5},{4,6},{5,7},{6,0},{7,1},{8,10},{9,11},{10,... | collective-permute-start | bytes 589832 | tf_op jit(solution)/shard_map/ppermute | solution.py:69
  150.9 12.7 %copy-start.2 = (bf16[128,768]{1,0:T(8,128)(2,1)}, bf16[128,768]{1,0:T(8,128)(2,1)S(1)}, u32[]{:S(2)}) copy-start(bf16[128,768]{1,0:T(8,128)(2,1)S(1)} %collective-permute-done.31.refs_2_.refs_5_) | copy-start | bytes 589828
  150.9 12.6 %collective-permute-start.35 = (bf16[128,768]{1,0:T(8,128)(2,1)S(1)}, bf16[128,768]{1,0:T(8,128)(2,1)}, u32[]{:S(2)}, u32[]{:S(2)}) collective-permute-start(bf16[128,768]{1,0:T(8,128)(2,1)S(1)} %get-tuple-element.97), channel_id=1, source_target_pairs={{0,6},{1,7},{2,0},{3,1},{4,2},{5,3},{6,4},{7,5},{8,14},{9,15},{10,... | collective-permute-start | bytes 589832 | tf_op jit(solution)/shard_map/ppermute | solution.py:69
  154.6 12.2 %collective-permute-start.34 = (bf16[128,768]{1,0:T(8,128)(2,1)}, bf16[128,768]{1,0:T(8,128)(2,1)}, u32[]{:S(2)}, u32[]{:S(2)}) collective-permute-start(bf16[128,768]{1,0:T(8,128)(2,1)} %get-tuple-element.98), channel_id=1, source_target_pairs={{0,4},{1,5},{2,6},{3,7},{4,0},{5,1},{6,2},{7,3},{8,12},{9,13},{10,... | collective-permute-start | bytes 589832 | tf_op jit(solution)/shard_map/ppermute | solution.py:69
  154.6 19.4 %collective-permute-start.33 = (bf16[128,768]{1,0:T(8,128)(2,1)}, bf16[128,768]{1,0:T(8,128)(2,1)}, u32[]{:S(2)}, u32[]{:S(2)}) collective-permute-start(bf16[128,768]{1,0:T(8,128)(2,1)} %get-tuple-element.99), channel_id=1, source_target_pairs={{0,2},{1,3},{2,4},{3,5},{4,6},{5,7},{6,0},{7,1},{8,10},{9,11},{10,... | collective-permute-start | bytes 589832 | tf_op jit(solution)/shard_map/ppermute | solution.py:69
  156.6 19.2 %collective-permute-start.38 = (bf16[128,768]{1,0:T(8,128)(2,1)}, bf16[128,768]{1,0:T(8,128)(2,1)}, u32[]{:S(2)}, u32[]{:S(2)}) collective-permute-start(bf16[128,768]{1,0:T(8,128)(2,1)} %get-tuple-element.94), channel_id=1, source_target_pairs={{0,6},{1,7},{2,0},{3,1},{4,2},{5,3},{6,4},{7,5},{8,14},{9,15},{10,... | collective-permute-start | bytes 589832 | tf_op jit(solution)/shard_map/ppermute | solution.py:69
  161.8 17.4 %collective-permute-start.37 = (bf16[128,768]{1,0:T(8,128)(2,1)}, bf16[128,768]{1,0:T(8,128)(2,1)}, u32[]{:S(2)}, u32[]{:S(2)}) collective-permute-start(bf16[128,768]{1,0:T(8,128)(2,1)} %get-tuple-element.95), channel_id=1, source_target_pairs={{0,4},{1,5},{2,6},{3,7},{4,0},{5,1},{6,2},{7,3},{8,12},{9,13},{10,... | collective-permute-start | bytes 589832 | tf_op jit(solution)/shard_map/ppermute | solution.py:69
  163.6 15.6 %collective-permute-start.36 = (bf16[128,768]{1,0:T(8,128)(2,1)}, bf16[128,768]{1,0:T(8,128)(2,1)}, u32[]{:S(2)}, u32[]{:S(2)}) collective-permute-start(bf16[128,768]{1,0:T(8,128)(2,1)} %get-tuple-element.96), channel_id=1, source_target_pairs={{0,2},{1,3},{2,4},{3,5},{4,6},{5,7},{6,0},{7,1},{8,10},{9,11},{10,... | collective-permute-start | bytes 589832 | tf_op jit(solution)/shard_map/ppermute | solution.py:69
  165.2 15.7 %copy-start.8 = (s32[1,32]{1,0:T(1,128)S(1)}, s32[1,32]{1,0:T(1,128)}, u32[]{:S(2)}) copy-start(s32[1,32]{1,0:T(1,128)} %param.39) | copy-start | bytes 388
  166.9 14.8 %collective-permute-start.42 = (bf16[4,128,256]{2,1,0:T(8,128)(2,1)}, bf16[4,128,256]{2,1,0:T(8,128)(2,1)S(1)}, u32[]{:S(2)}, u32[]{:S(2)}) collective-permute-start(bf16[4,128,256]{2,1,0:T(8,128)(2,1)} %collect.4), channel_id=1, source_target_pairs={{0,1},{1,0},{2,3},{3,2},{4,5},{5,4},{6,7},{7,6},{8,9},{9,8},{10,11... | collective-permute-start | bytes 786440 | tf_op jit(solution)/shard_map/ppermute | solution.py:298
  174.1 10.3 %collective-permute-start.45 = (bf16[4,128,256]{2,1,0:T(8,128)(2,1)}, bf16[4,128,256]{2,1,0:T(8,128)(2,1)}, u32[]{:S(2)}, u32[]{:S(2)}) collective-permute-start(bf16[4,128,256]{2,1,0:T(8,128)(2,1)} %collect.7), channel_id=1, source_target_pairs={{0,1},{1,0},{2,3},{3,2},{4,5},{5,4},{6,7},{7,6},{8,9},{9,8},{10,11... | collective-permute-start | bytes 786440 | tf_op jit(solution)/shard_map/ppermute | solution.py:298
  175.8 11.4 %collective-permute-start.43 = (bf16[4,128,256]{2,1,0:T(8,128)(2,1)}, bf16[4,128,256]{2,1,0:T(8,128)(2,1)}, u32[]{:S(2)}, u32[]{:S(2)}) collective-permute-start(bf16[4,128,256]{2,1,0:T(8,128)(2,1)} %collect.5), channel_id=1, source_target_pairs={{0,1},{1,0},{2,3},{3,2},{4,5},{5,4},{6,7},{7,6},{8,9},{9,8},{10,11... | collective-permute-start | bytes 786440 | tf_op jit(solution)/shard_map/ppermute | solution.py:298
  180.8 9.1 %collective-permute-start.44 = (bf16[4,128,256]{2,1,0:T(8,128)(2,1)}, bf16[4,128,256]{2,1,0:T(8,128)(2,1)}, u32[]{:S(2)}, u32[]{:S(2)}) collective-permute-start(bf16[4,128,256]{2,1,0:T(8,128)(2,1)} %collect.6), channel_id=1, source_target_pairs={{0,1},{1,0},{2,3},{3,2},{4,5},{5,4},{6,7},{7,6},{8,9},{9,8},{10,11... | collective-permute-start | bytes 786440 | tf_op jit(solution)/shard_map/ppermute | solution.py:298
  181.7 8.2 %copy-start.6 = (bf16[4,128,256]{2,1,0:T(8,128)(2,1)}, bf16[4,128,256]{2,1,0:T(8,128)(2,1)S(1)}, u32[]{:S(2)}) copy-start(bf16[4,128,256]{2,1,0:T(8,128)(2,1)S(1)} %collective-permute-done.42.refs_16_) | copy-start | bytes 786436
  220.5 21.4 %collective-permute-start.46 = (bf16[512,512]{1,0:T(8,128)(2,1)}, bf16[512,512]{1,0:T(8,128)(2,1)S(1)}, u32[]{:S(2)}, u32[]{:S(2)}) collective-permute-start(bf16[512,512]{1,0:T(8,128)(2,1)} %get-tuple-element.86), channel_id=1, source_target_pairs={{0,2},{1,3},{2,4},{3,5},{4,6},{5,7},{6,0},{7,1},{8,10},{9,11},{10,... | collective-permute-start | bytes 1572872 | tf_op jit(solution)/shard_map/ppermute | solution.py:69
  221.6 20.3 %collective-permute-start.47 = (bf16[512,512]{1,0:T(8,128)(2,1)}, bf16[512,512]{1,0:T(8,128)(2,1)S(1)}, u32[]{:S(2)}, u32[]{:S(2)}) collective-permute-start(bf16[512,512]{1,0:T(8,128)(2,1)} %get-tuple-element.87), channel_id=1, source_target_pairs={{0,4},{1,5},{2,6},{3,7},{4,0},{5,1},{6,2},{7,3},{8,12},{9,13},{10,... | collective-permute-start | bytes 1572872 | tf_op jit(solution)/shard_map/ppermute | solution.py:69
  224.0 18.6 %collective-permute-start.48 = (bf16[512,512]{1,0:T(8,128)(2,1)}, bf16[512,512]{1,0:T(8,128)(2,1)S(1)}, u32[]{:S(2)}, u32[]{:S(2)}) collective-permute-start(bf16[512,512]{1,0:T(8,128)(2,1)} %get-tuple-element.88), channel_id=1, source_target_pairs={{0,6},{1,7},{2,0},{3,1},{4,2},{5,3},{6,4},{7,5},{8,14},{9,15},{10,... | collective-permute-start | bytes 1572872 | tf_op jit(solution)/shard_map/ppermute | solution.py:69
  (5 other events, 9.4 us)
Sparse Core Ops, SparseCore 0:
  42.5 106.2 all-gather.1
